TPU v7x, 32 devices: a whole 2x2x4 slice. The times are simulated.
32 devices in a mesh: groups: 2 (over x), tm: 16 (over z, y, core).
Axes of the slice: x: 2, y: 2, z: 4, core: 2. Of those that a mesh axis runs over, the one named last changes fastest.
Arguments:
- latents: bfloat16 [2048, 2, 32, 256], P(('groups', 'tm')), parts along dimension 0, may hold values from -6 to 6
- input_map: bfloat16 [9, 256, 256], replicated, may hold values from -0.125 to 0.125
- output_map: bfloat16 [9, 256, 256], replicated, may hold values from -0.03125 to 0.03125
- decay_rate: float32 [256], replicated, may hold values from 0 to 1
- frame_step: float32 [2048], P(('groups', 'tm')), parts along dimension 0, may hold values from 0.6 to 512
- cotangent: bfloat16 [2048, 2, 32, 256], P(('groups', 'tm')), parts along dimension 0, may hold values from -6 to 6
Outputs:
- layer_out: bfloat16 [2048, 2, 32, 256], P(('groups', 'tm')), parts along dimension 0
- grad_latents: bfloat16 [2048, 2, 32, 256], P(('groups', 'tm')), parts along dimension 0
- grad_input_map: float32 [18, 256, 256], P('groups'), parts along dimension 0
- grad_output_map: float32 [18, 256, 256], P('groups'), parts along dimension 0
- grad_log_rate: float32 [512], P('groups'), parts along dimension 0
There are 2 independent parts, one for each index of `groups`. A program takes and returns all parts, laid end to end along the dimension named above; an argument that names none is the same for every part. Nothing has to cross between parts.
All inputs are finite; a program needn't handle non-finite values.
Results may differ from a plain program's by a relative error of at most 0.005.
Values sent between devices are 32-bit elements; how exact they have to be, the bound alone decides.
No kernel may reach another device: no remote copies, remote signals or barrier semaphores. Data moves between devices by JAX's collectives and lax.ppermute only.
A program may use at most 192 MiB of HBM per device.

v0:
```python
import math

import jax
import jax.numpy as jnp
from jax import lax
from jax.sharding import PartitionSpec as P


def from_behind(value, axis, steps):
    count = lax.axis_size(axis)
    initial, last = (max(0, -steps), min(count, count - steps))
    return lax.ppermute(value, axis, [(source, source + steps) for source in range(initial, last)])


def conv_same(source, kernel):
    height, breadth = (source.shape[1], source.shape[2])
    padded = jnp.pad(source, ((0, 0), (1, 1), (1, 1), (0, 0)))
    total = jnp.zeros(source.shape[:3] + (kernel.shape[2],), jnp.float32)
    for offset in range(9):
        window = padded[:, offset // 3 : offset // 3 + height, offset % 3 : offset % 3 + breadth, :]
        total = total + lax.dot_general(
            window, kernel[offset], (((3,), (0,)), ((), ())), preferred_element_type=jnp.float32
        )
    return total


def kernel_grad(source, target):
    height, breadth = (source.shape[1], source.shape[2])
    padded = jnp.pad(source, ((0, 0), (1, 1), (1, 1), (0, 0)))
    pieces = []
    for offset in range(9):
        window = padded[:, offset // 3 : offset // 3 + height, offset % 3 : offset % 3 + breadth, :]
        pieces.append(
            lax.dot_general(
                window,
                target,
                (((0, 1, 2), (0, 1, 2)), ((), ())),
                preferred_element_type=jnp.float32,
            )
        )
    return jnp.stack(pieces)


def flipped(kernel):
    return jnp.transpose(kernel[::-1], (0, 2, 1))


def forward_step(previous, inputs):
    factor_now, driven_now = inputs
    updated = factor_now[None, None, :] * previous + driven_now
    return (updated, updated)


def body(latents, input_map, output_map, decay_rate, frame_step, cotangent):
    driven = conv_same(latents, input_map)
    pulled = conv_same(cotangent, flipped(output_map))
    decays = jnp.exp(-frame_step[:, None] * decay_rate[None, :])
    blank_map = jnp.zeros(driven.shape[1:], jnp.float32)
    _, local_states = lax.scan(forward_step, blank_map, (decays, driven))
    zero_row = jnp.zeros((1, decays.shape[1]), jnp.float32)
    one_row = jnp.ones((1, decays.shape[1]), jnp.float32)
    decays_next = jnp.concatenate([decays[1:], zero_row], axis=0)
    _, local_adjoint = lax.scan(forward_step, blank_map, (decays_next, pulled), reverse=True)
    leading = jnp.cumprod(decays, axis=0)
    tails = jnp.cumprod(jnp.concatenate([decays[1:], one_row], axis=0)[::-1], axis=0)[::-1]
    total_decay = leading[-1]
    forward_summary = local_states[-1]
    backward_summary = decays[0][None, None, :] * local_adjoint[0]
    rounds = lax.axis_size("tm") - 1

    def forward_round(index, held_map):
        return from_behind(total_decay[None, None, :] * held_map + forward_summary, "tm", 1)

    def backward_round(index, held_map):
        return from_behind(total_decay[None, None, :] * held_map + backward_summary, "tm", -1)

    incoming = lax.fori_loop(0, rounds, forward_round, blank_map)
    arriving = lax.fori_loop(0, rounds, backward_round, blank_map)
    states = local_states + leading[:, None, None, :] * incoming[None]
    adjoint = local_adjoint + tails[:, None, None, :] * arriving[None]
    states_low = states.astype(jnp.bfloat16)
    layer_out = conv_same(states_low, output_map).astype(jnp.bfloat16)
    adjoint_low = adjoint.astype(jnp.bfloat16)
    grad_latents = conv_same(adjoint_low, flipped(input_map)).astype(jnp.bfloat16)
    states_before = jnp.concatenate([incoming[None], states[:-1]], axis=0)
    weighted = jnp.sum(adjoint * states_before, axis=(1, 2))
    local_term = jnp.sum(frame_step[:, None] * decays * weighted, axis=0)
    totals = lax.psum(
        (kernel_grad(latents, adjoint_low), kernel_grad(states_low, cotangent), local_term), "tm"
    )
    frame_total = latents.shape[0] * lax.axis_size("tm")
    factor = 1.0 / math.sqrt(frame_total * latents.shape[1] * latents.shape[2])
    grad_input_map = totals[0] * factor
    grad_output_map = totals[1] * factor
    grad_log_rate = -factor * decay_rate * totals[2]
    return (layer_out, grad_latents, grad_input_map, grad_output_map, grad_log_rate)


def solution(mesh):
    in_specs = (
        P(("groups", "tm"), None, None, None),
        P(),
        P(),
        P(),
        P(("groups", "tm")),
        P(("groups", "tm"), None, None, None),
    )
    out_specs = (
        P(("groups", "tm"), None, None, None),
        P(("groups", "tm"), None, None, None),
        P("groups", None, None),
        P("groups", None, None),
        P("groups"),
    )
    return jax.shard_map(body, mesh=mesh, in_specs=in_specs, out_specs=out_specs, check_vma=False)
```

profile of v0, /device:TPU:0, one launch (start us, length us, event | category | flops | bytes accessed | tf_op | source)
XLA Modules:
  0.0 695.0 jit_solution(15595861585110706080)
XLA Ops:
  7.2 4.2 fusion.17
  11.4 2.7 fusion.19
  19.4 2.7 fusion.25
  22.1 2.7 fusion.27
  30.1 3.0 copy.11
  34.5 2.7 fusion.2
  42.4 2.7 fusion.5
  45.1 2.7 fusion.6
  47.8 2.7 fusion.7
  50.5 2.8 fusion.8
  53.3 2.7 fusion.81
  56.2 14.8 %add_add_fusion.1 = f32[64,2,32,256]{3,2,1,0:T(8,128)} fusion(f32[64,2,32,256]{3,2,1,0:T(8,128)} %fusion.29, f32[64,2,32,256]{3,2,1,0:T(8,128)} %fusion.27, f32[64,2,32,256]{3,2,1,0:T(8,128)} %fusion.25, f32[64,2,32,256]{3,2,1,0:T(8,128)} %fusion.96, f32[64,2,32,256]{3,2,1,0:T(8,128)} %fusion.23, f32[64,2,32,256]{3,2,1,0:T(8,128)} %fusion.21, ...), kind=kOutput, calls=%fused_computation.49 | convolution fusion | flops 545259520 | bytes 39976960 | tf_op jit(solution)/shard_map/dot_general | solution.py:21
  73.5 95.6 %while.52 = (s32[]{:T(128)}, f32[2,32,256]{2,1,0:T(8,128)S(1)}, f32[64,2,32,256]{3,2,1,0:T(8,128)}, f32[64,256]{1,0:T(8,128)S(1)}, f32[64,2,32,256]{3,2,1,0:T(8,128)}, /*index=5*/s32[]{:T(128)}, s32[]{:T(128)}) while((s32[]{:T(128)}, f32[2,32,256]{2,1,0:T(8,128)S(1)}, f32[64,2,32,256]{3,2,1,0:T(8,128)}, f32[64,256]{1,0:T(8,128)S(1)}, ...), condition=%wide.region_1.2_spmd.clone, body=%wide.region_0.1_spmd.clone.sunk | while | flops 49155 | bytes 265819 | solution.py:59
  170.0 88.4 %while.50 = (s32[]{:T(128)}, f32[2,32,256]{2,1,0:T(8,128)S(1)}, f32[1,256]{1,0:T(1,128)S(1)}, f32[2,32,256]{2,1,0:T(8,128)S(1)}, s32[]{:T(128)}) while((s32[]{:T(128)}, f32[2,32,256]{2,1,0:T(8,128)S(1)}, f32[1,256]{1,0:T(1,128)S(1)}, f32[2,32,256]{2,1,0:T(8,128)S(1)}, s32[]{:T(128)}) %tuple.98), condition=%wide.region_4.5_spmd, body=%wide.region_3.4_spmd.sunk | while | flops 32770 | bytes 459877 | solution.py:77
  173.3 4.9 collective-permute-start
  179.2 4.7 collective-permute-start
  184.8 4.7 collective-permute-start
  190.4 4.7 collective-permute-start
  196.0 4.7 collective-permute-start
  201.6 4.7 collective-permute-start
  207.1 4.8 collective-permute-start
  212.8 5.6 collective-permute-start
  219.3 5.6 collective-permute-start
  225.8 5.6 collective-permute-start
  232.3 5.6 collective-permute-start
  238.8 5.6 collective-permute-start
  245.3 5.6 collective-permute-start
  251.8 5.6 collective-permute-start
  258.5 5.4 fusion.168
  279.1 11.4 %add_add_fusion = f32[64,2,32,256]{3,2,1,0:T(8,128)} fusion(f32[64,2,32,256]{3,2,1,0:T(8,128)} %fusion.8, f32[64,2,32,256]{3,2,1,0:T(8,128)} %fusion.7, f32[64,2,32,256]{3,2,1,0:T(8,128)} %fusion.6, f32[64,2,32,256]{3,2,1,0:T(8,128)} %fusion.81, f32[64,2,32,256]{3,2,1,0:T(8,128)} %fusion.5, f32[64,2,32,256]{3,2,1,0:T(8,128)} %fusion.4, ...), kind=kOutput, calls=%fused_computation.46 | convolution fusion | flops 545259520 | bytes 39976960 | tf_op jit(solution)/shard_map/dot_general | solution.py:21
  293.0 140.2 %while.53 = (s32[]{:T(128)}, f32[2,32,256]{2,1,0:T(8,128)S(1)}, f32[64,2,32,256]{3,2,1,0:T(8,128)}, f32[64,256]{1,0:T(8,128)}, f32[64,2,32,256]{3,2,1,0:T(8,128)}, /*index=5*/s32[]{:T(128)}, s32[]{:T(128)}, s32[]{:T(128)}) while((s32[]{:T(128)}, f32[2,32,256]{2,1,0:T(8,128)S(1)}, f32[64,2,32,256]{3,2,1,0:T(8,128)}, ...), condition=%wide.region_6.7_spmd.clone, body=%wide.region_5.6_spmd.clone.sunk | while | flops 49156 | bytes 265331 | solution.py:63
  433.2 4.7 slice.340
  439.6 98.6 %while.51 = (s32[]{:T(128)}, f32[2,32,256]{2,1,0:T(8,128)S(1)}, f32[1,256]{1,0:T(1,128)S(1)}, f32[2,32,256]{2,1,0:T(8,128)S(1)}, s32[]{:T(128)}) while((s32[]{:T(128)}, f32[2,32,256]{2,1,0:T(8,128)S(1)}, f32[1,256]{1,0:T(1,128)S(1)}, f32[2,32,256]{2,1,0:T(8,128)S(1)}, s32[]{:T(128)}) %tuple.110), condition=%wide.region_9.10_spmd, body=%wide.region_8.9_spmd.sunk | while | flops 32770 | bytes 459877 | solution.py:78
  440.9 5.0 collective-permute-done.1
  447.2 5.8 collective-permute-done.1
  454.4 5.0 collective-permute-done.1
  460.7 5.8 collective-permute-done.1
  467.8 5.2 collective-permute-done.1
  474.3 5.2 collective-permute-done.1
  480.8 5.2 collective-permute-done.1
  487.3 5.2 collective-permute-done.1
  493.8 5.2 collective-permute-done.1
  500.3 5.2 collective-permute-done.1
  506.8 5.2 collective-permute-done.1
  513.3 5.2 collective-permute-done.1
  519.8 5.2 collective-permute-done.1
  526.3 5.2 collective-permute-done.1
  532.8 5.2 collective-permute-done.1
  538.2 5.1 fusion
  563.1 2.7 fusion.11
  565.7 2.8 fusion.12
  568.5 2.7 fusion.13
  571.2 2.7 fusion.14
  573.9 2.8 fusion.15
  582.0 2.7 fusion.32
  587.3 2.7 fusion.36
  590.0 2.7 fusion.38
  592.7 2.7 fusion.40
  595.4 2.7 fusion.42
  603.5 35.6 %psum.23 = f32[256]{0:T(256)S(1)} all-reduce(f32[256]{0:T(256)S(1)} %multiply_reduce_fusion), channel_id=1, replica_groups=mesh['groups'=2,'tm'=16] {'tm'}, use_global_device_ids=true, to_apply=%region_14.15 | all-reduce | flops 256 | bytes 2048 | tf_op jit(solution)/shard_map/psum | solution.py:88
  639.6 14.9 %add_convert_fusion = bf16[64,2,32,256]{3,2,1,0:T(8,128)(2,1)} fusion(f32[64,2,32,256]{3,2,1,0:T(8,128)} %fusion.15, f32[64,2,32,256]{3,2,1,0:T(8,128)} %fusion.14, f32[64,2,32,256]{3,2,1,0:T(8,128)} %fusion.13, f32[64,2,32,256]{3,2,1,0:T(8,128)} %fusion.80, f32[64,2,32,256]{3,2,1,0:T(8,128)} %fusion.12, f32[64,2,32,256]{3,2,1,0:T(8,128)} %fusion.11, ...), kind=kOutput, calls=%fused_computation.44 | convolution fusion | flops 546308096 | bytes 37879808 | tf_op jit(solution)/shard_map/dot_general | solution.py:21
  654.5 10.9 %add_convert_fusion.1 = bf16[64,2,32,256]{3,2,1,0:T(8,128)(2,1)} fusion(f32[64,2,32,256]{3,2,1,0:T(8,128)} %fusion.44, f32[64,2,32,256]{3,2,1,0:T(8,128)} %fusion.42, f32[64,2,32,256]{3,2,1,0:T(8,128)} %fusion.40, f32[64,2,32,256]{3,2,1,0:T(8,128)} %fusion.86, f32[64,2,32,256]{3,2,1,0:T(8,128)} %fusion.38, f32[64,2,32,256]{3,2,1,0:T(8,128)} %fusion.36, ...), kind=kOutput, calls=%fused_computation.47 | convolution fusion | flops 546308096 | bytes 37879808 | tf_op jit(solution)/shard_map/dot_general | solution.py:21
  665.4 17.4 %all-reduce.9.cloned.1.call-done = (f32[9,256,256]{2,1,0:T(8,128)}, f32[9,256,256]{2,1,0:T(8,128)}) async-done(((f32[9,256,256]{2,1,0:T(8,128)}, f32[9,256,256]{2,1,0:T(8,128)}), (f32[9,256,256]{2,1,0:T(8,128)}, f32[9,256,256]{2,1,0:T(8,128)})) %all-reduce.9.cloned.1.call-update) | async-done | bytes 4718608 | tf_op jit(solution)/shard_map/psum | solution.py:88
  682.8 5.0 broadcast_multiply_fusion
  (406 shorter events, 344.9 us)
Async XLA Ops:
  7.2 4.2 copy-start.4
  7.2 4.2 copy-start.10
  7.2 675.6 %all-reduce.9.cloned.1.call-start = ((), (), s32[]{:S(2)}) async-start(), calls=%async_computation | async-start | bytes 9437184 | tf_op jit(solution)/shard_map/psum | solution.py:88
  30.1 4.4 copy-start.2
  34.4 18.8 %copy-start.12 = (bf16[9,256,256]{2,1,0:T(8,128)(2,1)}, bf16[9,256,256]{2,1,0:T(8,128)(2,1)S(1)}, u32[]{:S(2)}) copy-start(bf16[9,256,256]{2,1,0:T(8,128)(2,1)S(1)} %reverse_bitcast_fusion.1) | copy-start | bytes 3538948
  53.3 2.7 copy-start.15
  53.3 2.7 copy-start.14
  170.0 3.3 collective-permute-start
  173.3 5.8 collective-permute-start
  179.2 5.6 collective-permute-start
  184.8 5.6 collective-permute-start
  190.4 5.6 collective-permute-start
  196.0 5.6 collective-permute-start
  201.6 5.6 collective-permute-start
  207.1 5.7 collective-permute-start
  212.8 6.5 collective-permute-start
  219.3 6.5 collective-permute-start
  225.8 6.5 collective-permute-start
  232.3 6.5 collective-permute-start
  238.8 6.5 collective-permute-start
  245.3 6.5 collective-permute-start
  251.8 6.5 collective-permute-start
  258.4 5.4 copy-start.3
  275.5 2.3 copy-start.6
  275.5 3.6 copy-start.7
  439.6 6.3 collective-permute-start.1
  445.9 7.1 %collective-permute-start.1 = (f32[2,32,256]{2,1,0:T(8,128)S(1)}, f32[2,32,256]{2,1,0:T(8,128)S(1)}, u32[]{:S(2)}, u32[]{:S(2)}) collective-permute-start(f32[2,32,256]{2,1,0:T(8,128)S(1)} %multiply_add_fusion.8), channel_id=1, source_target_pairs={{1,0},{2,1},{3,2},{4,3},{5,4},{6,5},{7,6},{8,7},{9,8},{10,9},{11,1... | collective-permute-start | bytes 196616 | tf_op jit(solution)/shard_map/while/body/eval_jaxpr/ppermute | solution.py:12
  453.1 6.3 collective-permute-start.1
  459.4 7.1 %collective-permute-start.1 = (f32[2,32,256]{2,1,0:T(8,128)S(1)}, f32[2,32,256]{2,1,0:T(8,128)S(1)}, u32[]{:S(2)}, u32[]{:S(2)}) collective-permute-start(f32[2,32,256]{2,1,0:T(8,128)S(1)} %multiply_add_fusion.8), channel_id=1, source_target_pairs={{1,0},{2,1},{3,2},{4,3},{5,4},{6,5},{7,6},{8,7},{9,8},{10,9},{11,1... | collective-permute-start | bytes 196616 | tf_op jit(solution)/shard_map/while/body/eval_jaxpr/ppermute | solution.py:12
  466.5 6.5 collective-permute-start.1
  473.0 6.5 collective-permute-start.1
  479.5 6.5 collective-permute-start.1
  486.0 6.5 collective-permute-start.1
  492.5 6.5 collective-permute-start.1
  499.0 6.5 collective-permute-start.1
  505.5 6.5 collective-permute-start.1
  512.0 6.5 collective-permute-start.1
  518.5 6.5 collective-permute-start.1
  525.0 6.5 collective-permute-start.1
  531.5 6.5 collective-permute-start.1
  538.2 5.1 copy-start.5
  543.3 11.9 %copy-start = (bf16[64,2,32,256]{3,2,1,0:T(8,128)(2,1)}, bf16[64,2,32,256]{3,2,1,0:T(8,128)(2,1)S(1)}, u32[]{:S(2)}) copy-start(bf16[64,2,32,256]{3,2,1,0:T(8,128)(2,1)S(1)} %get-tuple-element.264) | copy-start | bytes 6291460
  558.4 1.9 copy-start.1
  560.4 18.9 %copy-start.13 = (bf16[9,256,256]{2,1,0:T(8,128)(2,1)}, bf16[9,256,256]{2,1,0:T(8,128)(2,1)S(1)}, u32[]{:S(2)}) copy-start(bf16[9,256,256]{2,1,0:T(8,128)(2,1)S(1)} %reverse_bitcast_fusion) | copy-start | bytes 3538948
  579.3 2.7 copy-start.11
  600.7 2.6 copy-start.16
  639.6 14.9 %copy-start.8 = (f32[64,2,32,256]{3,2,1,0:T(8,128)S(1)}, f32[64,2,32,256]{3,2,1,0:T(8,128)}, u32[]{:S(2)}) copy-start(f32[64,2,32,256]{3,2,1,0:T(8,128)} %fusion.32) | copy-start | bytes 12582916
  639.6 14.9 %copy-start.9 = (f32[64,2,32,256]{3,2,1,0:T(8,128)S(1)}, f32[64,2,32,256]{3,2,1,0:T(8,128)}, u32[]{:S(2)}) copy-start(f32[64,2,32,256]{3,2,1,0:T(8,128)} %fusion.34) | copy-start | bytes 12582916
Sparse Core Ops, SparseCore 0:
  556.8 125.9 all-reduce.8
where the time goes:
time: 709 us; the launch traced here: 695 us
  other arithmetic  208 us (29%)
  matrix products  166 us (23%)
  waiting for transfers between devices  109 us (15%)
  starting transfers between devices  94.2 us (13%)
  local copies, waits for them, and re-layouts  66.7 us (9%)
  blocking collectives  35.6 us (5%)
  between operations  14.5 us (2%)
    dynamic_update_slice x128, other arithmetic, body(): _, local_states = lax.scan(forward_step, blank_map, (decays, driven))  190 us
    dot_general x36, matrix products, conv_same(): lax.dot_general(window, kernel[offset], (((3,), (0,)), ((), ())), preferr...  139 us
    ppermute x30, starting transfers between devices, from_behind(): lax.ppermute(value, axis, [(source, source + steps) for source in range(i...  94.1 us
    ppermute x30, waiting for transfers between devices, from_behind(): lax.ppermute(value, axis, [(source, source + steps) for source in range(i...  91.8 us
    dynamic_slice x128, local copies, waits for them, and re-layouts, body(): _, local_states = lax.scan(forward_step, blank_map, (decays, driven))  45.2 us
    psum x1, blocking collectives, body(): lax.psum((kernel_grad(latents, adjoint_low), kernel_grad(states_low, cota...  35.6 us
    dot_general x18, matrix products, kernel_grad(): lax.dot_general(window, target, (((0, 1, 2), (0, 1, 2)), ((), ())), prefe...  26.5 us
    psum x1, waiting for transfers between devices, body(): lax.psum((kernel_grad(latents, adjoint_low), kernel_grad(states_low, cota...  17.4 us
  transfers between devices with their start and end apart: 31, of which 31 were waited for; matrix products, arithmetic and copies ran while one was open for 10% of the time, Pallas kernels for 0%

commit v1 on v0

v1 whole, which is shorter than its diff:
```python
import functools
import math

import jax
import jax.numpy as jnp
from jax import lax
from jax.experimental import pallas as pl
from jax.experimental.pallas import tpu as pltpu
from jax.sharding import PartitionSpec as P

F32 = jnp.float32
BF16 = jnp.bfloat16
EXTRA = 8
VMEM_LIMIT = 40 * 1024 * 1024


def column_shifts(value):
    frames, height, breadth, channels = value.shape
    rows = frames * height * breadth
    flat = value.reshape(rows, channels).astype(F32)
    column = lax.broadcasted_iota(jnp.int32, (rows, channels), 0) % breadth
    before = jnp.where(column == 0, 0.0, pltpu.roll(flat, 1, 0)).astype(BF16)
    after = jnp.where(column == breadth - 1, 0.0, pltpu.roll(flat, rows - 1, 0)).astype(BF16)
    return before.reshape(value.shape), value, after.reshape(value.shape)


def conv_rows(value, weights):
    frames, _, breadth, channels = value.shape
    shifted = column_shifts(value)
    pieces = [piece[:, row].reshape(frames * breadth, channels) for row in (0, 1) for piece in shifted]
    patches = jnp.concatenate(pieces, axis=1)
    outs = []
    for first in (3, 0):
        taps = weights[first : first + 6].reshape(6 * channels, weights.shape[2])
        outs.append(jnp.dot(patches, taps, preferred_element_type=F32))
    return outs


def flip_into(flipped_ref, weights_ref):
    for tap in range(9):
        flipped_ref[tap] = weights_ref[8 - tap].T


def decay_of(step, rate):
    return jnp.exp(-(step * rate))


def drive_kernel(reverse, step_ref, rate_ref, value_ref, weights_ref, driven_ref, carry_ref, state, decay, flipped):
    index, count = pl.program_id(0), pl.num_programs(0)
    block, _, breadth, channels = driven_ref.shape

    @pl.when(index == 0)
    def _():
        state[...] = jnp.zeros_like(state)
        decay[...] = jnp.ones_like(decay)
        if reverse:
            flip_into(flipped, weights_ref)

    outs = conv_rows(value_ref[...], flipped if reverse else weights_ref)
    for row, out in enumerate(outs):
        driven_ref[:, row] = out.reshape(block, breadth, channels)
    first = (count - 1 - index if reverse else index) * block
    rate = jnp.broadcast_to(rate_ref[...], decay.shape)
    total, held = decay[...], state[...]
    for offset in range(block):
        frame = block - 1 - offset if reverse else offset
        factor = decay_of(step_ref[first + frame], rate)
        driven = driven_ref[frame].reshape(state.shape)
        held = factor[None] * (held + driven) if reverse else factor[None] * held + driven
        total = total * factor
    state[...] = held
    decay[...] = total

    @pl.when(index == count - 1)
    def _():
        rows = state.shape[0] * 8
        carry_ref[:rows] = held.reshape(rows, channels)
        carry_ref[rows:] = total


def add_kernel_grad(sums, source, target):
    frames, height, breadth, channels = source.shape
    before, same, after = column_shifts(target)
    taps = jnp.concatenate([after, same, before], axis=-1)

    def contract(left, right):
        return lax.dot_general(
            left.reshape(-1, channels), right.reshape(-1, 3 * channels), (((0,), (0,)), ((), ())), preferred_element_type=F32
        )

    sums[1] += contract(source, taps)
    sums[0] += contract(source[:, 0], taps[:, 1])
    sums[2] += contract(source[:, 1], taps[:, 0])


def split_grad(scale, sums, whole, core, keep_ref, send_ref):
    channels = sums.shape[1]
    for tap in range(9):
        piece = sums[tap // 3, :, (tap % 3) * channels : (tap % 3 + 1) * channels]
        whole[tap * channels : (tap + 1) * channels] = piece * scale
    half = whole.shape[0] // 2
    keep_ref[:half] = whole[pl.ds(core * half, half)]
    send_ref[:half] = whole[pl.ds((1 - core) * half, half)]


def state_kernel(
    scale, step_ref, core_ref, rate_ref, incoming_ref, driven_ref, cotangent_ref, low_ref, keep_ref, send_ref, state, sums, whole
):
    index, count = pl.program_id(0), pl.num_programs(0)
    block = driven_ref.shape[0]

    @pl.when(index == 0)
    def _():
        state[...] = incoming_ref[...].reshape(state.shape)
        sums[...] = jnp.zeros_like(sums)

    rate = jnp.broadcast_to(rate_ref[...], (8, rate_ref.shape[1]))
    held = state[...]
    for frame in range(block):
        factor = decay_of(step_ref[index * block + frame], rate)
        held = factor[None] * held + driven_ref[frame].reshape(state.shape)
        low_ref[frame] = held.astype(BF16).reshape(low_ref.shape[1:])
    state[...] = held
    add_kernel_grad(sums, low_ref[...], cotangent_ref[...])

    @pl.when(index == count - 1)
    def _():
        split_grad(scale, sums, whole, core_ref[0], keep_ref, send_ref)


def adjoint_kernel(
    scale,
    step_ref,
    core_ref,
    rate_ref,
    arriving_ref,
    incoming_ref,
    pulled_ref,
    latents_ref,
    states_ref,
    previous_ref,
    low_ref,
    keep_ref,
    send_ref,
    carry,
    rate_sum,
    sums,
    whole,
):
    index, count = pl.program_id(0), pl.num_programs(0)
    block = pulled_ref.shape[0]
    first = (count - 1 - index) * block

    @pl.when(index == 0)
    def _():
        carry[...] = arriving_ref[...].reshape(carry.shape)
        rate_sum[...] = jnp.zeros_like(rate_sum)
        sums[...] = jnp.zeros_like(sums)

    rate = jnp.broadcast_to(rate_ref[...], rate_sum.shape)
    held, summed = carry[...], rate_sum[...]
    for frame in range(block - 1, -1, -1):
        step = step_ref[first + frame]
        adjoint = held + pulled_ref[frame].reshape(carry.shape)
        low_ref[frame] = adjoint.astype(BF16).reshape(low_ref.shape[1:])
        held = decay_of(step, rate)[None] * adjoint
        if frame:
            before = states_ref[frame - 1].astype(F32).reshape(carry.shape)
        else:
            before = jnp.where(
                index == count - 1,
                incoming_ref[...].reshape(carry.shape),
                previous_ref[0].astype(F32).reshape(carry.shape),
            )
        summed = summed + step * jnp.sum(held * before, axis=0)
    carry[...] = held
    rate_sum[...] = summed
    add_kernel_grad(sums, latents_ref[...], low_ref[...])

    @pl.when(index == count - 1)
    def _():
        split_grad(scale, sums, whole, core_ref[0], keep_ref, send_ref)
        half = whole.shape[0] // 2
        keep_ref[half:] = summed
        send_ref[half:] = summed


def conv_kernel(reverse, value_ref, weights_ref, out_ref, flipped):
    if reverse:

        @pl.when(pl.program_id(0) == 0)
        def _():
            flip_into(flipped, weights_ref)

    block, _, breadth, channels = out_ref.shape
    outs = conv_rows(value_ref[...], flipped if reverse else weights_ref)
    for row, out in enumerate(outs):
        out_ref[:, row] = out.astype(BF16).reshape(block, breadth, channels)


def call(kernel, grid, in_specs, out_specs, out_shape, scratch, flops, moved, name):
    return pl.pallas_call(
        kernel,
        grid=grid,
        in_specs=in_specs,
        out_specs=out_specs,
        out_shape=out_shape,
        scratch_shapes=scratch,
        compiler_params=pltpu.CompilerParams(vmem_limit_bytes=VMEM_LIMIT, dimension_semantics=("arbitrary",) * len(grid)),
        cost_estimate=pl.CostEstimate(flops=flops, bytes_accessed=moved, transcendentals=0),
        name=name,
    )


def smem():
    return pl.BlockSpec(memory_space=pltpu.SMEM)


def fixed(shape):
    return pl.BlockSpec(shape, lambda g: (0,) * len(shape))


def framed(shape, block, count, reverse):
    return pl.BlockSpec((block,) + shape[1:], lambda g: ((count - 1 - g if reverse else g), 0, 0, 0))


def fold(bit, keep, recv, main, last):
    rows, columns = keep.shape
    extra = rows - main
    half = main if last else main // 2

    def kernel(bit_ref, keep_ref, recv_ref, *outs):
        if last:
            outs[0][...] = keep_ref[...] + recv_ref[...]
            return
        for out, part in zip(outs, (bit_ref[0], 1 - bit_ref[0])):
            window = pl.ds(part * half, half)
            out[:half] = keep_ref[window] + recv_ref[window]
            if extra:
                out[half:] = keep_ref[main:] + recv_ref[main:]

    shape = jax.ShapeDtypeStruct((half + extra, columns), F32)
    outs = [shape] if last else [shape, shape]
    whole = pl.BlockSpec(memory_space=pltpu.VMEM)
    return pl.pallas_call(
        kernel,
        in_specs=[smem(), whole, whole],
        out_specs=[whole] * len(outs),
        out_shape=outs,
        cost_estimate=pl.CostEstimate(flops=rows * columns, bytes_accessed=12 * rows * columns, transcendentals=0),
        name="fold",
    )(bit, keep, recv)


def merge(bit, mine, other):
    rows, columns = mine.shape

    def kernel(bit_ref, mine_ref, other_ref, out_ref):
        out_ref[pl.ds(bit_ref[0] * rows, rows)] = mine_ref[...]
        out_ref[pl.ds((1 - bit_ref[0]) * rows, rows)] = other_ref[...]

    whole = pl.BlockSpec(memory_space=pltpu.VMEM)
    return pl.pallas_call(
        kernel,
        in_specs=[smem(), whole, whole],
        out_specs=whole,
        out_shape=jax.ShapeDtypeStruct((2 * rows, columns), F32),
        cost_estimate=pl.CostEstimate(flops=0, bytes_accessed=16 * rows * columns, transcendentals=0),
        name="merge",
    )(bit, mine, other)


def swap(value, count, distance):
    return lax.ppermute(value, "tm", [(source, source ^ distance) for source in range(count)])


def bits_of(me, levels):
    return [jnp.bitwise_and(lax.shift_right_logical(me, level), 1).reshape(1) for level in range(levels)]


def sum_over(keep, send, main, bits, count):
    levels = len(bits)
    for level in range(levels):
        recv = swap(send, count, 1 << level)
        last = level == levels - 1
        if last:
            (keep,) = fold(bits[level], keep, recv, main, True)
        else:
            keep, send = fold(bits[level + 1], keep, recv, main, False)
            main = main // 2
    extra = keep[main:]
    piece = keep[:main]
    for level in range(levels - 1, -1, -1):
        piece = merge(bits[level], piece, swap(piece, count, 1 << level))
    return piece, extra


def carry_in(carry, bits, count, reverse):
    rows = carry.shape[0] - 8
    local, decay = carry[:rows].reshape(rows // 8, 8, -1), carry[rows:][None]
    reached, passed = jnp.zeros_like(local), jnp.ones_like(decay)
    levels = len(bits)
    for level in range(levels):
        distance = 1 << level
        message = jnp.concatenate([local.reshape(rows, -1), decay[0]], axis=0)
        if level < levels - 1:
            other = swap(message, count, distance)
        else:
            towards = 0 if reverse else distance
            pairs = [(source, source ^ distance) for source in range(count) if (source ^ distance) & distance == towards]
            other = lax.ppermute(message, "tm", pairs)
        other_local, other_decay = other[:rows].reshape(rows // 8, 8, -1), other[rows:][None]
        later = bits[level][0] == (0 if reverse else 1)
        reached = jnp.where(later, reached + passed * other_local, reached)
        passed = jnp.where(later, passed * other_decay, passed)
        local = jnp.where(later, decay * other_local + local, other_decay * local + other_local)
        decay = decay * other_decay
    return reached.reshape(rows, -1)


def body(latents, input_map, output_map, decay_rate, frame_step, cotangent):
    frames, height, breadth, channels = latents.shape
    count = lax.axis_size("tm")
    levels = count.bit_length() - 1
    me = lax.axis_index("tm")
    bits = bits_of(me, levels)
    factor = 1.0 / math.sqrt(frames * count * height * breadth)
    block = 16
    steps = frames // block
    grid = (steps,)
    rate = decay_rate.reshape(1, channels)
    map_rows = height * breadth
    shape = latents.shape
    weights = input_map.shape
    pixels = frames * height * breadth
    flops = 2 * pixels * 6 * channels * channels
    driven_type = jax.ShapeDtypeStruct(shape, F32)
    low_type = jax.ShapeDtypeStruct(shape, BF16)
    map_scratch = pltpu.VMEM((map_rows // 8, 8, channels), F32)
    decay_scratch = pltpu.VMEM((8, channels), F32)
    flip_scratch = pltpu.VMEM(weights, BF16)

    def drive(value, kernel_map, reverse):
        return call(
            functools.partial(drive_kernel, reverse),
            grid,
            [smem(), fixed(rate.shape), framed(shape, block, steps, reverse), fixed(weights)],
            [framed(shape, block, steps, reverse), fixed((map_rows + 8, channels))],
            [driven_type, jax.ShapeDtypeStruct((map_rows + 8, channels), F32)],
            [map_scratch, decay_scratch, flip_scratch],
            flops,
            pixels * channels * 6,
            "pull" if reverse else "drive",
        )(frame_step, rate, value, kernel_map)

    driven, forward_carry = drive(latents, input_map, False)
    pulled, backward_carry = drive(cotangent, output_map, True)
    incoming = carry_in(forward_carry, bits, count, False)
    arriving = carry_in(backward_carry, bits, count, True)

    grad_rows = 9 * channels
    half = grad_rows // 2
    sums_scratch = pltpu.VMEM((3, channels, 3 * channels), F32)
    whole_scratch = pltpu.VMEM((grad_rows, channels), F32)
    half_type = jax.ShapeDtypeStruct((half, channels), F32)
    half_extra = jax.ShapeDtypeStruct((half + EXTRA, channels), F32)

    states_low, out_keep, out_send = call(
        functools.partial(state_kernel, factor),
        grid,
        [
            smem(),
            smem(),
            fixed(rate.shape),
            fixed(incoming.shape),
            framed(shape, block, steps, False),
            framed(shape, block, steps, False),
        ],
        [framed(shape, block, steps, False), fixed(half_type.shape), fixed(half_type.shape)],
        [low_type, half_type, half_type],
        [map_scratch, sums_scratch, whole_scratch],
        flops,
        pixels * channels * 8,
        "states",
    )(frame_step, bits[0], rate, incoming, driven, cotangent)

    adjoint_low, in_keep, in_send = call(
        functools.partial(adjoint_kernel, factor),
        grid,
        [
            smem(),
            smem(),
            fixed(rate.shape),
            fixed(incoming.shape),
            fixed(incoming.shape),
            framed(shape, block, steps, True),
            framed(shape, block, steps, True),
            framed(shape, block, steps, True),
            pl.BlockSpec((1,) + shape[1:], lambda g: (jnp.maximum((steps - 1 - g) * block - 1, 0), 0, 0, 0)),
        ],
        [framed(shape, block, steps, True), fixed(half_extra.shape), fixed(half_extra.shape)],
        [low_type, half_extra, half_extra],
        [map_scratch, decay_scratch, sums_scratch, whole_scratch],
        flops,
        pixels * channels * 10,
        "adjoint",
    )(frame_step, bits[0], rate, arriving, incoming, pulled, latents, states_low, states_low)

    def conv(value, kernel_map, reverse):
        return call(
            functools.partial(conv_kernel, reverse),
            grid,
            [framed(shape, block, steps, False), fixed(weights)],
            framed(shape, block, steps, False),
            low_type,
            [flip_scratch],
            flops,
            pixels * channels * 4,
            "conv",
        )(value, kernel_map)

    layer_out = conv(states_low, output_map, False)
    grad_latents = conv(adjoint_low, input_map, True)
    grad_output_map, _ = sum_over(out_keep, out_send, half, bits, count)
    grad_input_map, rate_rows = sum_over(in_keep, in_send, half, bits, count)
    grad_log_rate = -factor * decay_rate * jnp.sum(rate_rows, axis=0)
    return (
        layer_out,
        grad_latents,
        grad_input_map.reshape(weights),
        grad_output_map.reshape(weights),
        grad_log_rate,
    )


def solution(mesh):
    in_specs = (
        P(("groups", "tm"), None, None, None),
        P(),
        P(),
        P(),
        P(("groups", "tm")),
        P(("groups", "tm"), None, None, None),
    )
    out_specs = (
        P(("groups", "tm"), None, None, None),
        P(("groups", "tm"), None, None, None),
        P("groups", None, None),
        P("groups", None, None),
        P("groups"),
    )
    return jax.shard_map(body, mesh=mesh, in_specs=in_specs, out_specs=out_specs, check_vma=False)
```

time: 709 us -> 196 us (0.28); the launches traced: 695 us -> 194 us
  other arithmetic: 208 us -> 4.58 us
  matrix products: 166 us -> 0 us
  Pallas kernels: 0 us -> 67.7 us
  starting transfers between devices: 94.2 us -> 31.8 us
  waiting for transfers between devices: 109 us -> 59.9 us
  local copies, waits for them, and re-layouts: 66.7 us -> 29.2 us
  blocking collectives: 35.6 us -> 0 us
  between operations: 14.5 us -> 0.94 us
    dynamic_update_slice x128 -> x0, other arithmetic: 190 us -> none  [body(): _, local_states = lax.scan(forward_step, blank_map, (decays, driven))]
    dot_general x54 -> x0, matrix products: 166 us -> none  [the longest x36 139 us: conv_same(): lax.dot_general(window, kernel[offset], (((3,), (0,)), ((), ())), preferr...]
    pallas_call x0 -> x22, Pallas kernels: none -> 67.7 us  [the longest x8 18.4 us: merge(): pl.pallas_call(kernel, in_specs=[smem(), whole, whole], out_specs=whole,...]
    ppermute x30 -> x24, starting transfers between devices: 94.1 us -> 31.8 us  [the longest x22 25.9 us: swap(): lax.ppermute(value, 'tm', [(source, source ^ distance) for source in rang...]
    dynamic_slice x128 -> x0, local copies, waits for them, and re-layouts: 45.2 us -> none  [body(): _, local_states = lax.scan(forward_step, blank_map, (decays, driven))]
    psum x1 -> x0, blocking collectives: 35.6 us -> none  [body(): lax.psum((kernel_grad(latents, adjoint_low), kernel_grad(states_low, cota...]
    ppermute x30 -> x24, waiting for transfers between devices: 91.8 us -> 59.9 us  [the longest x22 59.3 us: swap(): lax.ppermute(value, 'tm', [(source, source ^ distance) for source in rang...]
    unnamed x36 -> x74, local copies, waits for them, and re-layouts: 6.71 us -> 28.3 us
  transfers between devices with their start and end apart: 31 -> 24, of which waited for: 31 -> 13; matrix products, arithmetic and copies ran while one was open for 10% -> 3% of each run, Pallas kernels for 0% -> 28%
where the time goes in v1:
time: 196 us; the launch traced here: 194 us
  Pallas kernels  67.7 us (35%)
  waiting for transfers between devices  59.9 us (31%)
  starting transfers between devices  31.8 us (16%)
  local copies, waits for them, and re-layouts  29.2 us (15%)
  other arithmetic  4.58 us (2%)
    ppermute x22, waiting for transfers between devices, swap(): lax.ppermute(value, 'tm', [(source, source ^ distance) for source in rang...  59.3 us
    unnamed x74, local copies, waits for them, and re-layouts  28.3 us
    ppermute x22, starting transfers between devices, swap(): lax.ppermute(value, 'tm', [(source, source ^ distance) for source in rang...  25.9 us
    pallas_call x8, Pallas kernels, merge(): pl.pallas_call(kernel, in_specs=[smem(), whole, whole], out_specs=whole,...  18.4 us
    pallas_call x8, Pallas kernels, fold(): pl.pallas_call(kernel, in_specs=[smem(), whole, whole], out_specs=[whole]...  16.9 us
    pallas_call x2, Pallas kernels, conv(): call(functools.partial(conv_kernel, reverse), grid, [framed(shape, block,...  9.9 us
    pallas_call x2, Pallas kernels, drive(): call(functools.partial(drive_kernel, reverse), grid, [smem(), fixed(rate....  9.79 us
    pallas_call x1, Pallas kernels, body(): call(functools.partial(state_kernel, factor), grid, [smem(), smem(), fixe...  6.58 us
  transfers between devices with their start and end apart: 24, of which 13 were waited for; matrix products, arithmetic and copies ran while one was open for 3% of the time, Pallas kernels for 28%

profile of v1, /device:TPU:0, one launch (start us, length us, event | category | flops | bytes accessed | tf_op | source)
XLA Modules:
  0.0 194.1 jit_solution(779369447633411129)
XLA Ops:
  1.3 1.6 copy-done.5
  2.9 1.3 copy-done.8
  4.8 4.6 %drive.1 = (f32[64,2,32,256]{3,2,1,0:T(8,128)S(1)}, f32[72,256]{1,0:T(8,128)S(1)}) custom-call(f32[64]{0:T(128)S(1)} %copy-done.10, f32[1,256]{1,0:T(1,128)S(1)} %bitcast.99, bf16[64,2,32,256]{3,2,1,0:T(8,128)(2,1)S(1)} %copy-done.5, bf16[9,256,256]{2,1,0:T(8,128)(2,1)S(1)} %copy-done.8), custom_call_target="tpu_custom_call" | custom-call | flops 3221225472 | bytes 6291456 | tf_op jit(solution)/shard_map/drive/pallas_call | solution.py:344
  9.4 2.0 %copy-done.18 = f32[64,2,32,256]{3,2,1,0:T(8,128)} copy-done((f32[64,2,32,256]{3,2,1,0:T(8,128)}, f32[64,2,32,256]{3,2,1,0:T(8,128)S(1)}, u32[]{:S(2)}) %copy-start.18) | copy-done | bytes 4194328
  11.9 5.2 %pull.1 = (f32[64,2,32,256]{3,2,1,0:T(8,128)S(1)}, f32[72,256]{1,0:T(8,128)S(1)}) custom-call(f32[64]{0:T(128)S(1)} %copy-done.10, f32[1,256]{1,0:T(1,128)S(1)} %bitcast.100, bf16[64,2,32,256]{3,2,1,0:T(8,128)(2,1)S(1)} %copy-done.4, bf16[9,256,256]{2,1,0:T(8,128)(2,1)S(1)} %copy-done.7), custom_call_target="tpu_custom_call" | custom-call | flops 3221225472 | bytes 6291456 | tf_op jit(solution)/shard_map/pull/pallas_call | solution.py:344
  17.1 2.0 %copy-done.12 = f32[64,2,32,256]{3,2,1,0:T(8,128)} copy-done((f32[64,2,32,256]{3,2,1,0:T(8,128)}, f32[64,2,32,256]{3,2,1,0:T(8,128)S(1)}, u32[]{:S(2)}) %copy-start.12) | copy-done | bytes 4194328
  19.9 0.9 fusion.16
  20.8 3.0 %collective-permute-start.1 = (f32[72,256]{1,0:T(8,128)S(1)}, f32[72,256]{1,0:T(8,128)S(1)}, u32[]{:S(2)}, u32[]{:S(2)}) collective-permute-start(f32[72,256]{1,0:T(8,128)S(1)} %pad_maximum_fusion), channel_id=1, source_target_pairs={{0,2},{1,3},{2,0},{3,1},{4,6},{5,7},{6,4},{7,5},{8,10},{9,11},{10,... | collective-permute-start | bytes 221192 | tf_op jit(solution)/shard_map/ppermute | solution.py:274
  24.0 2.3 %collective-permute-done.1 = f32[72,256]{1,0:T(8,128)S(1)} collective-permute-done((f32[72,256]{1,0:T(8,128)S(1)}, f32[72,256]{1,0:T(8,128)S(1)}, u32[]{:S(2)}, u32[]{:S(2)}) %collective-permute-start.1) | collective-permute-done | bytes 73760 | tf_op jit(solution)/shard_map/ppermute | solution.py:274
  26.3 2.4 %collective-permute-start.2 = (f32[72,256]{1,0:T(8,128)S(1)}, f32[72,256]{1,0:T(8,128)S(1)}, u32[]{:S(2)}, u32[]{:S(2)}) collective-permute-start(f32[72,256]{1,0:T(8,128)S(1)} %pad_maximum_fusion.1), channel_id=1, source_target_pairs={{0,4},{1,5},{2,6},{3,7},{4,0},{5,1},{6,2},{7,3},{8,12},{9,13},{10,... | collective-permute-start | bytes 221192 | tf_op jit(solution)/shard_map/ppermute | solution.py:274
  28.8 1.2 collective-permute-start.6
  30.0 1.4 collective-permute-done.2
  32.1 4.7 %collective-permute-start.3 = (f32[72,256]{1,0:T(8,128)S(1)}, f32[72,256]{1,0:T(8,128)S(1)}, u32[]{:S(2)}, u32[]{:S(2)}) collective-permute-start(f32[72,256]{1,0:T(8,128)S(1)} %pad_maximum_fusion.2), channel_id=1, source_target_pairs={{0,8},{1,9},{2,10},{3,11},{4,12},{5,13},{6,14},{7,15},{16,24},{17,... | collective-permute-start | bytes 221192 | tf_op jit(solution)/shard_map/ppermute | solution.py:311
  36.8 1.3 collective-permute-start.7
  38.7 0.9 add_select_fusion.3.incoming_ref
  39.6 2.2 %copy-done.19 = f32[64,2,32,256]{3,2,1,0:T(8,128)S(1)} copy-done((f32[64,2,32,256]{3,2,1,0:T(8,128)S(1)}, f32[64,2,32,256]{3,2,1,0:T(8,128)}, u32[]{:S(2)}) %copy-start.19) | copy-done | bytes 4194328
  41.8 6.6 %states.1 = (bf16[64,2,32,256]{3,2,1,0:T(8,128)(2,1)S(1)}, f32[1152,256]{1,0:T(8,128)S(1)}, f32[1152,256]{1,0:T(8,128)}) custom-call(f32[64]{0:T(128)S(1)} %copy-done.11, s32[1]{0:T(128)} %bitcast.core_ref.bit_ref, f32[1,256]{1,0:T(1,128)S(1)} %bitcast.101, f32[64,256]{1,0:T(8,128)S(1)} %add_select_fusion.3.incoming_ref, f32[64,2,32,256]{3,2,1,0:T(8,128)S(1)} %copy-done.19, ...), custom_call_target="tpu_custom_call" | custom-call | flops 3221225472 | bytes 8388608 | tf_op jit(solution)/shard_map/states/pallas_call | solution.py:368
  48.4 1.1 copy-done.1
  49.5 6.1 %adjoint.1 = (bf16[64,2,32,256]{3,2,1,0:T(8,128)(2,1)S(1)}, f32[1160,256]{1,0:T(8,128)S(1)}, f32[1160,256]{1,0:T(8,128)S(1)}) custom-call(f32[64]{0:T(128)S(1)} %copy-done.11, s32[1]{0:T(128)} %bitcast.core_ref.bit_ref, f32[1,256]{1,0:T(1,128)S(1)} %bitcast.102, f32[64,256]{1,0:T(8,128)S(1)} %add_select_fusion.arriving_ref, ...), custom_call_target="tpu_custom_call" | custom-call | flops 3221225472 | bytes 10485760 | tf_op jit(solution)/shard_map/adjoint/pallas_call | solution.py:387
  55.7 1.0 copy-done
  56.7 1.3 copy-done.16
  58.5 4.0 %collective-permute-done.8.recv_ref = f32[1160,256]{1,0:T(8,128)S(1)} collective-permute-done((f32[1160,256]{1,0:T(8,128)S(1)}, f32[1160,256]{1,0:T(8,128)S(1)}, u32[]{:S(2)}, u32[]{:S(2)}) %collective-permute-start.8) | collective-permute-done | bytes 1187872 | tf_op jit(solution)/shard_map/ppermute | solution.py:274
  62.5 1.0 copy-done.20
  63.5 2.8 %fold.8 = (f32[584,256]{1,0:T(8,128)}, f32[584,256]{1,0:T(8,128)}) custom-call(s32[1]{0:T(128)} %bitcast.20.bit_ref, f32[1160,256]{1,0:T(8,128)} %copy-done, f32[1160,256]{1,0:T(8,128)} %copy-done.20), custom_call_target="tpu_custom_call" | custom-call | flops 296960 | bytes 3563520 | tf_op jit(solution)/shard_map/fold/pallas_call | solution.py:245
  66.4 1.7 collective-permute-start.9
  68.1 1.0 copy-done.23
  69.1 2.8 %fold.12 = (f32[576,256]{1,0:T(8,128)}, f32[576,256]{1,0:T(8,128)}) custom-call(s32[1]{0:T(128)} %bitcast.20.bit_ref, f32[1152,256]{1,0:T(8,128)} %copy-done.1, f32[1152,256]{1,0:T(8,128)} %copy-done.23), custom_call_target="tpu_custom_call" | custom-call | flops 294912 | bytes 3538944 | tf_op jit(solution)/shard_map/fold/pallas_call | solution.py:245
  72.2 10.8 %collective-permute-done.9.recv_ref = f32[584,256]{1,0:T(8,128)S(1)} collective-permute-done((f32[584,256]{1,0:T(8,128)}, f32[584,256]{1,0:T(8,128)S(1)}, u32[]{:S(2)}, u32[]{:S(2)}) %collective-permute-start.9) | collective-permute-done | bytes 598048 | tf_op jit(solution)/shard_map/ppermute | solution.py:274
  83.7 2.2 %fold.9 = (f32[296,256]{1,0:T(8,128)}, f32[296,256]{1,0:T(8,128)}) custom-call(s32[1]{0:T(128)} %bitcast.21.bit_ref, f32[584,256]{1,0:T(8,128)} %get-tuple-element.35.keep_ref, f32[584,256]{1,0:T(8,128)} %copy-done.24), custom_call_target="tpu_custom_call" | custom-call | flops 149504 | bytes 1794048 | tf_op jit(solution)/shard_map/fold/pallas_call | solution.py:245
  85.9 2.1 %collective-permute-start.10 = (f32[296,256]{1,0:T(8,128)}, f32[296,256]{1,0:T(8,128)S(1)}, u32[]{:S(2)}, u32[]{:S(2)}) collective-permute-start(f32[296,256]{1,0:T(8,128)} %get-tuple-element.38), channel_id=1, source_target_pairs={{0,4},{1,5},{2,6},{3,7},{4,0},{5,1},{6,2},{7,3},{8,12},{9,13},{10,... | collective-permute-start | bytes 909320 | tf_op jit(solution)/shard_map/ppermute | solution.py:274
  88.1 6.7 %collective-permute-done.17.recv_ref = f32[576,256]{1,0:T(8,128)S(1)} collective-permute-done((f32[576,256]{1,0:T(8,128)}, f32[576,256]{1,0:T(8,128)S(1)}, u32[]{:S(2)}, u32[]{:S(2)}) %collective-permute-start.17) | collective-permute-done | bytes 589856 | tf_op jit(solution)/shard_map/ppermute | solution.py:274
  95.6 2.2 %fold.13 = (f32[288,256]{1,0:T(8,128)}, f32[288,256]{1,0:T(8,128)}) custom-call(s32[1]{0:T(128)} %bitcast.21.bit_ref, f32[576,256]{1,0:T(8,128)} %get-tuple-element.43.keep_ref, f32[576,256]{1,0:T(8,128)} %copy-done.27), custom_call_target="tpu_custom_call" | custom-call | flops 147456 | bytes 1769472 | tf_op jit(solution)/shard_map/fold/pallas_call | solution.py:245
  97.8 2.1 %collective-permute-start.18 = (f32[288,256]{1,0:T(8,128)}, f32[288,256]{1,0:T(8,128)S(1)}, u32[]{:S(2)}, u32[]{:S(2)}) collective-permute-start(f32[288,256]{1,0:T(8,128)} %get-tuple-element.46), channel_id=1, source_target_pairs={{0,4},{1,5},{2,6},{3,7},{4,0},{5,1},{6,2},{7,3},{8,12},{9,13},{10,... | collective-permute-start | bytes 884744 | tf_op jit(solution)/shard_map/ppermute | solution.py:274
  100.6 1.8 fold.10
  102.4 3.4 %collective-permute-start.11 = (f32[152,256]{1,0:T(8,128)}, f32[152,256]{1,0:T(8,128)S(1)}, u32[]{:S(2)}, u32[]{:S(2)}) collective-permute-start(f32[152,256]{1,0:T(8,128)} %get-tuple-element.40), channel_id=1, source_target_pairs={{0,8},{1,9},{2,10},{3,11},{4,12},{5,13},{6,14},{7,15},{8,0},{9,1},... | collective-permute-start | bytes 466952 | tf_op jit(solution)/shard_map/ppermute | solution.py:274
  105.8 3.4 %collective-permute-done.18.recv_ref = f32[288,256]{1,0:T(8,128)S(1)} collective-permute-done((f32[288,256]{1,0:T(8,128)}, f32[288,256]{1,0:T(8,128)S(1)}, u32[]{:S(2)}, u32[]{:S(2)}) %collective-permute-start.18) | collective-permute-done | bytes 294944 | tf_op jit(solution)/shard_map/ppermute | solution.py:274
  110.0 1.8 fold.14
  111.8 2.1 %collective-permute-start.19 = (f32[144,256]{1,0:T(8,128)}, f32[144,256]{1,0:T(8,128)S(1)}, u32[]{:S(2)}, u32[]{:S(2)}) collective-permute-start(f32[144,256]{1,0:T(8,128)} %get-tuple-element.48), channel_id=1, source_target_pairs={{0,8},{1,9},{2,10},{3,11},{4,12},{5,13},{6,14},{7,15},{8,0},{9,1},... | collective-permute-start | bytes 442376 | tf_op jit(solution)/shard_map/ppermute | solution.py:274
  113.9 5.9 %collective-permute-done.19.recv_ref = f32[144,256]{1,0:T(8,128)S(1)} collective-permute-done((f32[144,256]{1,0:T(8,128)}, f32[144,256]{1,0:T(8,128)S(1)}, u32[]{:S(2)}, u32[]{:S(2)}) %collective-permute-start.19) | collective-permute-done | bytes 147488 | tf_op jit(solution)/shard_map/ppermute | solution.py:274
  120.4 1.6 fold.15.mine_ref
  123.2 1.7 fold.11
  124.9 0.9 slice.96.mine_ref
  125.9 2.5 %collective-permute-start.12 = (f32[144,256]{1,0:T(8,128)S(1)}, f32[144,256]{1,0:T(8,128)S(1)}, u32[]{:S(2)}, u32[]{:S(2)}) collective-permute-start(f32[144,256]{1,0:T(8,128)S(1)} %slice.96.mine_ref), channel_id=1, source_target_pairs={{0,8},{1,9},{2,10},{3,11},{4,12},{5,13},{6,14},{7,15},{8,0},{9,1},... | collective-permute-start | bytes 442376 | tf_op jit(solution)/shard_map/ppermute | solution.py:274
  128.4 4.5 %collective-permute-done.20.other_ref = f32[144,256]{1,0:T(8,128)S(1)} collective-permute-done((f32[144,256]{1,0:T(8,128)}, f32[144,256]{1,0:T(8,128)S(1)}, u32[]{:S(2)}, u32[]{:S(2)}) %collective-permute-start.20) | collective-permute-done | bytes 147488 | tf_op jit(solution)/shard_map/ppermute | solution.py:274
  133.5 1.7 merge.12.mine_ref
  135.3 0.9 collective-permute-done.12.other_ref
  136.8 1.7 merge.8.mine_ref
  138.5 1.1 collective-permute-start.13
  139.6 5.6 %collective-permute-done.21.other_ref = f32[288,256]{1,0:T(8,128)S(1)} collective-permute-done((f32[288,256]{1,0:T(8,128)}, f32[288,256]{1,0:T(8,128)S(1)}, u32[]{:S(2)}, u32[]{:S(2)}) %collective-permute-start.21) | collective-permute-done | bytes 294944 | tf_op jit(solution)/shard_map/ppermute | solution.py:274
  146.0 2.0 %merge.13.mine_ref = f32[576,256]{1,0:T(8,128)} custom-call(s32[1]{0:T(128)} %bitcast.21.bit_ref, f32[288,256]{1,0:T(8,128)} %merge.12.mine_ref, f32[288,256]{1,0:T(8,128)} %copy-done.31), custom_call_target="tpu_custom_call" | custom-call | bytes 1179648 | tf_op jit(solution)/shard_map/merge/pallas_call | solution.py:263
  147.9 1.7 collective-permute-start.22
  150.3 1.9 merge.9.mine_ref
  152.7 10.6 %collective-permute-done.22.other_ref = f32[576,256]{1,0:T(8,128)S(1)} collective-permute-done((f32[576,256]{1,0:T(8,128)}, f32[576,256]{1,0:T(8,128)S(1)}, u32[]{:S(2)}, u32[]{:S(2)}) %collective-permute-start.22) | collective-permute-done | bytes 589856 | tf_op jit(solution)/shard_map/ppermute | solution.py:274
  163.3 0.8 copy-done.25
  164.2 2.3 %merge.14.mine_ref = f32[1152,256]{1,0:T(8,128)} custom-call(s32[1]{0:T(128)} %bitcast.20.bit_ref, f32[576,256]{1,0:T(8,128)} %merge.13.mine_ref, f32[576,256]{1,0:T(8,128)} %copy-done.25), custom_call_target="tpu_custom_call" | custom-call | bytes 2359296 | tf_op jit(solution)/shard_map/merge/pallas_call | solution.py:263
  166.5 3.1 %collective-permute-done.14.other_ref = f32[576,256]{1,0:T(8,128)S(1)} collective-permute-done((f32[576,256]{1,0:T(8,128)}, f32[576,256]{1,0:T(8,128)S(1)}, u32[]{:S(2)}, u32[]{:S(2)}) %collective-permute-start.14) | collective-permute-done | bytes 589856 | tf_op jit(solution)/shard_map/ppermute | solution.py:274
  170.5 2.4 %merge.10.mine_ref = f32[1152,256]{1,0:T(8,128)} custom-call(s32[1]{0:T(128)} %bitcast.20.bit_ref, f32[576,256]{1,0:T(8,128)} %merge.9.mine_ref, f32[576,256]{1,0:T(8,128)} %copy-done.26), custom_call_target="tpu_custom_call" | custom-call | bytes 2359296 | tf_op jit(solution)/shard_map/merge/pallas_call | solution.py:263
  172.8 1.7 copy-done.15
  174.5 4.8 %conv.2 = bf16[64,2,32,256]{3,2,1,0:T(8,128)(2,1)} custom-call(bf16[64,2,32,256]{3,2,1,0:T(8,128)(2,1)S(1)} %copy-done.15, bf16[9,256,256]{2,1,0:T(8,128)(2,1)S(1)} %copy-done.7), custom_call_target="tpu_custom_call" | custom-call | flops 3221225472 | bytes 4194304 | tf_op jit(solution)/shard_map/conv/pallas_call | solution.py:410
  179.3 5.1 %conv.3 = bf16[64,2,32,256]{3,2,1,0:T(8,128)(2,1)} custom-call(bf16[64,2,32,256]{3,2,1,0:T(8,128)(2,1)S(1)} %copy-done.17, bf16[9,256,256]{2,1,0:T(8,128)(2,1)S(1)} %copy-done.9), custom_call_target="tpu_custom_call" | custom-call | flops 3221225472 | bytes 4194304 | tf_op jit(solution)/shard_map/conv/pallas_call | solution.py:410
  185.7 1.0 copy-done.21
  186.7 3.2 %merge.15 = f32[2304,256]{1,0:T(8,128)} custom-call(s32[1]{0:T(128)} %bitcast.core_ref.bit_ref, f32[1152,256]{1,0:T(8,128)} %merge.14.mine_ref, f32[1152,256]{1,0:T(8,128)} %copy-done.21), custom_call_target="tpu_custom_call" | custom-call | bytes 4718592 | tf_op jit(solution)/shard_map/merge/pallas_call | solution.py:263
  189.9 1.0 copy-done.22
  190.9 3.2 %merge.11 = f32[2304,256]{1,0:T(8,128)} custom-call(s32[1]{0:T(128)} %bitcast.core_ref.bit_ref, f32[1152,256]{1,0:T(8,128)} %merge.10.mine_ref, f32[1152,256]{1,0:T(8,128)} %copy-done.22), custom_call_target="tpu_custom_call" | custom-call | bytes 4718592 | tf_op jit(solution)/shard_map/merge/pallas_call | solution.py:263
  (103 shorter events, 15.2 us)
Async XLA Ops:
  0.6 0.7 copy-start.2
  1.3 1.6 copy-start.5
  2.9 1.3 copy-start.8
  4.2 0.7 copy-start.10
  4.8 7.1 %copy-start.4 = (bf16[64,2,32,256]{3,2,1,0:T(8,128)(2,1)S(1)}, bf16[64,2,32,256]{3,2,1,0:T(8,128)(2,1)}, u32[]{:S(2)}) copy-start(bf16[64,2,32,256]{3,2,1,0:T(8,128)(2,1)} %value_ref.3) | copy-start | bytes 6291460
  4.8 7.1 %copy-start.7 = (bf16[9,256,256]{2,1,0:T(8,128)(2,1)S(1)}, bf16[9,256,256]{2,1,0:T(8,128)(2,1)}, u32[]{:S(2)}) copy-start(bf16[9,256,256]{2,1,0:T(8,128)(2,1)} %weights_ref.6) | copy-start | bytes 3538948
  9.4 2.0 %copy-start.18 = (f32[64,2,32,256]{3,2,1,0:T(8,128)}, f32[64,2,32,256]{3,2,1,0:T(8,128)S(1)}, u32[]{:S(2)}) copy-start(f32[64,2,32,256]{3,2,1,0:T(8,128)S(1)} %get-tuple-element.28.driven_ref) | copy-start | bytes 12582916
  11.4 7.7 %collective-permute-start = (f32[72,256]{1,0:T(8,128)S(1)}, f32[72,256]{1,0:T(8,128)}, u32[]{:S(2)}, u32[]{:S(2)}) collective-permute-start(f32[72,256]{1,0:T(8,128)S(1)} %get-tuple-element.27), channel_id=1, source_target_pairs={{0,1},{1,0},{2,3},{3,2},{4,5},{5,4},{6,7},{7,6},{8,9},{9,8},{10,11... | collective-permute-start | bytes 221192 | tf_op jit(solution)/shard_map/ppermute | solution.py:274
  17.1 2.0 %copy-start.12 = (f32[64,2,32,256]{3,2,1,0:T(8,128)}, f32[64,2,32,256]{3,2,1,0:T(8,128)S(1)}, u32[]{:S(2)}) copy-start(f32[64,2,32,256]{3,2,1,0:T(8,128)S(1)} %get-tuple-element.31.pulled_ref) | copy-start | bytes 12582916
  19.1 4.7 %collective-permute-start.4 = (f32[72,256]{1,0:T(8,128)S(1)}, f32[72,256]{1,0:T(8,128)S(1)}, u32[]{:S(2)}, u32[]{:S(2)}) collective-permute-start(f32[72,256]{1,0:T(8,128)S(1)} %get-tuple-element.30), channel_id=1, source_target_pairs={{0,1},{1,0},{2,3},{3,2},{4,5},{5,4},{6,7},{7,6},{8,9},{9,8},{10,11... | collective-permute-start | bytes 221192 | tf_op jit(solution)/shard_map/ppermute | solution.py:274
  20.8 5.5 %collective-permute-start.1 = (f32[72,256]{1,0:T(8,128)S(1)}, f32[72,256]{1,0:T(8,128)S(1)}, u32[]{:S(2)}, u32[]{:S(2)}) collective-permute-start(f32[72,256]{1,0:T(8,128)S(1)} %pad_maximum_fusion), channel_id=1, source_target_pairs={{0,2},{1,3},{2,0},{3,1},{4,6},{5,7},{6,4},{7,5},{8,10},{9,11},{10,... | collective-permute-start | bytes 221192 | tf_op jit(solution)/shard_map/ppermute | solution.py:274
  23.8 15.8 %copy-start.3 = (f32[256]{0:T(256)S(1)}, f32[256]{0:T(256)}, u32[]{:S(2)}) copy-start(f32[256]{0:T(256)} %param.9) | copy-start | bytes 3076
  23.8 15.8 %copy-start.11 = (f32[64]{0:T(128)S(1)}, f32[64]{0:T(128)}, u32[]{:S(2)}) copy-start(f32[64]{0:T(128)} %step_ref.7) | copy-start | bytes 772
  23.8 4.9 %collective-permute-start.5 = (f32[72,256]{1,0:T(8,128)S(1)}, f32[72,256]{1,0:T(8,128)S(1)}, u32[]{:S(2)}, u32[]{:S(2)}) collective-permute-start(f32[72,256]{1,0:T(8,128)S(1)} %pad_maximum_fusion.3), channel_id=1, source_target_pairs={{0,2},{1,3},{2,0},{3,1},{4,6},{5,7},{6,4},{7,5},{8,10},{9,11},{10,... | collective-permute-start | bytes 221192 | tf_op jit(solution)/shard_map/ppermute | solution.py:274
  26.3 5.0 %collective-permute-start.2 = (f32[72,256]{1,0:T(8,128)S(1)}, f32[72,256]{1,0:T(8,128)S(1)}, u32[]{:S(2)}, u32[]{:S(2)}) collective-permute-start(f32[72,256]{1,0:T(8,128)S(1)} %pad_maximum_fusion.1), channel_id=1, source_target_pairs={{0,4},{1,5},{2,6},{3,7},{4,0},{5,1},{6,2},{7,3},{8,12},{9,13},{10,... | collective-permute-start | bytes 221192 | tf_op jit(solution)/shard_map/ppermute | solution.py:274
  28.8 8.0 %collective-permute-start.6 = (f32[72,256]{1,0:T(8,128)S(1)}, f32[72,256]{1,0:T(8,128)S(1)}, u32[]{:S(2)}, u32[]{:S(2)}) collective-permute-start(f32[72,256]{1,0:T(8,128)S(1)} %pad_maximum_fusion.4), channel_id=1, source_target_pairs={{0,4},{1,5},{2,6},{3,7},{4,0},{5,1},{6,2},{7,3},{8,12},{9,13},{10,... | collective-permute-start | bytes 221192 | tf_op jit(solution)/shard_map/ppermute | solution.py:274
  32.1 6.7 %collective-permute-start.3 = (f32[72,256]{1,0:T(8,128)S(1)}, f32[72,256]{1,0:T(8,128)S(1)}, u32[]{:S(2)}, u32[]{:S(2)}) collective-permute-start(f32[72,256]{1,0:T(8,128)S(1)} %pad_maximum_fusion.2), channel_id=1, source_target_pairs={{0,8},{1,9},{2,10},{3,11},{4,12},{5,13},{6,14},{7,15},{16,24},{17,... | collective-permute-start | bytes 221192 | tf_op jit(solution)/shard_map/ppermute | solution.py:311
  36.8 12.6 %collective-permute-start.7 = (f32[72,256]{1,0:T(8,128)S(1)}, f32[72,256]{1,0:T(8,128)S(1)}, u32[]{:S(2)}, u32[]{:S(2)}) collective-permute-start(f32[72,256]{1,0:T(8,128)S(1)} %pad_maximum_fusion.5), channel_id=1, source_target_pairs={{8,0},{9,1},{10,2},{11,3},{12,4},{13,5},{14,6},{15,7},{24,16},{25,... | collective-permute-start | bytes 221192 | tf_op jit(solution)/shard_map/ppermute | solution.py:311
  39.6 2.2 %copy-start.19 = (f32[64,2,32,256]{3,2,1,0:T(8,128)S(1)}, f32[64,2,32,256]{3,2,1,0:T(8,128)}, u32[]{:S(2)}) copy-start(f32[64,2,32,256]{3,2,1,0:T(8,128)} %copy-done.18) | copy-start | bytes 12582916
  41.8 7.7 %copy-start.6 = (bf16[64,2,32,256]{3,2,1,0:T(8,128)(2,1)S(1)}, bf16[64,2,32,256]{3,2,1,0:T(8,128)(2,1)}, u32[]{:S(2)}) copy-start(bf16[64,2,32,256]{3,2,1,0:T(8,128)(2,1)} %latents_ref.1) | copy-start | bytes 6291460
  41.8 7.7 %copy-start.13 = (f32[64,2,32,256]{3,2,1,0:T(8,128)S(1)}, f32[64,2,32,256]{3,2,1,0:T(8,128)}, u32[]{:S(2)}) copy-start(f32[64,2,32,256]{3,2,1,0:T(8,128)} %copy-done.12) | copy-start | bytes 12582916
  48.4 1.1 copy-start.1
  49.5 6.2 %copy-start.14 = (bf16[64,2,32,256]{3,2,1,0:T(8,128)(2,1)}, bf16[64,2,32,256]{3,2,1,0:T(8,128)(2,1)S(1)}, u32[]{:S(2)}) copy-start(bf16[64,2,32,256]{3,2,1,0:T(8,128)(2,1)S(1)} %get-tuple-element.29.value_ref.states_ref.previous_ref) | copy-start | bytes 6291460
  55.7 1.0 copy-start
  56.7 1.3 copy-start.16
  58.0 4.5 %collective-permute-start.8 = (f32[1160,256]{1,0:T(8,128)S(1)}, f32[1160,256]{1,0:T(8,128)S(1)}, u32[]{:S(2)}, u32[]{:S(2)}) collective-permute-start(f32[1160,256]{1,0:T(8,128)S(1)} %get-tuple-element.34), channel_id=1, source_target_pairs={{0,1},{1,0},{2,3},{3,2},{4,5},{5,4},{6,7},{7,6},{8,9},{9,8},{10,11... | collective-permute-start | bytes 3563528 | tf_op jit(solution)/shard_map/ppermute | solution.py:274
  58.0 10.1 %collective-permute-start.16 = (f32[1152,256]{1,0:T(8,128)}, f32[1152,256]{1,0:T(8,128)S(1)}, u32[]{:S(2)}, u32[]{:S(2)}) collective-permute-start(f32[1152,256]{1,0:T(8,128)} %get-tuple-element.42), channel_id=1, source_target_pairs={{0,1},{1,0},{2,3},{3,2},{4,5},{5,4},{6,7},{7,6},{8,9},{9,8},{10,11... | collective-permute-start | bytes 3538952 | tf_op jit(solution)/shard_map/ppermute | solution.py:274
  62.5 1.0 copy-start.20
  66.4 16.6 %collective-permute-start.9 = (f32[584,256]{1,0:T(8,128)}, f32[584,256]{1,0:T(8,128)S(1)}, u32[]{:S(2)}, u32[]{:S(2)}) collective-permute-start(f32[584,256]{1,0:T(8,128)} %get-tuple-element.36), channel_id=1, source_target_pairs={{0,2},{1,3},{2,0},{3,1},{4,6},{5,7},{6,4},{7,5},{8,10},{9,11},{10,... | collective-permute-start | bytes 1794056 | tf_op jit(solution)/shard_map/ppermute | solution.py:274
  68.1 1.0 copy-start.23
  71.8 22.9 %collective-permute-start.17 = (f32[576,256]{1,0:T(8,128)}, f32[576,256]{1,0:T(8,128)S(1)}, u32[]{:S(2)}, u32[]{:S(2)}) collective-permute-start(f32[576,256]{1,0:T(8,128)} %get-tuple-element.44), channel_id=1, source_target_pairs={{0,2},{1,3},{2,0},{3,1},{4,6},{5,7},{6,4},{7,5},{8,10},{9,11},{10,... | collective-permute-start | bytes 1769480 | tf_op jit(solution)/shard_map/ppermute | solution.py:274
  82.9 0.8 copy-start.24
  85.9 14.0 %collective-permute-start.10 = (f32[296,256]{1,0:T(8,128)}, f32[296,256]{1,0:T(8,128)S(1)}, u32[]{:S(2)}, u32[]{:S(2)}) collective-permute-start(f32[296,256]{1,0:T(8,128)} %get-tuple-element.38), channel_id=1, source_target_pairs={{0,4},{1,5},{2,6},{3,7},{4,0},{5,1},{6,2},{7,3},{8,12},{9,13},{10,... | collective-permute-start | bytes 909320 | tf_op jit(solution)/shard_map/ppermute | solution.py:274
  94.8 0.8 copy-start.27
  97.8 11.5 %collective-permute-start.18 = (f32[288,256]{1,0:T(8,128)}, f32[288,256]{1,0:T(8,128)S(1)}, u32[]{:S(2)}, u32[]{:S(2)}) collective-permute-start(f32[288,256]{1,0:T(8,128)} %get-tuple-element.46), channel_id=1, source_target_pairs={{0,4},{1,5},{2,6},{3,7},{4,0},{5,1},{6,2},{7,3},{8,12},{9,13},{10,... | collective-permute-start | bytes 884744 | tf_op jit(solution)/shard_map/ppermute | solution.py:274
  99.9 0.7 copy-start.29
  102.4 20.1 %collective-permute-start.11 = (f32[152,256]{1,0:T(8,128)}, f32[152,256]{1,0:T(8,128)S(1)}, u32[]{:S(2)}, u32[]{:S(2)}) collective-permute-start(f32[152,256]{1,0:T(8,128)} %get-tuple-element.40), channel_id=1, source_target_pairs={{0,8},{1,9},{2,10},{3,11},{4,12},{5,13},{6,14},{7,15},{8,0},{9,1},... | collective-permute-start | bytes 466952 | tf_op jit(solution)/shard_map/ppermute | solution.py:274
  109.3 0.7 copy-start.30
  111.8 8.0 %collective-permute-start.19 = (f32[144,256]{1,0:T(8,128)}, f32[144,256]{1,0:T(8,128)S(1)}, u32[]{:S(2)}, u32[]{:S(2)}) collective-permute-start(f32[144,256]{1,0:T(8,128)} %get-tuple-element.48), channel_id=1, source_target_pairs={{0,8},{1,9},{2,10},{3,11},{4,12},{5,13},{6,14},{7,15},{8,0},{9,1},... | collective-permute-start | bytes 442376 | tf_op jit(solution)/shard_map/ppermute | solution.py:274
  119.8 0.7 copy-start.36
  122.1 10.8 %collective-permute-start.20 = (f32[144,256]{1,0:T(8,128)}, f32[144,256]{1,0:T(8,128)S(1)}, u32[]{:S(2)}, u32[]{:S(2)}) collective-permute-start(f32[144,256]{1,0:T(8,128)} %fold.15.mine_ref), channel_id=1, source_target_pairs={{0,8},{1,9},{2,10},{3,11},{4,12},{5,13},{6,14},{7,15},{8,0},{9,1},... | collective-permute-start | bytes 442376 | tf_op jit(solution)/shard_map/ppermute | solution.py:274
  122.6 0.7 copy-start.33
  125.9 10.3 %copy-start.28 = (f32[144,256]{1,0:T(8,128)}, f32[144,256]{1,0:T(8,128)S(1)}, u32[]{:S(2)}) copy-start(f32[144,256]{1,0:T(8,128)S(1)} %slice.96.mine_ref) | copy-start | bytes 442372
  125.9 10.3 %collective-permute-start.12 = (f32[144,256]{1,0:T(8,128)S(1)}, f32[144,256]{1,0:T(8,128)S(1)}, u32[]{:S(2)}, u32[]{:S(2)}) collective-permute-start(f32[144,256]{1,0:T(8,128)S(1)} %slice.96.mine_ref), channel_id=1, source_target_pairs={{0,8},{1,9},{2,10},{3,11},{4,12},{5,13},{6,14},{7,15},{8,0},{9,1},... | collective-permute-start | bytes 442376 | tf_op jit(solution)/shard_map/ppermute | solution.py:274
  132.9 0.7 copy-start.34
  135.3 10.0 %collective-permute-start.21 = (f32[288,256]{1,0:T(8,128)}, f32[288,256]{1,0:T(8,128)S(1)}, u32[]{:S(2)}, u32[]{:S(2)}) collective-permute-start(f32[288,256]{1,0:T(8,128)} %merge.12.mine_ref), channel_id=1, source_target_pairs={{0,4},{1,5},{2,6},{3,7},{4,0},{5,1},{6,2},{7,3},{8,12},{9,13},{10,... | collective-permute-start | bytes 884744 | tf_op jit(solution)/shard_map/ppermute | solution.py:274
  136.1 0.6 copy-start.35
  138.5 11.1 %collective-permute-start.13 = (f32[288,256]{1,0:T(8,128)}, f32[288,256]{1,0:T(8,128)S(1)}, u32[]{:S(2)}, u32[]{:S(2)}) collective-permute-start(f32[288,256]{1,0:T(8,128)} %merge.8.mine_ref), channel_id=1, source_target_pairs={{0,4},{1,5},{2,6},{3,7},{4,0},{5,1},{6,2},{7,3},{8,12},{9,13},{10,... | collective-permute-start | bytes 884744 | tf_op jit(solution)/shard_map/ppermute | solution.py:274
  145.2 0.7 copy-start.31
  147.9 15.4 %collective-permute-start.22 = (f32[576,256]{1,0:T(8,128)}, f32[576,256]{1,0:T(8,128)S(1)}, u32[]{:S(2)}, u32[]{:S(2)}) collective-permute-start(f32[576,256]{1,0:T(8,128)} %merge.13.mine_ref), channel_id=1, source_target_pairs={{0,2},{1,3},{2,0},{3,1},{4,6},{5,7},{6,4},{7,5},{8,10},{9,11},{10,... | collective-permute-start | bytes 1769480 | tf_op jit(solution)/shard_map/ppermute | solution.py:274
  149.6 0.7 copy-start.32
  152.2 17.4 %collective-permute-start.14 = (f32[576,256]{1,0:T(8,128)}, f32[576,256]{1,0:T(8,128)S(1)}, u32[]{:S(2)}, u32[]{:S(2)}) collective-permute-start(f32[576,256]{1,0:T(8,128)} %merge.9.mine_ref), channel_id=1, source_target_pairs={{0,2},{1,3},{2,0},{3,1},{4,6},{5,7},{6,4},{7,5},{8,10},{9,11},{10,... | collective-permute-start | bytes 1769480 | tf_op jit(solution)/shard_map/ppermute | solution.py:274
  163.3 0.8 copy-start.25
  166.5 19.2 %collective-permute-start.23 = (f32[1152,256]{1,0:T(8,128)}, f32[1152,256]{1,0:T(8,128)S(1)}, u32[]{:S(2)}, u32[]{:S(2)}) collective-permute-start(f32[1152,256]{1,0:T(8,128)} %merge.14.mine_ref), channel_id=1, source_target_pairs={{0,1},{1,0},{2,3},{3,2},{4,5},{5,4},{6,7},{7,6},{8,9},{9,8},{10,11... | collective-permute-start | bytes 3538952 | tf_op jit(solution)/shard_map/ppermute | solution.py:274
  169.7 0.8 copy-start.26
  172.8 6.5 %copy-start.9 = (bf16[9,256,256]{2,1,0:T(8,128)(2,1)S(1)}, bf16[9,256,256]{2,1,0:T(8,128)(2,1)}, u32[]{:S(2)}) copy-start(bf16[9,256,256]{2,1,0:T(8,128)(2,1)} %weights_ref.7) | copy-start | bytes 3538948
  172.8 17.1 %collective-permute-start.15 = (f32[1152,256]{1,0:T(8,128)}, f32[1152,256]{1,0:T(8,128)S(1)}, u32[]{:S(2)}, u32[]{:S(2)}) collective-permute-start(f32[1152,256]{1,0:T(8,128)} %merge.10.mine_ref), channel_id=1, source_target_pairs={{0,1},{1,0},{2,3},{3,2},{4,5},{5,4},{6,7},{7,6},{8,9},{9,8},{10,11... | collective-permute-start | bytes 3538952 | tf_op jit(solution)/shard_map/ppermute | solution.py:274
  172.8 1.7 copy-start.15
  174.5 4.8 %copy-start.17 = (bf16[64,2,32,256]{3,2,1,0:T(8,128)(2,1)S(1)}, bf16[64,2,32,256]{3,2,1,0:T(8,128)(2,1)}, u32[]{:S(2)}) copy-start(bf16[64,2,32,256]{3,2,1,0:T(8,128)(2,1)} %copy-done.16) | copy-start | bytes 6291460
  185.7 1.0 copy-start.21
  189.9 1.0 copy-start.22

commit v2 on v1

--- a/solution.py
+++ b/solution.py
@@ -11,7 +11,7 @@
 F32 = jnp.float32
 BF16 = jnp.bfloat16
 EXTRA = 8
-VMEM_LIMIT = 40 * 1024 * 1024
+VMEM_LIMIT = 20 * 1024 * 1024
 
 
 def column_shifts(value):
@@ -45,21 +45,24 @@
     return jnp.exp(-(step * rate))
 
 
-def drive_kernel(reverse, step_ref, rate_ref, value_ref, weights_ref, driven_ref, carry_ref, state, decay, flipped):
+def drive_kernel(reverse, base, fresh, step_ref, rate_ref, value_ref, weights_ref, *refs):
+    start_ref, refs = (None, refs) if fresh else (refs[0], refs[1:])
+    driven_ref, carry_ref, state, decay, flipped = refs
     index, count = pl.program_id(0), pl.num_programs(0)
     block, _, breadth, channels = driven_ref.shape
+    map_rows = state.shape[0] * 8
 
     @pl.when(index == 0)
     def _():
-        state[...] = jnp.zeros_like(state)
-        decay[...] = jnp.ones_like(decay)
+        state[...] = jnp.zeros_like(state) if fresh else start_ref[:map_rows].reshape(state.shape)
+        decay[...] = jnp.ones_like(decay) if fresh else start_ref[map_rows:]
         if reverse:
             flip_into(flipped, weights_ref)
 
     outs = conv_rows(value_ref[...], flipped if reverse else weights_ref)
     for row, out in enumerate(outs):
         driven_ref[:, row] = out.reshape(block, breadth, channels)
-    first = (count - 1 - index if reverse else index) * block
+    first = (base + (count - 1 - index if reverse else index)) * block
     rate = jnp.broadcast_to(rate_ref[...], decay.shape)
     total, held = decay[...], state[...]
     for offset in range(block):
@@ -73,9 +76,8 @@
 
     @pl.when(index == count - 1)
     def _():
-        rows = state.shape[0] * 8
-        carry_ref[:rows] = held.reshape(rows, channels)
-        carry_ref[rows:] = total
+        carry_ref[:map_rows] = held.reshape(map_rows, channels)
+        carry_ref[map_rows:] = total
 
 
 def add_kernel_grad(sums, source, target):
@@ -130,12 +132,14 @@
 
 def adjoint_kernel(
     scale,
+    late_steps,
     step_ref,
     core_ref,
     rate_ref,
     arriving_ref,
     incoming_ref,
-    pulled_ref,
+    late_ref,
+    early_ref,
     latents_ref,
     states_ref,
     previous_ref,
@@ -148,7 +152,7 @@
     whole,
 ):
     index, count = pl.program_id(0), pl.num_programs(0)
-    block = pulled_ref.shape[0]
+    block = late_ref.shape[0]
     first = (count - 1 - index) * block
 
     @pl.when(index == 0)
@@ -161,7 +165,8 @@
     held, summed = carry[...], rate_sum[...]
     for frame in range(block - 1, -1, -1):
         step = step_ref[first + frame]
-        adjoint = held + pulled_ref[frame].reshape(carry.shape)
+        pulled = jnp.where(index < late_steps, late_ref[frame], early_ref[frame])
+        adjoint = held + pulled.reshape(carry.shape)
         low_ref[frame] = adjoint.astype(BF16).reshape(low_ref.shape[1:])
         held = decay_of(step, rate)[None] * adjoint
         if frame:
@@ -212,6 +217,10 @@
     )
 
 
+def far(value):
+    return pltpu.with_memory_space_constraint(value, pltpu.HBM)
+
+
 def smem():
     return pl.BlockSpec(memory_space=pltpu.SMEM)
 
@@ -220,54 +229,17 @@
     return pl.BlockSpec(shape, lambda g: (0,) * len(shape))
 
 
-def framed(shape, block, count, reverse):
-    return pl.BlockSpec((block,) + shape[1:], lambda g: ((count - 1 - g if reverse else g), 0, 0, 0))
-
-
-def fold(bit, keep, recv, main, last):
-    rows, columns = keep.shape
-    extra = rows - main
-    half = main if last else main // 2
-
-    def kernel(bit_ref, keep_ref, recv_ref, *outs):
-        if last:
-            outs[0][...] = keep_ref[...] + recv_ref[...]
-            return
-        for out, part in zip(outs, (bit_ref[0], 1 - bit_ref[0])):
-            window = pl.ds(part * half, half)
-            out[:half] = keep_ref[window] + recv_ref[window]
-            if extra:
-                out[half:] = keep_ref[main:] + recv_ref[main:]
-
-    shape = jax.ShapeDtypeStruct((half + extra, columns), F32)
-    outs = [shape] if last else [shape, shape]
-    whole = pl.BlockSpec(memory_space=pltpu.VMEM)
-    return pl.pallas_call(
-        kernel,
-        in_specs=[smem(), whole, whole],
-        out_specs=[whole] * len(outs),
-        out_shape=outs,
-        cost_estimate=pl.CostEstimate(flops=rows * columns, bytes_accessed=12 * rows * columns, transcendentals=0),
-        name="fold",
-    )(bit, keep, recv)
+def framed(shape, block, count, reverse, base=0):
+    return pl.BlockSpec((block,) + shape[1:], lambda g: (base + (count - 1 - g if reverse else g), 0, 0, 0))
+
+
+def part_of(bit, value):
+    half = value.shape[0] // 2
+    return lax.dynamic_slice_in_dim(value, bit[0] * half, half)
 
 
 def merge(bit, mine, other):
-    rows, columns = mine.shape
-
-    def kernel(bit_ref, mine_ref, other_ref, out_ref):
-        out_ref[pl.ds(bit_ref[0] * rows, rows)] = mine_ref[...]
-        out_ref[pl.ds((1 - bit_ref[0]) * rows, rows)] = other_ref[...]
-
-    whole = pl.BlockSpec(memory_space=pltpu.VMEM)
-    return pl.pallas_call(
-        kernel,
-        in_specs=[smem(), whole, whole],
-        out_specs=whole,
-        out_shape=jax.ShapeDtypeStruct((2 * rows, columns), F32),
-        cost_estimate=pl.CostEstimate(flops=0, bytes_accessed=16 * rows * columns, transcendentals=0),
-        name="merge",
-    )(bit, mine, other)
+    return jnp.where(bit[0] == 0, jnp.concatenate([mine, other]), jnp.concatenate([other, mine]))
 
 
 def swap(value, count, distance):
@@ -278,44 +250,86 @@
     return [jnp.bitwise_and(lax.shift_right_logical(me, level), 1).reshape(1) for level in range(levels)]
 
 
-def sum_over(keep, send, main, bits, count):
-    levels = len(bits)
-    for level in range(levels):
-        recv = swap(send, count, 1 << level)
-        last = level == levels - 1
-        if last:
-            (keep,) = fold(bits[level], keep, recv, main, True)
+def after(value, *others):
+    return lax.optimization_barrier((value, *others))[0]
+
+
+class Sum:
+    def __init__(self, keep, send, main, bits, orders, count):
+        self.keep, self.send, self.main, self.count = keep, send, main, count
+        self.orders = orders
+        self.bits = [jnp.where(bits[0] == 0, bits[even], bits[odd]) for even, odd in zip(*orders)]
+        self.stage = 0
+        self.left = 2 * len(self.bits)
+
+    def swap(self, value):
+        levels = [order[self.stage] for order in self.orders]
+        return lax.ppermute(value, "tm", [(source, source ^ (1 << levels[source & 1])) for source in range(self.count)])
+
+    def start(self):
+        self.recv = self.swap(self.send)
+
+    def wait(self, *others):
+        self.recv = after(self.recv, *others)
+
+    def fold(self):
+        total_main = self.keep[: self.main] + self.recv[: self.main]
+        total_extra = self.keep[self.main :] + self.recv[self.main :]
+        self.stage += 1
+        if self.stage == len(self.bits):
+            self.send, self.extra = total_main, total_extra
+            return
+        bit = self.bits[self.stage]
+        self.keep = jnp.concatenate([part_of(bit, total_main), total_extra])
+        self.send = jnp.concatenate([part_of(1 - bit, total_main), total_extra])
+        self.main = self.main // 2
+
+    def step(self):
+        if self.left == 0:
+            return
+        if self.left > len(self.bits):
+            self.fold()
         else:
-            keep, send = fold(bits[level + 1], keep, recv, main, False)
-            main = main // 2
-    extra = keep[main:]
-    piece = keep[:main]
-    for level in range(levels - 1, -1, -1):
-        piece = merge(bits[level], piece, swap(piece, count, 1 << level))
-    return piece, extra
-
-
-def carry_in(carry, bits, count, reverse):
-    rows = carry.shape[0] - 8
-    local, decay = carry[:rows].reshape(rows // 8, 8, -1), carry[rows:][None]
-    reached, passed = jnp.zeros_like(local), jnp.ones_like(decay)
-    levels = len(bits)
-    for level in range(levels):
-        distance = 1 << level
-        message = jnp.concatenate([local.reshape(rows, -1), decay[0]], axis=0)
-        if level < levels - 1:
-            other = swap(message, count, distance)
-        else:
-            towards = 0 if reverse else distance
-            pairs = [(source, source ^ distance) for source in range(count) if (source ^ distance) & distance == towards]
-            other = lax.ppermute(message, "tm", pairs)
-        other_local, other_decay = other[:rows].reshape(rows // 8, 8, -1), other[rows:][None]
-        later = bits[level][0] == (0 if reverse else 1)
-        reached = jnp.where(later, reached + passed * other_local, reached)
-        passed = jnp.where(later, passed * other_decay, passed)
+            self.send = merge(self.bits[self.stage], self.send, self.recv)
+        self.left -= 1
+        if self.left > len(self.bits):
+            self.start()
+        elif self.left:
+            self.stage -= 1
+            self.start()
+
+
+class Carry:
+    def __init__(self, message, bits, count, reverse):
+        self.message, self.bits, self.count, self.reverse = message, bits, count, reverse
+        self.rows = message.shape[0] - 8
+        self.reached = jnp.zeros((self.rows // 8, 8, message.shape[1]), F32)
+        self.passed = jnp.ones((1, 8, message.shape[1]), F32)
+        self.level = 0
+
+    def split(self, message):
+        return message[: self.rows].reshape(self.reached.shape), message[self.rows :][None]
+
+    def start(self):
+        distance = 1 << self.level
+        pairs = [(source, source ^ distance) for source in range(self.count)]
+        if self.level == len(self.bits) - 1:
+            towards = 0 if self.reverse else distance
+            pairs = [pair for pair in pairs if pair[1] & distance == towards]
+        self.other = lax.ppermute(self.message, "tm", pairs)
+
+    def combine(self, *others):
+        self.other = after(self.other, *others)
+        (local, decay), (other_local, other_decay) = self.split(self.message), self.split(self.other)
+        later = self.bits[self.level][0] == (0 if self.reverse else 1)
+        self.reached = jnp.where(later, self.reached + self.passed * other_local, self.reached)
+        self.passed = jnp.where(later, self.passed * other_decay, self.passed)
         local = jnp.where(later, decay * other_local + local, other_decay * local + other_local)
-        decay = decay * other_decay
-    return reached.reshape(rows, -1)
+        self.level += 1
+        self.message = jnp.concatenate([local.reshape(self.rows, -1), (decay * other_decay)[0]], axis=0)
+
+    def result(self):
+        return self.reached.reshape(self.rows, -1)
 
 
 def body(latents, input_map, output_map, decay_rate, frame_step, cotangent):
@@ -334,29 +348,51 @@
     weights = input_map.shape
     pixels = frames * height * breadth
     flops = 2 * pixels * 6 * channels * channels
-    driven_type = jax.ShapeDtypeStruct(shape, F32)
-    low_type = jax.ShapeDtypeStruct(shape, BF16)
+    driven_type = pltpu.HBM(shape, F32)
+    low_type = pltpu.HBM(shape, BF16)
     map_scratch = pltpu.VMEM((map_rows // 8, 8, channels), F32)
     decay_scratch = pltpu.VMEM((8, channels), F32)
     flip_scratch = pltpu.VMEM(weights, BF16)
 
-    def drive(value, kernel_map, reverse):
+    def drive(value, kernel_map, reverse, base, size, start=None):
+        specs = [smem(), fixed(rate.shape), framed(shape, block, size, reverse, base), fixed(weights)]
+        operands = [frame_step, rate, far(value), far(kernel_map)]
+        if start is not None:
+            specs.append(fixed((map_rows + 8, channels)))
+            operands.append(start)
         return call(
-            functools.partial(drive_kernel, reverse),
-            grid,
-            [smem(), fixed(rate.shape), framed(shape, block, steps, reverse), fixed(weights)],
-            [framed(shape, block, steps, reverse), fixed((map_rows + 8, channels))],
-            [driven_type, jax.ShapeDtypeStruct((map_rows + 8, channels), F32)],
+            functools.partial(drive_kernel, reverse, base, start is None),
+            (size,),
+            specs,
+            [framed(shape, block, size, reverse), fixed((map_rows + 8, channels))],
+            [pltpu.HBM((size * block,) + shape[1:], F32), jax.ShapeDtypeStruct((map_rows + 8, channels), F32)],
             [map_scratch, decay_scratch, flip_scratch],
-            flops,
-            pixels * channels * 6,
+            flops * size // steps,
+            pixels * channels * 6 * size // steps,
             "pull" if reverse else "drive",
-        )(frame_step, rate, value, kernel_map)
-
-    driven, forward_carry = drive(latents, input_map, False)
-    pulled, backward_carry = drive(cotangent, output_map, True)
-    incoming = carry_in(forward_carry, bits, count, False)
-    arriving = carry_in(backward_carry, bits, count, True)
+        )(*operands)
+
+    driven, forward_carry = drive(latents, input_map, False, 0, steps)
+    forward = Carry(forward_carry, bits, count, False)
+    forward.start()
+    later = steps // 2
+    pulled_late, late_carry = drive(after(cotangent, forward_carry), output_map, True, later, steps - later)
+    forward.combine(late_carry)
+    forward.start()
+    pulled_early, backward_carry = drive(cotangent, output_map, True, 0, later, after(late_carry, forward.message))
+    forward.combine(backward_carry)
+    forward.start()
+    backward = Carry(after(backward_carry, forward.message), bits, count, True)
+    backward.start()
+    for _ in range(levels - 3):
+        forward.combine()
+        forward.start()
+        backward.combine(forward.message)
+        backward.start()
+    forward.combine()
+    incoming = forward.result()
+    backward.combine(incoming)
+    backward.start()
 
     grad_rows = 9 * channels
     half = grad_rows // 2
@@ -382,29 +418,7 @@
         flops,
         pixels * channels * 8,
         "states",
-    )(frame_step, bits[0], rate, incoming, driven, cotangent)
-
-    adjoint_low, in_keep, in_send = call(
-        functools.partial(adjoint_kernel, factor),
-        grid,
-        [
-            smem(),
-            smem(),
-            fixed(rate.shape),
-            fixed(incoming.shape),
-            fixed(incoming.shape),
-            framed(shape, block, steps, True),
-            framed(shape, block, steps, True),
-            framed(shape, block, steps, True),
-            pl.BlockSpec((1,) + shape[1:], lambda g: (jnp.maximum((steps - 1 - g) * block - 1, 0), 0, 0, 0)),
-        ],
-        [framed(shape, block, steps, True), fixed(half_extra.shape), fixed(half_extra.shape)],
-        [low_type, half_extra, half_extra],
-        [map_scratch, decay_scratch, sums_scratch, whole_scratch],
-        flops,
-        pixels * channels * 10,
-        "adjoint",
-    )(frame_step, bits[0], rate, arriving, incoming, pulled, latents, states_low, states_low)
+    )(frame_step, bits[0], rate, after(incoming, backward.message), far(driven), far(cotangent))
 
     def conv(value, kernel_map, reverse):
         return call(
@@ -417,12 +431,69 @@
             flops,
             pixels * channels * 4,
             "conv",
-        )(value, kernel_map)
-
-    layer_out = conv(states_low, output_map, False)
-    grad_latents = conv(adjoint_low, input_map, True)
-    grad_output_map, _ = sum_over(out_keep, out_send, half, bits, count)
-    grad_input_map, rate_rows = sum_over(in_keep, in_send, half, bits, count)
+        )(far(value), far(kernel_map))
+
+    orders = (list(range(levels)), [0] + list(range(2, levels)) + [1])
+    backward.combine(out_send)
+    backward.start()
+    out_sum = Sum(out_keep, after(out_send, backward.message), half, bits, orders, count)
+    out_sum.start()
+    out_sum.step()
+    backward.combine(out_sum.send)
+    arriving = backward.result()
+
+    adjoint_low, in_keep, in_send = call(
+        functools.partial(adjoint_kernel, factor, steps - later),
+        grid,
+        [
+            smem(),
+            smem(),
+            fixed(rate.shape),
+            fixed(incoming.shape),
+            fixed(incoming.shape),
+            pl.BlockSpec((block,) + shape[1:], lambda g: (jnp.maximum(steps - 1 - g - later, 0), 0, 0, 0)),
+            pl.BlockSpec((block,) + shape[1:], lambda g: (jnp.minimum(steps - 1 - g, later - 1), 0, 0, 0)),
+            framed(shape, block, steps, True),
+            framed(shape, block, steps, True),
+            pl.BlockSpec((1,) + shape[1:], lambda g: (jnp.maximum((steps - 1 - g) * block - 1, 0), 0, 0, 0)),
+        ],
+        [framed(shape, block, steps, True), fixed(half_extra.shape), fixed(half_extra.shape)],
+        [low_type, half_extra, half_extra],
+        [map_scratch, decay_scratch, sums_scratch, whole_scratch],
+        flops,
+        pixels * channels * 10,
+        "adjoint",
+    )(
+        frame_step,
+        bits[0],
+        rate,
+        arriving,
+        incoming,
+        far(pulled_late),
+        far(pulled_early),
+        far(latents),
+        far(states_low),
+        far(states_low),
+    )
+
+    out_sum.wait(in_send)
+    out_sum.step()
+    in_sum = Sum(in_keep, after(in_send, out_sum.send), half, bits, orders, count)
+    in_sum.start()
+    in_sum.step()
+    fillers = [(adjoint_low, input_map, True), (states_low, output_map, False)]
+    results = []
+    for stage in range(1, 2 * levels):
+        if fillers:
+            value, kernel_map, reverse = fillers.pop()
+            results.append(conv(after(value, in_sum.send), kernel_map, reverse))
+            out_sum.wait(results[-1])
+        out_sum.wait(in_sum.send)
+        out_sum.step()
+        in_sum.wait(out_sum.send)
+        in_sum.step()
+    layer_out, grad_latents = results
+    grad_output_map, grad_input_map, rate_rows = out_sum.send, in_sum.send, in_sum.extra
     grad_log_rate = -factor * decay_rate * jnp.sum(rate_rows, axis=0)
     return (
         layer_out,

time: 196 us -> 144 us (0.73)
  local copies, waits for them, and re-layouts: 29.2 us -> 1.54 us
  Pallas kernels: 67.7 us -> 46.7 us
  starting transfers between devices: 31.8 us -> 16.8 us
  waiting for transfers between devices: 59.9 us -> 67.2 us
  other arithmetic: 4.58 us -> 9.55 us
    unnamed x74 -> x12, local copies, waits for them, and re-layouts: 28.3 us -> 1.34 us
    pallas_call x19 -> x4, Pallas kernels: 51.2 us -> 25.6 us  [the longest x3 16.8 us: drive(): call(functools.partial(drive_kernel, reverse, base, start is None), (size...]
    ppermute x24, starting transfers between devices: 31.8 us -> 16.8 us  [the longest x8 12.9 us: start(): self.other = lax.ppermute(self.message, 'tm', pairs)]
    ppermute x24, waiting for transfers between devices: 59.9 us -> 67.2 us  [the longest x16 56.6 us: swap(): lax.ppermute(value, 'tm', [(source, source ^ 1 << levels[source & 1]) for...]
    add x0 -> x11, other arithmetic: none -> 4.89 us  [the longest x8 4.18 us: fold(): total_main = self.keep[:self.main] + self.recv[:self.main]]
    pallas_call x2, Pallas kernels: 9.9 us -> 13.3 us  [conv(): call(functools.partial(conv_kernel, reverse), grid, [framed(shape, block,...]
    select_n x10 -> x18, other arithmetic: 2.55 us -> 3.93 us  [the longest x8 3.74 us: merge(): jnp.where(bit[0] == 0, jnp.concatenate([mine, other]), jnp.concatenate([o...]
  transfers between devices with their start and end apart: 24 -> 24, of which waited for: 13 -> 16; matrix products, arithmetic and copies ran while one was open for 3% -> 5% of each run, Pallas kernels for 28% -> 28%
where the time goes in v2:
time: 144 us; the launch traced here: 143 us
  waiting for transfers between devices  67.2 us (47%)
  Pallas kernels  46.7 us (32%)
  starting transfers between devices  16.8 us (12%)
  other arithmetic  9.55 us (7%)
  local copies, waits for them, and re-layouts  1.54 us (1%)
    ppermute x16, waiting for transfers between devices, swap(): lax.ppermute(value, 'tm', [(source, source ^ 1 << levels[source & 1]) for...  56.6 us
    pallas_call x3, Pallas kernels, drive(): call(functools.partial(drive_kernel, reverse, base, start is None), (size...  16.8 us
    pallas_call x2, Pallas kernels, conv(): call(functools.partial(conv_kernel, reverse), grid, [framed(shape, block,...  13.3 us
    ppermute x8, starting transfers between devices, start(): self.other = lax.ppermute(self.message, 'tm', pairs)  12.9 us
    ppermute x8, waiting for transfers between devices, start(): self.other = lax.ppermute(self.message, 'tm', pairs)  10.6 us
    pallas_call x1, Pallas kernels, body(): call(functools.partial(adjoint_kernel, factor, steps - later), grid, [sme...  8.87 us
    pallas_call x1, Pallas kernels, body(): call(functools.partial(state_kernel, factor), grid, [smem(), smem(), fixe...  7.7 us
    add x8, other arithmetic, fold(): total_main = self.keep[:self.main] + self.recv[:self.main]  4.18 us
  transfers between devices with their start and end apart: 24, of which 16 were waited for; matrix products, arithmetic and copies ran while one was open for 5% of the time, Pallas kernels for 28%

profile of v2, /device:TPU:0, one launch (start us, length us, event | category | flops | bytes accessed | tf_op | source)
XLA Modules:
  0.0 142.8 jit_solution(8431733139426212735)
XLA Ops:
  0.6 0.0 copy-start
  0.6 0.7 copy-done
  1.3 0.7 copy-done.2
  2.0 6.9 %drive.1 = (f32[64,2,32,256]{3,2,1,0:T(8,128)}, f32[72,256]{1,0:T(8,128)S(1)}) custom-call(f32[64]{0:T(128)S(1)} %copy-done.2, f32[1,256]{1,0:T(1,128)S(1)} %bitcast.110, bf16[64,2,32,256]{3,2,1,0:T(8,128)(2,1)} %latents_ref.1, bf16[9,256,256]{2,1,0:T(8,128)(2,1)} %weights_ref.9), custom_call_target="tpu_custom_call" | custom-call | flops 3221225472 | bytes 6291456 | tf_op jit(solution)/shard_map/drive/pallas_call | solution.py:363
  8.9 0.5 collective-permute-start
  9.3 4.9 %pull.2 = (f32[32,2,32,256]{3,2,1,0:T(8,128)}, f32[72,256]{1,0:T(8,128)S(1)}) custom-call(f32[64]{0:T(128)S(1)} %copy-done.2, f32[1,256]{1,0:T(1,128)S(1)} %bitcast.111, bf16[64,2,32,256]{3,2,1,0:T(8,128)(2,1)} %cotangent_ref.1, bf16[9,256,256]{2,1,0:T(8,128)(2,1)} %weights_ref.8), custom_call_target="tpu_custom_call" | custom-call | flops 1610612736 | bytes 3145728 | tf_op jit(solution)/shard_map/pull/pallas_call | solution.py:363
  14.3 0.0 collective-permute-done
  14.3 2.6 %collective-permute-start.1 = (f32[72,256]{1,0:T(8,128)S(1)}, f32[72,256]{1,0:T(8,128)S(1)}, u32[]{:S(2)}, u32[]{:S(2)}) collective-permute-start(f32[72,256]{1,0:T(8,128)S(1)} %pad_maximum_fusion.3), channel_id=1, source_target_pairs={{0,2},{1,3},{2,0},{3,1},{4,6},{5,7},{6,4},{7,5},{8,10},{9,11},{10,... | collective-permute-start | bytes 221192 | tf_op jit(solution)/shard_map/ppermute | solution.py:319
  16.9 4.9 %pull.3 = (f32[32,2,32,256]{3,2,1,0:T(8,128)}, f32[72,256]{1,0:T(8,128)S(1)}) custom-call(f32[64]{0:T(128)S(1)} %copy-done.3, f32[1,256]{1,0:T(1,128)S(1)} %bitcast.112, bf16[64,2,32,256]{3,2,1,0:T(8,128)(2,1)} %cotangent_ref.1, bf16[9,256,256]{2,1,0:T(8,128)(2,1)} %weights_ref.8, f32[72,256]{1,0:T(8,128)S(1)} %get-tuple-element.51.refs_0_), custom_call_target="tpu_custom_call" | custom-call | flops 1610612736 | bytes 3145728 | tf_op jit(solution)/shard_map/pull/pallas_call | solution.py:363
  21.9 0.0 collective-permute-done.1
  21.9 1.6 %collective-permute-start.2 = (f32[72,256]{1,0:T(8,128)S(1)}, f32[72,256]{1,0:T(8,128)S(1)}, u32[]{:S(2)}, u32[]{:S(2)}) collective-permute-start(f32[72,256]{1,0:T(8,128)S(1)} %pad_maximum_fusion.4), channel_id=1, source_target_pairs={{0,4},{1,5},{2,6},{3,7},{4,0},{5,1},{6,2},{7,3},{8,12},{9,13},{10,... | collective-permute-start | bytes 221192 | tf_op jit(solution)/shard_map/ppermute | solution.py:319
  23.6 0.0 collective-permute-start.4
  23.6 2.8 %collective-permute-done.2 = f32[72,256]{1,0:T(8,128)S(1)} collective-permute-done((f32[72,256]{1,0:T(8,128)S(1)}, f32[72,256]{1,0:T(8,128)S(1)}, u32[]{:S(2)}, u32[]{:S(2)}) %collective-permute-start.2) | collective-permute-done | bytes 73760 | tf_op jit(solution)/shard_map/ppermute | solution.py:319
  26.4 4.5 %collective-permute-start.3 = (f32[72,256]{1,0:T(8,128)S(1)}, f32[72,256]{1,0:T(8,128)S(1)}, u32[]{:S(2)}, u32[]{:S(2)}) collective-permute-start(f32[72,256]{1,0:T(8,128)S(1)} %pad_maximum_fusion.5), channel_id=1, source_target_pairs={{0,8},{1,9},{2,10},{3,11},{4,12},{5,13},{6,14},{7,15},{16,24},{17,... | collective-permute-start | bytes 221192 | tf_op jit(solution)/shard_map/ppermute | solution.py:319
  31.0 0.6 collective-permute-start.5
  31.5 1.3 collective-permute-done.3
  32.9 2.5 %collective-permute-done.5 = f32[72,256]{1,0:T(8,128)S(1)} collective-permute-done((f32[72,256]{1,0:T(8,128)S(1)}, f32[72,256]{1,0:T(8,128)S(1)}, u32[]{:S(2)}, u32[]{:S(2)}) %collective-permute-start.5) | collective-permute-done | bytes 73760 | tf_op jit(solution)/shard_map/ppermute | solution.py:319
  35.4 1.6 %collective-permute-start.6 = (f32[72,256]{1,0:T(8,128)S(1)}, f32[72,256]{1,0:T(8,128)S(1)}, u32[]{:S(2)}, u32[]{:S(2)}) collective-permute-start(f32[72,256]{1,0:T(8,128)S(1)} %pad_maximum_fusion.7), channel_id=1, source_target_pairs={{0,4},{1,5},{2,6},{3,7},{4,0},{5,1},{6,2},{7,3},{8,12},{9,13},{10,... | collective-permute-start | bytes 221192 | tf_op jit(solution)/shard_map/ppermute | solution.py:319
  37.1 7.7 %states.1 = (bf16[64,2,32,256]{3,2,1,0:T(8,128)(2,1)}, f32[1152,256]{1,0:T(8,128)S(1)}, f32[1152,256]{1,0:T(8,128)S(1)}) custom-call(f32[64]{0:T(128)S(1)} %copy-done.3, s32[1]{0:T(128)} %bitcast.core_ref, f32[1,256]{1,0:T(1,128)S(1)} %bitcast.113, f32[64,256]{1,0:T(8,128)S(1)} %add_select_fusion.3.incoming_ref, ...), custom_call_target="tpu_custom_call" | custom-call | flops 3221225472 | bytes 8388608 | tf_op jit(solution)/shard_map/states/pallas_call | solution.py:404
  44.8 0.0 collective-permute-done.6
  44.8 0.1 collective-permute-start.8
  44.9 1.5 %collective-permute-start.7 = (f32[72,256]{1,0:T(8,128)S(1)}, f32[72,256]{1,0:T(8,128)S(1)}, u32[]{:S(2)}, u32[]{:S(2)}) collective-permute-start(f32[72,256]{1,0:T(8,128)S(1)} %pad_maximum_fusion.8), channel_id=1, source_target_pairs={{8,0},{9,1},{10,2},{11,3},{12,4},{13,5},{14,6},{15,7},{24,16},{25,... | collective-permute-start | bytes 221192 | tf_op jit(solution)/shard_map/ppermute | solution.py:319
  46.4 1.5 %collective-permute-done.8 = f32[1152,256]{1,0:T(8,128)} collective-permute-done((f32[1152,256]{1,0:T(8,128)S(1)}, f32[1152,256]{1,0:T(8,128)}, u32[]{:S(2)}, u32[]{:S(2)}) %collective-permute-start.8) | collective-permute-done | bytes 1179680 | tf_op jit(solution)/shard_map/ppermute | solution.py:267
  47.9 1.4 add.161
  49.3 0.6 collective-permute-start.9
  49.9 4.0 %collective-permute-done.7 = f32[72,256]{1,0:T(8,128)S(1)} collective-permute-done((f32[72,256]{1,0:T(8,128)S(1)}, f32[72,256]{1,0:T(8,128)S(1)}, u32[]{:S(2)}, u32[]{:S(2)}) %collective-permute-start.7) | collective-permute-done | bytes 73760 | tf_op jit(solution)/shard_map/ppermute | solution.py:319
  54.0 8.9 %adjoint.1 = (bf16[64,2,32,256]{3,2,1,0:T(8,128)(2,1)}, f32[1160,256]{1,0:T(8,128)S(1)}, f32[1160,256]{1,0:T(8,128)S(1)}) custom-call(f32[64]{0:T(128)S(1)} %copy-done.3, s32[1]{0:T(128)} %bitcast.core_ref, f32[1,256]{1,0:T(1,128)S(1)} %bitcast.114, f32[64,256]{1,0:T(8,128)S(1)} %add_select_fusion.arriving_ref, f32[64,256]{1,0:T(8,128)S(1)} %add_select_fusion.3.incoming_ref, ...), custom_call_target="tpu_custom_call" | custom-call | flops 3221225472 | bytes 10485760 | tf_op jit(solution)/shard_map/adjoint/pallas_call | solution.py:445
  62.8 0.0 collective-permute-done.9
  62.9 1.1 dynamic-slice_add_fusion
  64.0 0.1 collective-permute-start.10
  64.1 0.1 collective-permute-start.12
  64.2 2.9 %collective-permute-done.10 = f32[1160,256]{1,0:T(8,128)} collective-permute-done((f32[1160,256]{1,0:T(8,128)S(1)}, f32[1160,256]{1,0:T(8,128)}, u32[]{:S(2)}, u32[]{:S(2)}) %collective-permute-start.10) | collective-permute-done | bytes 1187872 | tf_op jit(solution)/shard_map/ppermute | solution.py:267
  67.1 1.4 slice_add_fusion
  68.6 0.7 slice_add_fusion.4
  69.3 0.6 collective-permute-start.11
  69.9 6.5 %conv.2 = bf16[64,2,32,256]{3,2,1,0:T(8,128)(2,1)} custom-call(bf16[64,2,32,256]{3,2,1,0:T(8,128)(2,1)} %get-tuple-element.71.states_ref.previous_ref.value_ref, bf16[9,256,256]{2,1,0:T(8,128)(2,1)} %weights_ref.8), custom_call_target="tpu_custom_call" | custom-call | flops 3221225472 | bytes 4194304 | tf_op jit(solution)/shard_map/conv/pallas_call | solution.py:424
  76.5 0.1 collective-permute-start.14
  76.5 3.3 %collective-permute-done.11 = f32[584,256]{1,0:T(8,128)S(1)} collective-permute-done((f32[584,256]{1,0:T(8,128)S(1)}, f32[584,256]{1,0:T(8,128)S(1)}, u32[]{:S(2)}, u32[]{:S(2)}) %collective-permute-start.11) | collective-permute-done | bytes 598048 | tf_op jit(solution)/shard_map/ppermute | solution.py:267
  79.9 0.1 slice_add_fusion.1
  80.0 0.1 collective-permute-start.13
  80.1 6.9 %conv.3 = bf16[64,2,32,256]{3,2,1,0:T(8,128)(2,1)} custom-call(bf16[64,2,32,256]{3,2,1,0:T(8,128)(2,1)} %get-tuple-element.76.value_ref, bf16[9,256,256]{2,1,0:T(8,128)(2,1)} %weights_ref.9), custom_call_target="tpu_custom_call" | custom-call | flops 3221225472 | bytes 4194304 | tf_op jit(solution)/shard_map/conv/pallas_call | solution.py:424
  87.0 0.1 collective-permute-start.16
  87.1 2.1 %collective-permute-done.13 = f32[296,256]{1,0:T(8,128)S(1)} collective-permute-done((f32[296,256]{1,0:T(8,128)S(1)}, f32[296,256]{1,0:T(8,128)S(1)}, u32[]{:S(2)}, u32[]{:S(2)}) %collective-permute-start.13) | collective-permute-done | bytes 303136 | tf_op jit(solution)/shard_map/ppermute | solution.py:267
  89.2 0.9 collective-permute-start.15
  90.2 7.6 %collective-permute-done.16 = f32[144,256]{1,0:T(8,128)S(1)} collective-permute-done((f32[144,256]{1,0:T(8,128)S(1)}, f32[144,256]{1,0:T(8,128)S(1)}, u32[]{:S(2)}, u32[]{:S(2)}) %collective-permute-start.16) | collective-permute-done | bytes 147488 | tf_op jit(solution)/shard_map/ppermute | solution.py:267
  97.8 0.1 collective-permute-start.18
  97.9 5.1 %collective-permute-done.15 = f32[152,256]{1,0:T(8,128)S(1)} collective-permute-done((f32[152,256]{1,0:T(8,128)S(1)}, f32[152,256]{1,0:T(8,128)S(1)}, u32[]{:S(2)}, u32[]{:S(2)}) %collective-permute-start.15) | collective-permute-done | bytes 155680 | tf_op jit(solution)/shard_map/ppermute | solution.py:267
  103.0 5.0 %collective-permute-done.18 = f32[288,256]{1,0:T(8,128)S(1)} collective-permute-done((f32[288,256]{1,0:T(8,128)S(1)}, f32[288,256]{1,0:T(8,128)S(1)}, u32[]{:S(2)}, u32[]{:S(2)}) %collective-permute-start.18) | collective-permute-done | bytes 294944 | tf_op jit(solution)/shard_map/ppermute | solution.py:267
  108.0 0.6 collective-permute-start.20
  108.6 0.0 collective-permute-start.17
  108.6 7.1 %collective-permute-done.17 = f32[144,256]{1,0:T(8,128)S(1)} collective-permute-done((f32[144,256]{1,0:T(8,128)S(1)}, f32[144,256]{1,0:T(8,128)S(1)}, u32[]{:S(2)}, u32[]{:S(2)}) %collective-permute-start.17) | collective-permute-done | bytes 147488 | tf_op jit(solution)/shard_map/ppermute | solution.py:267
  115.7 2.3 %collective-permute-done.20 = f32[576,256]{1,0:T(8,128)S(1)} collective-permute-done((f32[576,256]{1,0:T(8,128)S(1)}, f32[576,256]{1,0:T(8,128)S(1)}, u32[]{:S(2)}, u32[]{:S(2)}) %collective-permute-start.20) | collective-permute-done | bytes 589856 | tf_op jit(solution)/shard_map/ppermute | solution.py:267
  118.0 0.1 maximum_select_fusion.2
  118.1 0.1 collective-permute-start.22
  118.1 0.1 collective-permute-start.19
  118.2 9.9 %collective-permute-done.19 = f32[288,256]{1,0:T(8,128)S(1)} collective-permute-done((f32[288,256]{1,0:T(8,128)S(1)}, f32[288,256]{1,0:T(8,128)S(1)}, u32[]{:S(2)}, u32[]{:S(2)}) %collective-permute-start.19) | collective-permute-done | bytes 294944 | tf_op jit(solution)/shard_map/ppermute | solution.py:267
  128.1 0.6 collective-permute-start.21
  128.7 1.7 %maximum_select_fusion = f32[2304,256]{1,0:T(8,128)} fusion(f32[1152,256]{1,0:T(8,128)S(1)} %collective-permute-done.22, f32[1152,256]{1,0:T(8,128)S(1)} %maximum_select_fusion.2, pred[]{:T(512)S(6)} %eq.62), kind=kLoop, calls=%fused_computation | loop fusion | flops 1769472 | bytes 4718593 | tf_op jit(solution)/shard_map/jit(_where)/select_n | solution.py:242
  130.4 7.7 %collective-permute-done.21 = f32[576,256]{1,0:T(8,128)S(1)} collective-permute-done((f32[576,256]{1,0:T(8,128)S(1)}, f32[576,256]{1,0:T(8,128)S(1)}, u32[]{:S(2)}, u32[]{:S(2)}) %collective-permute-start.21) | collective-permute-done | bytes 589856 | tf_op jit(solution)/shard_map/ppermute | solution.py:267
  138.1 0.1 maximum_select_fusion.3
  138.2 0.1 collective-permute-start.23
  138.3 0.6 multiply_multiply_fusion
  138.9 2.2 %collective-permute-done.23 = f32[1152,256]{1,0:T(8,128)S(1)} collective-permute-done((f32[1152,256]{1,0:T(8,128)S(1)}, f32[1152,256]{1,0:T(8,128)S(1)}, u32[]{:S(2)}, u32[]{:S(2)}) %collective-permute-start.23) | collective-permute-done | bytes 1179680 | tf_op jit(solution)/shard_map/ppermute | solution.py:267
  141.1 1.7 %maximum_select_fusion.1 = f32[2304,256]{1,0:T(8,128)} fusion(f32[1152,256]{1,0:T(8,128)S(1)} %collective-permute-done.23, f32[1152,256]{1,0:T(8,128)S(1)} %maximum_select_fusion.3, pred[]{:T(512)S(6)} %eq.62), kind=kLoop, calls=%fused_computation.1 | loop fusion | flops 1769472 | bytes 4718593 | tf_op jit(solution)/shard_map/jit(_where)/select_n | solution.py:242
  (53 shorter events, 0.8 us)
Async XLA Ops:
  0.6 0.7 copy-start
  1.3 0.7 copy-start.2
  8.9 8.0 %copy-start.1 = (f32[256]{0:T(256)S(1)}, f32[256]{0:T(256)}, u32[]{:S(2)}) copy-start(f32[256]{0:T(256)} %param.9) | copy-start | bytes 3076
  8.9 8.0 %copy-start.3 = (f32[64]{0:T(128)S(1)}, f32[64]{0:T(128)}, u32[]{:S(2)}) copy-start(f32[64]{0:T(128)} %step_ref.9) | copy-start | bytes 772
  8.9 5.4 %collective-permute-start = (f32[72,256]{1,0:T(8,128)S(1)}, f32[72,256]{1,0:T(8,128)S(1)}, u32[]{:S(2)}, u32[]{:S(2)}) collective-permute-start(f32[72,256]{1,0:T(8,128)S(1)} %get-tuple-element.47), channel_id=1, source_target_pairs={{0,1},{1,0},{2,3},{3,2},{4,5},{5,4},{6,7},{7,6},{8,9},{9,8},{10,11... | collective-permute-start | bytes 221192 | tf_op jit(solution)/shard_map/ppermute | solution.py:319
  14.3 7.6 %collective-permute-start.1 = (f32[72,256]{1,0:T(8,128)S(1)}, f32[72,256]{1,0:T(8,128)S(1)}, u32[]{:S(2)}, u32[]{:S(2)}) collective-permute-start(f32[72,256]{1,0:T(8,128)S(1)} %pad_maximum_fusion.3), channel_id=1, source_target_pairs={{0,2},{1,3},{2,0},{3,1},{4,6},{5,7},{6,4},{7,5},{8,10},{9,11},{10,... | collective-permute-start | bytes 221192 | tf_op jit(solution)/shard_map/ppermute | solution.py:319
  21.9 4.4 %collective-permute-start.2 = (f32[72,256]{1,0:T(8,128)S(1)}, f32[72,256]{1,0:T(8,128)S(1)}, u32[]{:S(2)}, u32[]{:S(2)}) collective-permute-start(f32[72,256]{1,0:T(8,128)S(1)} %pad_maximum_fusion.4), channel_id=1, source_target_pairs={{0,4},{1,5},{2,6},{3,7},{4,0},{5,1},{6,2},{7,3},{8,12},{9,13},{10,... | collective-permute-start | bytes 221192 | tf_op jit(solution)/shard_map/ppermute | solution.py:319
  23.6 7.3 %collective-permute-start.4 = (f32[72,256]{1,0:T(8,128)S(1)}, f32[72,256]{1,0:T(8,128)S(1)}, u32[]{:S(2)}, u32[]{:S(2)}) collective-permute-start(f32[72,256]{1,0:T(8,128)S(1)} %get-tuple-element.54), channel_id=1, source_target_pairs={{0,1},{1,0},{2,3},{3,2},{4,5},{5,4},{6,7},{7,6},{8,9},{9,8},{10,11... | collective-permute-start | bytes 221192 | tf_op jit(solution)/shard_map/ppermute | solution.py:319
  26.4 6.5 %collective-permute-start.3 = (f32[72,256]{1,0:T(8,128)S(1)}, f32[72,256]{1,0:T(8,128)S(1)}, u32[]{:S(2)}, u32[]{:S(2)}) collective-permute-start(f32[72,256]{1,0:T(8,128)S(1)} %pad_maximum_fusion.5), channel_id=1, source_target_pairs={{0,8},{1,9},{2,10},{3,11},{4,12},{5,13},{6,14},{7,15},{16,24},{17,... | collective-permute-start | bytes 221192 | tf_op jit(solution)/shard_map/ppermute | solution.py:319
  31.0 4.4 %collective-permute-start.5 = (f32[72,256]{1,0:T(8,128)S(1)}, f32[72,256]{1,0:T(8,128)S(1)}, u32[]{:S(2)}, u32[]{:S(2)}) collective-permute-start(f32[72,256]{1,0:T(8,128)S(1)} %pad_maximum_fusion.6), channel_id=1, source_target_pairs={{0,2},{1,3},{2,0},{3,1},{4,6},{5,7},{6,4},{7,5},{8,10},{9,11},{10,... | collective-permute-start | bytes 221192 | tf_op jit(solution)/shard_map/ppermute | solution.py:319
  35.4 9.3 %collective-permute-start.6 = (f32[72,256]{1,0:T(8,128)S(1)}, f32[72,256]{1,0:T(8,128)S(1)}, u32[]{:S(2)}, u32[]{:S(2)}) collective-permute-start(f32[72,256]{1,0:T(8,128)S(1)} %pad_maximum_fusion.7), channel_id=1, source_target_pairs={{0,4},{1,5},{2,6},{3,7},{4,0},{5,1},{6,2},{7,3},{8,12},{9,13},{10,... | collective-permute-start | bytes 221192 | tf_op jit(solution)/shard_map/ppermute | solution.py:319
  44.8 3.0 %collective-permute-start.8 = (f32[1152,256]{1,0:T(8,128)S(1)}, f32[1152,256]{1,0:T(8,128)}, u32[]{:S(2)}, u32[]{:S(2)}) collective-permute-start(f32[1152,256]{1,0:T(8,128)S(1)} %get-tuple-element.63), channel_id=1, source_target_pairs={{0,1},{1,0},{2,3},{3,2},{4,5},{5,4},{6,7},{7,6},{8,9},{9,8},{10,11... | collective-permute-start | bytes 3538952 | tf_op jit(solution)/shard_map/ppermute | solution.py:267
  44.9 9.0 %collective-permute-start.7 = (f32[72,256]{1,0:T(8,128)S(1)}, f32[72,256]{1,0:T(8,128)S(1)}, u32[]{:S(2)}, u32[]{:S(2)}) collective-permute-start(f32[72,256]{1,0:T(8,128)S(1)} %pad_maximum_fusion.8), channel_id=1, source_target_pairs={{8,0},{9,1},{10,2},{11,3},{12,4},{13,5},{14,6},{15,7},{24,16},{25,... | collective-permute-start | bytes 221192 | tf_op jit(solution)/shard_map/ppermute | solution.py:319
  49.3 4.7 %copy-start.4 = (f32[1152,256]{1,0:T(8,128)}, f32[1152,256]{1,0:T(8,128)S(1)}, u32[]{:S(2)}) copy-start(f32[1152,256]{1,0:T(8,128)S(1)} %add.161) | copy-start | bytes 3538948
  49.3 13.5 %collective-permute-start.9 = (f32[576,256]{1,0:T(8,128)S(1)}, f32[576,256]{1,0:T(8,128)}, u32[]{:S(2)}, u32[]{:S(2)}) collective-permute-start(f32[576,256]{1,0:T(8,128)S(1)} %constant_dynamic-slice_fusion.5), channel_id=1, source_target_pairs={{0,2},{1,5},{2,0},{3,7},{4,6},{5,1},{6,4},{7,3},{8,10},{9,13},{10,... | collective-permute-start | bytes 1769480 | tf_op jit(solution)/shard_map/ppermute | solution.py:267
  54.0 8.9 %copy-start.5 = (f32[1152,256]{1,0:T(8,128)S(1)}, f32[1152,256]{1,0:T(8,128)}, u32[]{:S(2)}) copy-start(f32[1152,256]{1,0:T(8,128)} %copy-done.4) | copy-start | bytes 3538948
  64.0 3.1 %collective-permute-start.10 = (f32[1160,256]{1,0:T(8,128)S(1)}, f32[1160,256]{1,0:T(8,128)}, u32[]{:S(2)}, u32[]{:S(2)}) collective-permute-start(f32[1160,256]{1,0:T(8,128)S(1)} %get-tuple-element.70), channel_id=1, source_target_pairs={{0,1},{1,0},{2,3},{3,2},{4,5},{5,4},{6,7},{7,6},{8,9},{9,8},{10,11... | collective-permute-start | bytes 3563528 | tf_op jit(solution)/shard_map/ppermute | solution.py:267
  64.1 12.2 %collective-permute-start.12 = (f32[288,256]{1,0:T(8,128)S(1)}, f32[288,256]{1,0:T(8,128)S(1)}, u32[]{:S(2)}, u32[]{:S(2)}) collective-permute-start(f32[288,256]{1,0:T(8,128)S(1)} %constant_dynamic-slice_fusion.4), channel_id=1, source_target_pairs={{0,4},{1,9},{2,6},{3,11},{4,0},{5,13},{6,2},{7,15},{8,12},{9,1},{1... | collective-permute-start | bytes 884744 | tf_op jit(solution)/shard_map/ppermute | solution.py:267
  69.3 10.6 %collective-permute-start.11 = (f32[584,256]{1,0:T(8,128)S(1)}, f32[584,256]{1,0:T(8,128)S(1)}, u32[]{:S(2)}, u32[]{:S(2)}) collective-permute-start(f32[584,256]{1,0:T(8,128)S(1)} %pad_maximum_fusion), channel_id=1, source_target_pairs={{0,2},{1,5},{2,0},{3,7},{4,6},{5,1},{6,4},{7,3},{8,10},{9,13},{10,... | collective-permute-start | bytes 1794056 | tf_op jit(solution)/shard_map/ppermute | solution.py:267
  76.5 10.5 %collective-permute-start.14 = (f32[144,256]{1,0:T(8,128)S(1)}, f32[144,256]{1,0:T(8,128)S(1)}, u32[]{:S(2)}, u32[]{:S(2)}) collective-permute-start(f32[144,256]{1,0:T(8,128)S(1)} %constant_dynamic-slice_fusion.2), channel_id=1, source_target_pairs={{0,8},{1,3},{2,10},{3,1},{4,12},{5,7},{6,14},{7,5},{8,0},{9,11},{1... | collective-permute-start | bytes 442376 | tf_op jit(solution)/shard_map/ppermute | solution.py:267
  80.0 9.1 %collective-permute-start.13 = (f32[296,256]{1,0:T(8,128)S(1)}, f32[296,256]{1,0:T(8,128)S(1)}, u32[]{:S(2)}, u32[]{:S(2)}) collective-permute-start(f32[296,256]{1,0:T(8,128)S(1)} %pad_maximum_fusion.1), channel_id=1, source_target_pairs={{0,4},{1,9},{2,6},{3,11},{4,0},{5,13},{6,2},{7,15},{8,12},{9,1},{1... | collective-permute-start | bytes 909320 | tf_op jit(solution)/shard_map/ppermute | solution.py:267
  87.0 10.8 %collective-permute-start.16 = (f32[144,256]{1,0:T(8,128)S(1)}, f32[144,256]{1,0:T(8,128)S(1)}, u32[]{:S(2)}, u32[]{:S(2)}) collective-permute-start(f32[144,256]{1,0:T(8,128)S(1)} %dynamic-slice_add_fusion.2), channel_id=1, source_target_pairs={{0,8},{1,3},{2,10},{3,1},{4,12},{5,7},{6,14},{7,5},{8,0},{9,11},{1... | collective-permute-start | bytes 442376 | tf_op jit(solution)/shard_map/ppermute | solution.py:267
  89.2 13.7 %collective-permute-start.15 = (f32[152,256]{1,0:T(8,128)S(1)}, f32[152,256]{1,0:T(8,128)S(1)}, u32[]{:S(2)}, u32[]{:S(2)}) collective-permute-start(f32[152,256]{1,0:T(8,128)S(1)} %pad_maximum_fusion.2), channel_id=1, source_target_pairs={{0,8},{1,3},{2,10},{3,1},{4,12},{5,7},{6,14},{7,5},{8,0},{9,11},{1... | collective-permute-start | bytes 466952 | tf_op jit(solution)/shard_map/ppermute | solution.py:267
  97.8 10.2 %collective-permute-start.18 = (f32[288,256]{1,0:T(8,128)S(1)}, f32[288,256]{1,0:T(8,128)S(1)}, u32[]{:S(2)}, u32[]{:S(2)}) collective-permute-start(f32[288,256]{1,0:T(8,128)S(1)} %maximum_select_fusion.6), channel_id=1, source_target_pairs={{0,4},{1,9},{2,6},{3,11},{4,0},{5,13},{6,2},{7,15},{8,12},{9,1},{1... | collective-permute-start | bytes 884744 | tf_op jit(solution)/shard_map/ppermute | solution.py:267
  108.0 9.9 %collective-permute-start.20 = (f32[576,256]{1,0:T(8,128)S(1)}, f32[576,256]{1,0:T(8,128)S(1)}, u32[]{:S(2)}, u32[]{:S(2)}) collective-permute-start(f32[576,256]{1,0:T(8,128)S(1)} %maximum_select_fusion.4), channel_id=1, source_target_pairs={{0,2},{1,5},{2,0},{3,7},{4,6},{5,1},{6,4},{7,3},{8,10},{9,13},{10,... | collective-permute-start | bytes 1769480 | tf_op jit(solution)/shard_map/ppermute | solution.py:267
  108.6 7.1 %collective-permute-start.17 = (f32[144,256]{1,0:T(8,128)S(1)}, f32[144,256]{1,0:T(8,128)S(1)}, u32[]{:S(2)}, u32[]{:S(2)}) collective-permute-start(f32[144,256]{1,0:T(8,128)S(1)} %slice_add_fusion.3), channel_id=1, source_target_pairs={{0,8},{1,3},{2,10},{3,1},{4,12},{5,7},{6,14},{7,5},{8,0},{9,11},{1... | collective-permute-start | bytes 442376 | tf_op jit(solution)/shard_map/ppermute | solution.py:267
  118.1 10.7 %collective-permute-start.22 = (f32[1152,256]{1,0:T(8,128)S(1)}, f32[1152,256]{1,0:T(8,128)S(1)}, u32[]{:S(2)}, u32[]{:S(2)}) collective-permute-start(f32[1152,256]{1,0:T(8,128)S(1)} %maximum_select_fusion.2), channel_id=1, source_target_pairs={{0,1},{1,0},{2,3},{3,2},{4,5},{5,4},{6,7},{7,6},{8,9},{9,8},{10,11... | collective-permute-start | bytes 3538952 | tf_op jit(solution)/shard_map/ppermute | solution.py:267
  118.1 9.9 %collective-permute-start.19 = (f32[288,256]{1,0:T(8,128)S(1)}, f32[288,256]{1,0:T(8,128)S(1)}, u32[]{:S(2)}, u32[]{:S(2)}) collective-permute-start(f32[288,256]{1,0:T(8,128)S(1)} %maximum_select_fusion.7), channel_id=1, source_target_pairs={{0,4},{1,9},{2,6},{3,11},{4,0},{5,13},{6,2},{7,15},{8,12},{9,1},{1... | collective-permute-start | bytes 884744 | tf_op jit(solution)/shard_map/ppermute | solution.py:267
  128.1 9.9 %collective-permute-start.21 = (f32[576,256]{1,0:T(8,128)S(1)}, f32[576,256]{1,0:T(8,128)S(1)}, u32[]{:S(2)}, u32[]{:S(2)}) collective-permute-start(f32[576,256]{1,0:T(8,128)S(1)} %maximum_select_fusion.5), channel_id=1, source_target_pairs={{0,2},{1,5},{2,0},{3,7},{4,6},{5,1},{6,4},{7,3},{8,10},{9,13},{10,... | collective-permute-start | bytes 1769480 | tf_op jit(solution)/shard_map/ppermute | solution.py:267
  138.2 2.9 %collective-permute-start.23 = (f32[1152,256]{1,0:T(8,128)S(1)}, f32[1152,256]{1,0:T(8,128)S(1)}, u32[]{:S(2)}, u32[]{:S(2)}) collective-permute-start(f32[1152,256]{1,0:T(8,128)S(1)} %maximum_select_fusion.3), channel_id=1, source_target_pairs={{0,1},{1,0},{2,3},{3,2},{4,5},{5,4},{6,7},{7,6},{8,9},{9,8},{10,11... | collective-permute-start | bytes 3538952 | tf_op jit(solution)/shard_map/ppermute | solution.py:267

commit v3 on v2

--- a/solution.py
+++ b/solution.py
@@ -10,7 +10,6 @@
 
 F32 = jnp.float32
 BF16 = jnp.bfloat16
-EXTRA = 8
 VMEM_LIMIT = 20 * 1024 * 1024
 
 
@@ -95,14 +94,18 @@
     sums[2] += contract(source[:, 1], taps[:, 0])
 
 
-def split_grad(scale, sums, whole, core, keep_ref, send_ref):
+def split_grad(scale, sums, whole, core, keep_ref, send_ref, rate_sum=None):
     channels = sums.shape[1]
+    rows = 9 * channels
+    if rate_sum is not None:
+        whole[rows:] = jnp.zeros((whole.shape[0] - rows, channels), F32)
+        whole[rows : rows + 8] = rate_sum
     for tap in range(9):
         piece = sums[tap // 3, :, (tap % 3) * channels : (tap % 3 + 1) * channels]
         whole[tap * channels : (tap + 1) * channels] = piece * scale
     half = whole.shape[0] // 2
-    keep_ref[:half] = whole[pl.ds(core * half, half)]
-    send_ref[:half] = whole[pl.ds((1 - core) * half, half)]
+    keep_ref[...] = whole[pl.ds(core * half, half)]
+    send_ref[...] = whole[pl.ds((1 - core) * half, half)]
 
 
 def state_kernel(
@@ -184,13 +187,11 @@
 
     @pl.when(index == count - 1)
     def _():
-        split_grad(scale, sums, whole, core_ref[0], keep_ref, send_ref)
-        half = whole.shape[0] // 2
-        keep_ref[half:] = summed
-        send_ref[half:] = summed
-
-
-def conv_kernel(reverse, value_ref, weights_ref, out_ref, flipped):
+        split_grad(scale, sums, whole, core_ref[0], keep_ref, send_ref, summed)
+
+
+def conv_kernel(reverse, value_ref, weights_ref, *refs):
+    out_ref, flipped = refs[-2:]
     if reverse:
 
         @pl.when(pl.program_id(0) == 0)
@@ -203,7 +204,7 @@
         out_ref[:, row] = out.astype(BF16).reshape(block, breadth, channels)
 
 
-def call(kernel, grid, in_specs, out_specs, out_shape, scratch, flops, moved, name):
+def call(kernel, grid, in_specs, out_specs, out_shape, scratch, flops, moved, name, aliases=None):
     return pl.pallas_call(
         kernel,
         grid=grid,
@@ -211,6 +212,7 @@
         out_specs=out_specs,
         out_shape=out_shape,
         scratch_shapes=scratch,
+        input_output_aliases=aliases or {},
         compiler_params=pltpu.CompilerParams(vmem_limit_bytes=VMEM_LIMIT, dimension_semantics=("arbitrary",) * len(grid)),
         cost_estimate=pl.CostEstimate(flops=flops, bytes_accessed=moved, transcendentals=0),
         name=name,
@@ -255,8 +257,8 @@
 
 
 class Sum:
-    def __init__(self, keep, send, main, bits, orders, count):
-        self.keep, self.send, self.main, self.count = keep, send, main, count
+    def __init__(self, keep, send, bits, orders, count):
+        self.keep, self.send, self.count = keep, send, count
         self.orders = orders
         self.bits = [jnp.where(bits[0] == 0, bits[even], bits[odd]) for even, odd in zip(*orders)]
         self.stage = 0
@@ -273,16 +275,13 @@
         self.recv = after(self.recv, *others)
 
     def fold(self):
-        total_main = self.keep[: self.main] + self.recv[: self.main]
-        total_extra = self.keep[self.main :] + self.recv[self.main :]
+        total = self.keep + self.recv
         self.stage += 1
         if self.stage == len(self.bits):
-            self.send, self.extra = total_main, total_extra
+            self.send = total
             return
         bit = self.bits[self.stage]
-        self.keep = jnp.concatenate([part_of(bit, total_main), total_extra])
-        self.send = jnp.concatenate([part_of(1 - bit, total_main), total_extra])
-        self.main = self.main // 2
+        self.keep, self.send = part_of(bit, total), part_of(1 - bit, total)
 
     def step(self):
         if self.left == 0:
@@ -328,8 +327,29 @@
         self.level += 1
         self.message = jnp.concatenate([local.reshape(self.rows, -1), (decay * other_decay)[0]], axis=0)
 
+    def start_rest(self):
+        runs = self.count // 4
+        hops = [-4 * hop if self.reverse else 4 * hop for hop in range(1, runs)]
+        self.rest = [
+            lax.ppermute(
+                self.message, "tm", [(source, source + hop) for source in range(self.count) if 0 <= source + hop < self.count]
+            )
+            for hop in hops
+        ]
+
+    def combine_rest(self, *others):
+        held = jnp.zeros_like(self.reached)
+        for message in self.rest[::-1]:
+            local, decay = self.split(after(message, *others))
+            held = local + decay * held
+        self.reached = self.reached + self.passed * held
+
     def result(self):
         return self.reached.reshape(self.rows, -1)
+
+
+def turns(levels):
+    return "icoic" + "oi" * (2 * levels - 3) + "i"
 
 
 def body(latents, input_map, output_map, decay_rate, frame_step, cotangent):
@@ -356,7 +376,7 @@
 
     def drive(value, kernel_map, reverse, base, size, start=None):
         specs = [smem(), fixed(rate.shape), framed(shape, block, size, reverse, base), fixed(weights)]
-        operands = [frame_step, rate, far(value), far(kernel_map)]
+        operands = [frame_step, rate, far(value), kernel_map if reverse else far(kernel_map)]
         if start is not None:
             specs.append(fixed((map_rows + 8, channels)))
             operands.append(start)
@@ -387,19 +407,21 @@
     for _ in range(levels - 3):
         forward.combine()
         forward.start()
-        backward.combine(forward.message)
-        backward.start()
+        if backward.level == 0:
+            backward.combine(forward.message)
+            backward.start()
     forward.combine()
     incoming = forward.result()
     backward.combine(incoming)
-    backward.start()
+    backward.start_rest()
 
     grad_rows = 9 * channels
     half = grad_rows // 2
     sums_scratch = pltpu.VMEM((3, channels, 3 * channels), F32)
     whole_scratch = pltpu.VMEM((grad_rows, channels), F32)
     half_type = jax.ShapeDtypeStruct((half, channels), F32)
-    half_extra = jax.ShapeDtypeStruct((half + EXTRA, channels), F32)
+    padded_rows = grad_rows + 8 * count
+    padded_type = jax.ShapeDtypeStruct((padded_rows // 2, channels), F32)
 
     states_low, out_keep, out_send = call(
         functools.partial(state_kernel, factor),
@@ -420,27 +442,33 @@
         "states",
     )(frame_step, bits[0], rate, after(incoming, backward.message), far(driven), far(cotangent))
 
-    def conv(value, kernel_map, reverse):
+    def conv(value, kernel_map, reverse, base, size, previous=None):
+        specs = [framed(shape, block, size, False, base), fixed(weights)]
+        operands = [far(value), kernel_map]
+        aliases = {}
+        if previous is not None:
+            specs.append(pl.BlockSpec(memory_space=pl.ANY))
+            operands.append(previous)
+            aliases = {2: 0}
         return call(
             functools.partial(conv_kernel, reverse),
-            grid,
-            [framed(shape, block, steps, False), fixed(weights)],
-            framed(shape, block, steps, False),
+            (size,),
+            specs,
+            framed(shape, block, size, False, base),
             low_type,
             [flip_scratch],
-            flops,
-            pixels * channels * 4,
+            flops * size // steps,
+            pixels * channels * 4 * size // steps,
             "conv",
-        )(far(value), far(kernel_map))
+            aliases,
+        )(*operands)
 
     orders = (list(range(levels)), [0] + list(range(2, levels)) + [1])
-    backward.combine(out_send)
-    backward.start()
-    out_sum = Sum(out_keep, after(out_send, backward.message), half, bits, orders, count)
+    backward.combine_rest(out_send)
+    arriving = backward.result()
+    out_sum = Sum(out_keep, out_send, bits, orders, count)
     out_sum.start()
     out_sum.step()
-    backward.combine(out_sum.send)
-    arriving = backward.result()
 
     adjoint_low, in_keep, in_send = call(
         functools.partial(adjoint_kernel, factor, steps - later),
@@ -457,9 +485,9 @@
             framed(shape, block, steps, True),
             pl.BlockSpec((1,) + shape[1:], lambda g: (jnp.maximum((steps - 1 - g) * block - 1, 0), 0, 0, 0)),
         ],
-        [framed(shape, block, steps, True), fixed(half_extra.shape), fixed(half_extra.shape)],
-        [low_type, half_extra, half_extra],
-        [map_scratch, decay_scratch, sums_scratch, whole_scratch],
+        [framed(shape, block, steps, True), fixed(padded_type.shape), fixed(padded_type.shape)],
+        [low_type, padded_type, padded_type],
+        [map_scratch, decay_scratch, sums_scratch, pltpu.VMEM((padded_rows, channels), F32)],
         flops,
         pixels * channels * 10,
         "adjoint",
@@ -467,7 +495,7 @@
         frame_step,
         bits[0],
         rate,
-        arriving,
+        after(arriving, out_sum.send),
         incoming,
         far(pulled_late),
         far(pulled_early),
@@ -478,22 +506,24 @@
 
     out_sum.wait(in_send)
     out_sum.step()
-    in_sum = Sum(in_keep, after(in_send, out_sum.send), half, bits, orders, count)
+    in_sum = Sum(in_keep, after(in_send, out_sum.send), bits, orders, count)
     in_sum.start()
-    in_sum.step()
-    fillers = [(adjoint_low, input_map, True), (states_low, output_map, False)]
-    results = []
-    for stage in range(1, 2 * levels):
-        if fillers:
-            value, kernel_map, reverse = fillers.pop()
-            results.append(conv(after(value, in_sum.send), kernel_map, reverse))
-            out_sum.wait(results[-1])
-        out_sum.wait(in_sum.send)
-        out_sum.step()
-        in_sum.wait(out_sum.send)
-        in_sum.step()
-    layer_out, grad_latents = results
-    grad_output_map, grad_input_map, rate_rows = out_sum.send, in_sum.send, in_sum.extra
+    covers = [(adjoint_low, input_map, True), (states_low, output_map, False)]
+    convs = []
+    latest = out_sum.send
+    for turn in turns(levels):
+        if turn == "c":
+            value, kernel_map, reverse = covers.pop()
+            convs.append(conv(after(value, latest), kernel_map, reverse, 0, steps))
+            latest = convs[-1]
+        else:
+            one = out_sum if turn == "o" else in_sum
+            one.wait(latest)
+            one.step()
+            latest = one.send
+    layer_out, grad_latents = convs
+    grad_output_map, grad_input_map = out_sum.send, in_sum.send[:grad_rows]
+    rate_rows = in_sum.send[grad_rows : grad_rows + 8]
     grad_log_rate = -factor * decay_rate * jnp.sum(rate_rows, axis=0)
     return (
         layer_out,

time: 144 us -> 140 us (0.972)
  waiting for transfers between devices: 67.2 us -> 63.3 us
  other arithmetic: 9.55 us -> 6.32 us
  starting transfers between devices: 16.8 us -> 19.3 us
  local copies, waits for them, and re-layouts: 1.54 us -> 3.74 us
  Pallas kernels: 46.7 us -> 45.1 us
    ppermute x0 -> x3, waiting for transfers between devices: none -> 6.93 us  [start_rest(): lax.ppermute(self.message, 'tm', [(source, source + hop) for source in ra...]
    ppermute x16, waiting for transfers between devices: 56.6 us -> 49.7 us  [swap(): lax.ppermute(value, 'tm', [(source, source ^ 1 << levels[source & 1]) for...]
    ppermute x0 -> x3, starting transfers between devices: none -> 4.05 us  [start_rest(): lax.ppermute(self.message, 'tm', [(source, source + hop) for source in ra...]
    ppermute x8 -> x6, waiting for transfers between devices: 10.6 us -> 6.6 us  [start(): self.other = lax.ppermute(self.message, 'tm', pairs)]
    ppermute x8 -> x6, starting transfers between devices: 12.9 us -> 9.78 us  [start(): self.other = lax.ppermute(self.message, 'tm', pairs)]
    add x11 -> x9, other arithmetic: 4.89 us -> 3.2 us  [the longest x8 3.15 us: fold(): total = self.keep + self.recv]
    ppermute x16, starting transfers between devices: 3.92 us -> 5.51 us  [swap(): lax.ppermute(value, 'tm', [(source, source ^ 1 << levels[source & 1]) for...]
    slice x0 -> x3, local copies, waits for them, and re-layouts: none -> 1.56 us  [the longest x1 1.56 us: body(): grad_output_map, grad_input_map = (out_sum.send, in_sum.send[:grad_rows])]
  transfers between devices with their start and end apart: 24 -> 25, of which waited for: 16 -> 16; matrix products, arithmetic and copies ran while one was open for 5% -> 4% of each run, Pallas kernels for 28% -> 22%
where the time goes in v3:
time: 140 us; the launch traced here: 139 us
  waiting for transfers between devices  63.3 us (45%)
  Pallas kernels  45.1 us (32%)
  starting transfers between devices  19.3 us (14%)
  other arithmetic  6.32 us (5%)
  local copies, waits for them, and re-layouts  3.74 us (3%)
    ppermute x16, waiting for transfers between devices, swap(): lax.ppermute(value, 'tm', [(source, source ^ 1 << levels[source & 1]) for...  49.7 us
    pallas_call x3, Pallas kernels, drive(): call(functools.partial(drive_kernel, reverse, base, start is None), (size...  16.1 us
    pallas_call x2, Pallas kernels, conv(): call(functools.partial(conv_kernel, reverse), (size,), specs, framed(shap...  12.5 us
    ppermute x6, starting transfers between devices, start(): self.other = lax.ppermute(self.message, 'tm', pairs)  9.78 us
    pallas_call x1, Pallas kernels, body(): call(functools.partial(adjoint_kernel, factor, steps - later), grid, [sme...  8.8 us
    pallas_call x1, Pallas kernels, body(): call(functools.partial(state_kernel, factor), grid, [smem(), smem(), fixe...  7.72 us
    ppermute x3, waiting for transfers between devices, start_rest(): lax.ppermute(self.message, 'tm', [(source, source + hop) for source in ra...  6.93 us
    ppermute x6, waiting for transfers between devices, start(): self.other = lax.ppermute(self.message, 'tm', pairs)  6.6 us
  transfers between devices with their start and end apart: 25, of which 16 were waited for; matrix products, arithmetic and copies ran while one was open for 4% of the time, Pallas kernels for 22%

profile of v3, /device:TPU:0, one launch (start us, length us, event | category | flops | bytes accessed | tf_op | source)
XLA Modules:
  0.0 138.8 jit_solution(1891236715253149598)
XLA Ops:
  0.6 0.0 copy-start
  0.6 0.7 copy-done
  1.3 0.7 copy-done.5
  2.0 7.0 %drive.1 = (f32[64,2,32,256]{3,2,1,0:T(8,128)}, f32[72,256]{1,0:T(8,128)S(1)}) custom-call(f32[64]{0:T(128)S(1)} %copy-done.5, f32[1,256]{1,0:T(1,128)S(1)} %bitcast.116, bf16[64,2,32,256]{3,2,1,0:T(8,128)(2,1)} %latents_ref.1, bf16[9,256,256]{2,1,0:T(8,128)(2,1)} %weights_ref.9), custom_call_target="tpu_custom_call" | custom-call | flops 3221225472 | bytes 6291456 | tf_op jit(solution)/shard_map/drive/pallas_call | solution.py:383
  9.0 0.5 collective-permute-start
  9.5 4.5 %pull.2 = (f32[32,2,32,256]{3,2,1,0:T(8,128)}, f32[72,256]{1,0:T(8,128)S(1)}) custom-call(f32[64]{0:T(128)S(1)} %copy-done.5, f32[1,256]{1,0:T(1,128)S(1)} %bitcast.117, bf16[64,2,32,256]{3,2,1,0:T(8,128)(2,1)} %cotangent_ref.1, bf16[9,256,256]{2,1,0:T(8,128)(2,1)S(1)} %copy-done.2), custom_call_target="tpu_custom_call" | custom-call | flops 1610612736 | bytes 3145728 | tf_op jit(solution)/shard_map/pull/pallas_call | solution.py:383
  14.0 2.6 %collective-permute-start.1 = (f32[72,256]{1,0:T(8,128)S(1)}, f32[72,256]{1,0:T(8,128)S(1)}, u32[]{:S(2)}, u32[]{:S(2)}) collective-permute-start(f32[72,256]{1,0:T(8,128)S(1)} %pad_maximum_fusion), channel_id=1, source_target_pairs={{0,2},{1,3},{2,0},{3,1},{4,6},{5,7},{6,4},{7,5},{8,10},{9,11},{10,... | collective-permute-start | bytes 221192 | tf_op jit(solution)/shard_map/ppermute | solution.py:318
  16.6 4.5 %pull.3 = (f32[32,2,32,256]{3,2,1,0:T(8,128)}, f32[72,256]{1,0:T(8,128)S(1)}) custom-call(f32[64]{0:T(128)S(1)} %copy-done.6, f32[1,256]{1,0:T(1,128)S(1)} %bitcast.118, bf16[64,2,32,256]{3,2,1,0:T(8,128)(2,1)} %cotangent_ref.1, bf16[9,256,256]{2,1,0:T(8,128)(2,1)S(1)} %copy-done.2, f32[72,256]{1,0:T(8,128)S(1)} %get-tuple-element.50.refs_0_), custom_call_target="tpu_custom_call" | custom-call | flops 1610612736 | bytes 3145728 | tf_op jit(solution)/shard_map/pull/pallas_call | solution.py:383
  21.2 0.0 collective-permute-done.1
  21.2 1.6 %collective-permute-start.2 = (f32[72,256]{1,0:T(8,128)S(1)}, f32[72,256]{1,0:T(8,128)S(1)}, u32[]{:S(2)}, u32[]{:S(2)}) collective-permute-start(f32[72,256]{1,0:T(8,128)S(1)} %pad_maximum_fusion.1), channel_id=1, source_target_pairs={{0,4},{1,5},{2,6},{3,7},{4,0},{5,1},{6,2},{7,3},{8,12},{9,13},{10,... | collective-permute-start | bytes 221192 | tf_op jit(solution)/shard_map/ppermute | solution.py:318
  22.9 2.8 %collective-permute-done.2 = f32[72,256]{1,0:T(8,128)S(1)} collective-permute-done((f32[72,256]{1,0:T(8,128)S(1)}, f32[72,256]{1,0:T(8,128)S(1)}, u32[]{:S(2)}, u32[]{:S(2)}) %collective-permute-start.2) | collective-permute-done | bytes 73760 | tf_op jit(solution)/shard_map/ppermute | solution.py:318
  25.7 4.5 %collective-permute-start.3 = (f32[72,256]{1,0:T(8,128)S(1)}, f32[72,256]{1,0:T(8,128)S(1)}, u32[]{:S(2)}, u32[]{:S(2)}) collective-permute-start(f32[72,256]{1,0:T(8,128)S(1)} %pad_maximum_fusion.2), channel_id=1, source_target_pairs={{0,8},{1,9},{2,10},{3,11},{4,12},{5,13},{6,14},{7,15},{16,24},{17,... | collective-permute-start | bytes 221192 | tf_op jit(solution)/shard_map/ppermute | solution.py:318
  30.3 0.6 collective-permute-start.5
  30.8 1.3 collective-permute-done.3
  32.2 2.5 %collective-permute-done.5 = f32[72,256]{1,0:T(8,128)S(1)} collective-permute-done((f32[72,256]{1,0:T(8,128)S(1)}, f32[72,256]{1,0:T(8,128)S(1)}, u32[]{:S(2)}, u32[]{:S(2)}) %collective-permute-start.5) | collective-permute-done | bytes 73760 | tf_op jit(solution)/shard_map/ppermute | solution.py:318
  34.7 7.7 %states.1 = (bf16[64,2,32,256]{3,2,1,0:T(8,128)(2,1)}, f32[1152,256]{1,0:T(8,128)S(1)}, f32[1152,256]{1,0:T(8,128)S(1)}) custom-call(f32[64]{0:T(128)S(1)} %copy-done.6, s32[1]{0:T(128)} %bitcast.core_ref, f32[1,256]{1,0:T(1,128)S(1)} %bitcast.119, f32[64,256]{1,0:T(8,128)S(1)} %add_select_fusion.1.incoming_ref, ...), custom_call_target="tpu_custom_call" | custom-call | flops 3221225472 | bytes 8388608 | tf_op jit(solution)/shard_map/states/pallas_call | solution.py:426
  42.4 0.0 collective-permute-start.9
  42.5 1.3 collective-permute-start.8
  43.8 1.3 collective-permute-start.6
  45.1 1.5 %collective-permute-start.7 = (f32[72,256]{1,0:T(8,128)S(1)}, f32[72,256]{1,0:T(8,128)S(1)}, u32[]{:S(2)}, u32[]{:S(2)}) collective-permute-start(f32[72,256]{1,0:T(8,128)S(1)} %pad_maximum_fusion.4), channel_id=1, source_target_pairs={{8,0},{9,1},{10,2},{11,3},{12,4},{13,5},{14,6},{15,7},{24,16},{25,... | collective-permute-start | bytes 221192 | tf_op jit(solution)/shard_map/ppermute | solution.py:334
  46.5 4.6 %collective-permute-done.8 = f32[72,256]{1,0:T(8,128)S(1)} collective-permute-done((f32[72,256]{1,0:T(8,128)S(1)}, f32[72,256]{1,0:T(8,128)S(1)}, u32[]{:S(2)}, u32[]{:S(2)}) %collective-permute-start.8) | collective-permute-done | bytes 73760 | tf_op jit(solution)/shard_map/ppermute | solution.py:334
  51.2 0.0 collective-permute-done.9
  51.2 1.4 %add.158 = f32[1152,256]{1,0:T(8,128)S(1)} add(f32[1152,256]{1,0:T(8,128)S(1)} %get-tuple-element.63, f32[1152,256]{1,0:T(8,128)} %collective-permute-done.9) | non-fusion elementwise | flops 294912 | bytes 3538944 | tf_op jit(solution)/shard_map/add | solution.py:278
  52.7 0.6 collective-permute-start.10
  53.2 2.3 %collective-permute-done.7 = f32[72,256]{1,0:T(8,128)S(1)} collective-permute-done((f32[72,256]{1,0:T(8,128)S(1)}, f32[72,256]{1,0:T(8,128)S(1)}, u32[]{:S(2)}, u32[]{:S(2)}) %collective-permute-start.7) | collective-permute-done | bytes 73760 | tf_op jit(solution)/shard_map/ppermute | solution.py:334
  55.6 8.8 %adjoint.1 = (bf16[64,2,32,256]{3,2,1,0:T(8,128)(2,1)}, f32[1216,256]{1,0:T(8,128)S(1)}, f32[1216,256]{1,0:T(8,128)S(1)}) custom-call(f32[64]{0:T(128)S(1)} %copy-done.6, s32[1]{0:T(128)} %bitcast.core_ref, f32[1,256]{1,0:T(1,128)S(1)} %bitcast.120, f32[64,256]{1,0:T(8,128)S(1)} %fusion.arriving_ref, f32[64,256]{1,0:T(8,128)S(1)} %add_select_fusion.1.incoming_ref, ...), custom_call_target="tpu_custom_call" | custom-call | flops 3221225472 | bytes 10485760 | tf_op jit(solution)/shard_map/adjoint/pallas_call | solution.py:473
  64.4 0.1 dynamic-slice_add_fusion.1
  64.5 0.1 collective-permute-start.11
  64.6 0.1 collective-permute-start.13
  64.7 3.0 %collective-permute-done.11 = f32[1216,256]{1,0:T(8,128)} collective-permute-done((f32[1216,256]{1,0:T(8,128)S(1)}, f32[1216,256]{1,0:T(8,128)}, u32[]{:S(2)}, u32[]{:S(2)}) %collective-permute-start.11) | collective-permute-done | bytes 1245216 | tf_op jit(solution)/shard_map/ppermute | solution.py:269
  67.6 1.5 %add.163 = f32[1216,256]{1,0:T(8,128)S(1)} add(f32[1216,256]{1,0:T(8,128)S(1)} %get-tuple-element.67, f32[1216,256]{1,0:T(8,128)} %collective-permute-done.11) | non-fusion elementwise | flops 311296 | bytes 3735552 | tf_op jit(solution)/shard_map/add | solution.py:278
  69.1 0.0 copy-start.3
  69.1 0.1 constant_dynamic-slice_fusion.3
  69.2 0.6 collective-permute-start.12
  69.7 0.6 copy-done.3
  70.4 6.1 %conv.2 = bf16[64,2,32,256]{3,2,1,0:T(8,128)(2,1)} custom-call(bf16[64,2,32,256]{3,2,1,0:T(8,128)(2,1)} %get-tuple-element.72.states_ref.previous_ref.value_ref, bf16[9,256,256]{2,1,0:T(8,128)(2,1)S(1)} %copy-done.3), custom_call_target="tpu_custom_call" | custom-call | flops 3221225472 | bytes 4194304 | tf_op jit(solution)/shard_map/conv/pallas_call | solution.py:453
  76.5 0.0 copy-start.4
  76.5 0.1 collective-permute-start.15
  76.6 2.9 %collective-permute-done.12 = f32[608,256]{1,0:T(8,128)S(1)} collective-permute-done((f32[608,256]{1,0:T(8,128)S(1)}, f32[608,256]{1,0:T(8,128)S(1)}, u32[]{:S(2)}, u32[]{:S(2)}) %collective-permute-start.12) | collective-permute-done | bytes 622624 | tf_op jit(solution)/shard_map/ppermute | solution.py:269
  79.5 0.1 dynamic-slice_add_fusion
  79.7 0.1 collective-permute-start.14
  79.7 6.5 %conv.3 = bf16[64,2,32,256]{3,2,1,0:T(8,128)(2,1)} custom-call(bf16[64,2,32,256]{3,2,1,0:T(8,128)(2,1)} %get-tuple-element.76.value_ref, bf16[9,256,256]{2,1,0:T(8,128)(2,1)S(1)} %copy-done.4), custom_call_target="tpu_custom_call" | custom-call | flops 3221225472 | bytes 4194304 | tf_op jit(solution)/shard_map/conv/pallas_call | solution.py:453
  86.2 0.1 collective-permute-start.17
  86.3 1.5 %collective-permute-done.14 = f32[304,256]{1,0:T(8,128)S(1)} collective-permute-done((f32[304,256]{1,0:T(8,128)S(1)}, f32[304,256]{1,0:T(8,128)S(1)}, u32[]{:S(2)}, u32[]{:S(2)}) %collective-permute-start.14) | collective-permute-done | bytes 311328 | tf_op jit(solution)/shard_map/ppermute | solution.py:269
  87.9 1.5 %collective-permute-start.16 = (f32[152,256]{1,0:T(8,128)S(1)}, f32[152,256]{1,0:T(8,128)S(1)}, u32[]{:S(2)}, u32[]{:S(2)}) collective-permute-start(f32[152,256]{1,0:T(8,128)S(1)} %constant_dynamic-slice_fusion), channel_id=1, source_target_pairs={{0,8},{1,3},{2,10},{3,1},{4,12},{5,7},{6,14},{7,5},{8,0},{9,11},{1... | collective-permute-start | bytes 466952 | tf_op jit(solution)/shard_map/ppermute | solution.py:269
  89.4 7.1 %collective-permute-done.17 = f32[144,256]{1,0:T(8,128)S(1)} collective-permute-done((f32[144,256]{1,0:T(8,128)S(1)}, f32[144,256]{1,0:T(8,128)S(1)}, u32[]{:S(2)}, u32[]{:S(2)}) %collective-permute-start.17) | collective-permute-done | bytes 147488 | tf_op jit(solution)/shard_map/ppermute | solution.py:269
  96.5 0.1 collective-permute-start.19
  96.6 2.7 %collective-permute-done.16 = f32[152,256]{1,0:T(8,128)S(1)} collective-permute-done((f32[152,256]{1,0:T(8,128)S(1)}, f32[152,256]{1,0:T(8,128)S(1)}, u32[]{:S(2)}, u32[]{:S(2)}) %collective-permute-start.16) | collective-permute-done | bytes 155680 | tf_op jit(solution)/shard_map/ppermute | solution.py:269
  99.4 6.8 %collective-permute-done.19 = f32[288,256]{1,0:T(8,128)S(1)} collective-permute-done((f32[288,256]{1,0:T(8,128)S(1)}, f32[288,256]{1,0:T(8,128)S(1)}, u32[]{:S(2)}, u32[]{:S(2)}) %collective-permute-start.19) | collective-permute-done | bytes 294944 | tf_op jit(solution)/shard_map/ppermute | solution.py:269
  106.2 0.5 collective-permute-start.21
  106.7 7.5 %collective-permute-done.18 = f32[152,256]{1,0:T(8,128)S(1)} collective-permute-done((f32[152,256]{1,0:T(8,128)S(1)}, f32[152,256]{1,0:T(8,128)S(1)}, u32[]{:S(2)}, u32[]{:S(2)}) %collective-permute-start.18) | collective-permute-done | bytes 155680 | tf_op jit(solution)/shard_map/ppermute | solution.py:269
  114.3 0.1 collective-permute-start.20
  114.4 1.8 %collective-permute-done.21 = f32[576,256]{1,0:T(8,128)S(1)} collective-permute-done((f32[576,256]{1,0:T(8,128)S(1)}, f32[576,256]{1,0:T(8,128)S(1)}, u32[]{:S(2)}, u32[]{:S(2)}) %collective-permute-start.21) | collective-permute-done | bytes 589856 | tf_op jit(solution)/shard_map/ppermute | solution.py:269
  116.2 0.1 maximum_select_fusion.3
  116.3 6.6 %collective-permute-done.20 = f32[304,256]{1,0:T(8,128)S(1)} collective-permute-done((f32[304,256]{1,0:T(8,128)S(1)}, f32[304,256]{1,0:T(8,128)S(1)}, u32[]{:S(2)}, u32[]{:S(2)}) %collective-permute-start.20) | collective-permute-done | bytes 311328 | tf_op jit(solution)/shard_map/ppermute | solution.py:269
  123.0 1.8 %collective-permute-start.22 = (f32[608,256]{1,0:T(8,128)S(1)}, f32[608,256]{1,0:T(8,128)S(1)}, u32[]{:S(2)}, u32[]{:S(2)}) collective-permute-start(f32[608,256]{1,0:T(8,128)S(1)} %maximum_select_fusion.4), channel_id=1, source_target_pairs={{0,2},{1,5},{2,0},{3,7},{4,6},{5,1},{6,4},{7,3},{8,10},{9,13},{10,... | collective-permute-start | bytes 1867784 | tf_op jit(solution)/shard_map/ppermute | solution.py:269
  124.7 8.5 %collective-permute-done.22 = f32[608,256]{1,0:T(8,128)S(1)} collective-permute-done((f32[608,256]{1,0:T(8,128)S(1)}, f32[608,256]{1,0:T(8,128)S(1)}, u32[]{:S(2)}, u32[]{:S(2)}) %collective-permute-start.22) | collective-permute-done | bytes 622624 | tf_op jit(solution)/shard_map/ppermute | solution.py:269
  133.3 0.1 maximum_select_fusion.2
  133.4 0.1 collective-permute-start.23
  133.4 1.7 %maximum_select_fusion.1 = f32[2304,256]{1,0:T(8,128)} fusion(f32[1152,256]{1,0:T(8,128)S(1)} %collective-permute-done.24, f32[1152,256]{1,0:T(8,128)S(1)} %maximum_select_fusion.3, pred[]{:T(512)S(6)} %eq.56), kind=kLoop, calls=%fused_computation.1 | loop fusion | flops 1769472 | bytes 4718593 | tf_op jit(solution)/shard_map/jit(_where)/select_n | solution.py:244
  135.2 1.2 collective-permute-done.23
  136.4 0.3 maximum_select_fusion
  136.7 1.6 %slice.95 = f32[2304,256]{1,0:T(8,128)} slice(f32[2432,256]{1,0:T(8,128)S(1)} %maximum_select_fusion), slice={[0:2304], [0:256]} | slice | bytes 4718592 | tf_op jit(solution)/shard_map/slice | solution.py:525
  138.3 0.6 multiply_multiply_fusion
  (52 shorter events, 0.7 us)
Async XLA Ops:
  0.6 0.7 copy-start
  1.3 0.7 copy-start.5
  2.0 7.5 %copy-start.2 = (bf16[9,256,256]{2,1,0:T(8,128)(2,1)S(1)}, bf16[9,256,256]{2,1,0:T(8,128)(2,1)}, u32[]{:S(2)}) copy-start(bf16[9,256,256]{2,1,0:T(8,128)(2,1)} %weights_ref.8) | copy-start | bytes 3538948
  9.0 7.6 %copy-start.1 = (f32[256]{0:T(256)S(1)}, f32[256]{0:T(256)}, u32[]{:S(2)}) copy-start(f32[256]{0:T(256)} %param.9) | copy-start | bytes 3076
  9.0 7.6 %copy-start.6 = (f32[64]{0:T(128)S(1)}, f32[64]{0:T(128)}, u32[]{:S(2)}) copy-start(f32[64]{0:T(128)} %step_ref.9) | copy-start | bytes 772
  9.0 5.0 %collective-permute-start = (f32[72,256]{1,0:T(8,128)S(1)}, f32[72,256]{1,0:T(8,128)S(1)}, u32[]{:S(2)}, u32[]{:S(2)}) collective-permute-start(f32[72,256]{1,0:T(8,128)S(1)} %get-tuple-element.46), channel_id=1, source_target_pairs={{0,1},{1,0},{2,3},{3,2},{4,5},{5,4},{6,7},{7,6},{8,9},{9,8},{10,11... | collective-permute-start | bytes 221192 | tf_op jit(solution)/shard_map/ppermute | solution.py:318
  14.0 7.2 %collective-permute-start.1 = (f32[72,256]{1,0:T(8,128)S(1)}, f32[72,256]{1,0:T(8,128)S(1)}, u32[]{:S(2)}, u32[]{:S(2)}) collective-permute-start(f32[72,256]{1,0:T(8,128)S(1)} %pad_maximum_fusion), channel_id=1, source_target_pairs={{0,2},{1,3},{2,0},{3,1},{4,6},{5,7},{6,4},{7,5},{8,10},{9,11},{10,... | collective-permute-start | bytes 221192 | tf_op jit(solution)/shard_map/ppermute | solution.py:318
  21.2 4.4 %collective-permute-start.2 = (f32[72,256]{1,0:T(8,128)S(1)}, f32[72,256]{1,0:T(8,128)S(1)}, u32[]{:S(2)}, u32[]{:S(2)}) collective-permute-start(f32[72,256]{1,0:T(8,128)S(1)} %pad_maximum_fusion.1), channel_id=1, source_target_pairs={{0,4},{1,5},{2,6},{3,7},{4,0},{5,1},{6,2},{7,3},{8,12},{9,13},{10,... | collective-permute-start | bytes 221192 | tf_op jit(solution)/shard_map/ppermute | solution.py:318
  22.9 7.3 %collective-permute-start.4 = (f32[72,256]{1,0:T(8,128)S(1)}, f32[72,256]{1,0:T(8,128)S(1)}, u32[]{:S(2)}, u32[]{:S(2)}) collective-permute-start(f32[72,256]{1,0:T(8,128)S(1)} %get-tuple-element.53), channel_id=1, source_target_pairs={{0,1},{1,0},{2,3},{3,2},{4,5},{5,4},{6,7},{7,6},{8,9},{9,8},{10,11... | collective-permute-start | bytes 221192 | tf_op jit(solution)/shard_map/ppermute | solution.py:318
  25.7 6.5 %collective-permute-start.3 = (f32[72,256]{1,0:T(8,128)S(1)}, f32[72,256]{1,0:T(8,128)S(1)}, u32[]{:S(2)}, u32[]{:S(2)}) collective-permute-start(f32[72,256]{1,0:T(8,128)S(1)} %pad_maximum_fusion.2), channel_id=1, source_target_pairs={{0,8},{1,9},{2,10},{3,11},{4,12},{5,13},{6,14},{7,15},{16,24},{17,... | collective-permute-start | bytes 221192 | tf_op jit(solution)/shard_map/ppermute | solution.py:318
  30.3 4.4 %collective-permute-start.5 = (f32[72,256]{1,0:T(8,128)S(1)}, f32[72,256]{1,0:T(8,128)S(1)}, u32[]{:S(2)}, u32[]{:S(2)}) collective-permute-start(f32[72,256]{1,0:T(8,128)S(1)} %pad_maximum_fusion.3), channel_id=1, source_target_pairs={{0,2},{1,3},{2,0},{3,1},{4,6},{5,7},{6,4},{7,5},{8,10},{9,11},{10,... | collective-permute-start | bytes 221192 | tf_op jit(solution)/shard_map/ppermute | solution.py:318
  42.4 8.7 %collective-permute-start.9 = (f32[1152,256]{1,0:T(8,128)S(1)}, f32[1152,256]{1,0:T(8,128)}, u32[]{:S(2)}, u32[]{:S(2)}) collective-permute-start(f32[1152,256]{1,0:T(8,128)S(1)} %get-tuple-element.59), channel_id=1, source_target_pairs={{0,1},{1,0},{2,3},{3,2},{4,5},{5,4},{6,7},{7,6},{8,9},{9,8},{10,11... | collective-permute-start | bytes 3538952 | tf_op jit(solution)/shard_map/ppermute | solution.py:269
  42.5 8.7 %collective-permute-start.8 = (f32[72,256]{1,0:T(8,128)S(1)}, f32[72,256]{1,0:T(8,128)S(1)}, u32[]{:S(2)}, u32[]{:S(2)}) collective-permute-start(f32[72,256]{1,0:T(8,128)S(1)} %pad_maximum_fusion.4), channel_id=1, source_target_pairs={{12,0},{13,1},{14,2},{15,3},{28,16},{29,17},{30,18},{31,19}} | collective-permute-start | bytes 221192 | tf_op jit(solution)/shard_map/ppermute | solution.py:334
  43.8 9.5 %collective-permute-start.6 = (f32[72,256]{1,0:T(8,128)S(1)}, f32[72,256]{1,0:T(8,128)S(1)}, u32[]{:S(2)}, u32[]{:S(2)}) collective-permute-start(f32[72,256]{1,0:T(8,128)S(1)} %pad_maximum_fusion.4), channel_id=1, source_target_pairs={{4,0},{5,1},{6,2},{7,3},{8,4},{9,5},{10,6},{11,7},{12,8},{13,9},{1... | collective-permute-start | bytes 221192 | tf_op jit(solution)/shard_map/ppermute | solution.py:334
  45.1 10.5 %collective-permute-start.7 = (f32[72,256]{1,0:T(8,128)S(1)}, f32[72,256]{1,0:T(8,128)S(1)}, u32[]{:S(2)}, u32[]{:S(2)}) collective-permute-start(f32[72,256]{1,0:T(8,128)S(1)} %pad_maximum_fusion.4), channel_id=1, source_target_pairs={{8,0},{9,1},{10,2},{11,3},{12,4},{13,5},{14,6},{15,7},{24,16},{25,... | collective-permute-start | bytes 221192 | tf_op jit(solution)/shard_map/ppermute | solution.py:334
  52.7 11.7 %collective-permute-start.10 = (f32[576,256]{1,0:T(8,128)S(1)}, f32[576,256]{1,0:T(8,128)S(1)}, u32[]{:S(2)}, u32[]{:S(2)}) collective-permute-start(f32[576,256]{1,0:T(8,128)S(1)} %constant_dynamic-slice_fusion.5), channel_id=1, source_target_pairs={{0,2},{1,5},{2,0},{3,7},{4,6},{5,1},{6,4},{7,3},{8,10},{9,13},{10,... | collective-permute-start | bytes 1769480 | tf_op jit(solution)/shard_map/ppermute | solution.py:269
  64.5 3.1 %collective-permute-start.11 = (f32[1216,256]{1,0:T(8,128)S(1)}, f32[1216,256]{1,0:T(8,128)}, u32[]{:S(2)}, u32[]{:S(2)}) collective-permute-start(f32[1216,256]{1,0:T(8,128)S(1)} %get-tuple-element.70), channel_id=1, source_target_pairs={{0,1},{1,0},{2,3},{3,2},{4,5},{5,4},{6,7},{7,6},{8,9},{9,8},{10,11... | collective-permute-start | bytes 3735560 | tf_op jit(solution)/shard_map/ppermute | solution.py:269
  64.6 11.9 %collective-permute-start.13 = (f32[288,256]{1,0:T(8,128)S(1)}, f32[288,256]{1,0:T(8,128)S(1)}, u32[]{:S(2)}, u32[]{:S(2)}) collective-permute-start(f32[288,256]{1,0:T(8,128)S(1)} %constant_dynamic-slice_fusion.4), channel_id=1, source_target_pairs={{0,4},{1,9},{2,6},{3,11},{4,0},{5,13},{6,2},{7,15},{8,12},{9,1},{1... | collective-permute-start | bytes 884744 | tf_op jit(solution)/shard_map/ppermute | solution.py:269
  69.1 1.3 copy-start.3
  69.2 10.4 %collective-permute-start.12 = (f32[608,256]{1,0:T(8,128)S(1)}, f32[608,256]{1,0:T(8,128)S(1)}, u32[]{:S(2)}, u32[]{:S(2)}) collective-permute-start(f32[608,256]{1,0:T(8,128)S(1)} %constant_dynamic-slice_fusion.3), channel_id=1, source_target_pairs={{0,2},{1,5},{2,0},{3,7},{4,6},{5,1},{6,4},{7,3},{8,10},{9,13},{10,... | collective-permute-start | bytes 1867784 | tf_op jit(solution)/shard_map/ppermute | solution.py:269
  76.5 3.2 %copy-start.4 = (bf16[9,256,256]{2,1,0:T(8,128)(2,1)S(1)}, bf16[9,256,256]{2,1,0:T(8,128)(2,1)}, u32[]{:S(2)}) copy-start(bf16[9,256,256]{2,1,0:T(8,128)(2,1)} %weights_ref.9) | copy-start | bytes 3538948
  76.5 9.7 %collective-permute-start.15 = (f32[144,256]{1,0:T(8,128)S(1)}, f32[144,256]{1,0:T(8,128)S(1)}, u32[]{:S(2)}, u32[]{:S(2)}) collective-permute-start(f32[144,256]{1,0:T(8,128)S(1)} %constant_dynamic-slice_fusion.2), channel_id=1, source_target_pairs={{0,8},{1,3},{2,10},{3,1},{4,12},{5,7},{6,14},{7,5},{8,0},{9,11},{1... | collective-permute-start | bytes 442376 | tf_op jit(solution)/shard_map/ppermute | solution.py:269
  79.7 8.1 %collective-permute-start.14 = (f32[304,256]{1,0:T(8,128)S(1)}, f32[304,256]{1,0:T(8,128)S(1)}, u32[]{:S(2)}, u32[]{:S(2)}) collective-permute-start(f32[304,256]{1,0:T(8,128)S(1)} %constant_dynamic-slice_fusion.1), channel_id=1, source_target_pairs={{0,4},{1,9},{2,6},{3,11},{4,0},{5,13},{6,2},{7,15},{8,12},{9,1},{1... | collective-permute-start | bytes 933896 | tf_op jit(solution)/shard_map/ppermute | solution.py:269
  86.2 10.3 %collective-permute-start.17 = (f32[144,256]{1,0:T(8,128)S(1)}, f32[144,256]{1,0:T(8,128)S(1)}, u32[]{:S(2)}, u32[]{:S(2)}) collective-permute-start(f32[144,256]{1,0:T(8,128)S(1)} %dynamic-slice_add_fusion.5), channel_id=1, source_target_pairs={{0,8},{1,3},{2,10},{3,1},{4,12},{5,7},{6,14},{7,5},{8,0},{9,11},{1... | collective-permute-start | bytes 442376 | tf_op jit(solution)/shard_map/ppermute | solution.py:269
  87.9 11.5 %collective-permute-start.16 = (f32[152,256]{1,0:T(8,128)S(1)}, f32[152,256]{1,0:T(8,128)S(1)}, u32[]{:S(2)}, u32[]{:S(2)}) collective-permute-start(f32[152,256]{1,0:T(8,128)S(1)} %constant_dynamic-slice_fusion), channel_id=1, source_target_pairs={{0,8},{1,3},{2,10},{3,1},{4,12},{5,7},{6,14},{7,5},{8,0},{9,11},{1... | collective-permute-start | bytes 466952 | tf_op jit(solution)/shard_map/ppermute | solution.py:269
  96.5 9.7 %collective-permute-start.19 = (f32[288,256]{1,0:T(8,128)S(1)}, f32[288,256]{1,0:T(8,128)S(1)}, u32[]{:S(2)}, u32[]{:S(2)}) collective-permute-start(f32[288,256]{1,0:T(8,128)S(1)} %maximum_select_fusion.7), channel_id=1, source_target_pairs={{0,4},{1,9},{2,6},{3,11},{4,0},{5,13},{6,2},{7,15},{8,12},{9,1},{1... | collective-permute-start | bytes 884744 | tf_op jit(solution)/shard_map/ppermute | solution.py:269
  106.2 9.9 %collective-permute-start.21 = (f32[576,256]{1,0:T(8,128)S(1)}, f32[576,256]{1,0:T(8,128)S(1)}, u32[]{:S(2)}, u32[]{:S(2)}) collective-permute-start(f32[576,256]{1,0:T(8,128)S(1)} %maximum_select_fusion.5), channel_id=1, source_target_pairs={{0,2},{1,5},{2,0},{3,7},{4,6},{5,1},{6,4},{7,3},{8,10},{9,13},{10,... | collective-permute-start | bytes 1769480 | tf_op jit(solution)/shard_map/ppermute | solution.py:269
  106.7 7.5 %collective-permute-start.18 = (f32[152,256]{1,0:T(8,128)S(1)}, f32[152,256]{1,0:T(8,128)S(1)}, u32[]{:S(2)}, u32[]{:S(2)}) collective-permute-start(f32[152,256]{1,0:T(8,128)S(1)} %dynamic-slice_add_fusion.4), channel_id=1, source_target_pairs={{0,8},{1,3},{2,10},{3,1},{4,12},{5,7},{6,14},{7,5},{8,0},{9,11},{1... | collective-permute-start | bytes 466952 | tf_op jit(solution)/shard_map/ppermute | solution.py:269
  114.3 8.6 %collective-permute-start.20 = (f32[304,256]{1,0:T(8,128)S(1)}, f32[304,256]{1,0:T(8,128)S(1)}, u32[]{:S(2)}, u32[]{:S(2)}) collective-permute-start(f32[304,256]{1,0:T(8,128)S(1)} %maximum_select_fusion.6), channel_id=1, source_target_pairs={{0,4},{1,9},{2,6},{3,11},{4,0},{5,13},{6,2},{7,15},{8,12},{9,1},{1... | collective-permute-start | bytes 933896 | tf_op jit(solution)/shard_map/ppermute | solution.py:269
  123.0 10.3 %collective-permute-start.22 = (f32[608,256]{1,0:T(8,128)S(1)}, f32[608,256]{1,0:T(8,128)S(1)}, u32[]{:S(2)}, u32[]{:S(2)}) collective-permute-start(f32[608,256]{1,0:T(8,128)S(1)} %maximum_select_fusion.4), channel_id=1, source_target_pairs={{0,2},{1,5},{2,0},{3,7},{4,6},{5,1},{6,4},{7,3},{8,10},{9,13},{10,... | collective-permute-start | bytes 1867784 | tf_op jit(solution)/shard_map/ppermute | solution.py:269
  124.7 8.7 %collective-permute-start.24 = (f32[1152,256]{1,0:T(8,128)S(1)}, f32[1152,256]{1,0:T(8,128)S(1)}, u32[]{:S(2)}, u32[]{:S(2)}) collective-permute-start(f32[1152,256]{1,0:T(8,128)S(1)} %maximum_select_fusion.3), channel_id=1, source_target_pairs={{0,1},{1,0},{2,3},{3,2},{4,5},{5,4},{6,7},{7,6},{8,9},{9,8},{10,11... | collective-permute-start | bytes 3538952 | tf_op jit(solution)/shard_map/ppermute | solution.py:269
  133.4 3.0 %collective-permute-start.23 = (f32[1216,256]{1,0:T(8,128)S(1)}, f32[1216,256]{1,0:T(8,128)S(1)}, u32[]{:S(2)}, u32[]{:S(2)}) collective-permute-start(f32[1216,256]{1,0:T(8,128)S(1)} %maximum_select_fusion.2), channel_id=1, source_target_pairs={{0,1},{1,0},{2,3},{3,2},{4,5},{5,4},{6,7},{7,6},{8,9},{9,8},{10,11... | collective-permute-start | bytes 3735560 | tf_op jit(solution)/shard_map/ppermute | solution.py:269

commit v4 on v3

--- a/solution.py
+++ b/solution.py
@@ -240,8 +240,13 @@
     return lax.dynamic_slice_in_dim(value, bit[0] * half, half)
 
 
-def merge(bit, mine, other):
-    return jnp.where(bit[0] == 0, jnp.concatenate([mine, other]), jnp.concatenate([other, mine]))
+def merge(bit, mine, other, rows=None):
+    if rows is None or rows == 2 * mine.shape[0]:
+        return jnp.where(bit[0] == 0, jnp.concatenate([mine, other]), jnp.concatenate([other, mine]))
+    cut = rows - mine.shape[0]
+    first, last = (mine, other[: cut + 8]), (other, mine[: cut + 8])
+    main = jnp.where(bit[0] == 0, jnp.concatenate([first[0], first[1][:cut]]), jnp.concatenate([last[0], last[1][:cut]]))
+    return main, jnp.where(bit[0] == 0, first[1][cut:], last[1][cut:])
 
 
 def swap(value, count, distance):
@@ -257,8 +262,8 @@
 
 
 class Sum:
-    def __init__(self, keep, send, bits, orders, count):
-        self.keep, self.send, self.count = keep, send, count
+    def __init__(self, keep, send, bits, orders, count, rows):
+        self.keep, self.send, self.count, self.rows = keep, send, count, rows
         self.orders = orders
         self.bits = [jnp.where(bits[0] == 0, bits[even], bits[odd]) for even, odd in zip(*orders)]
         self.stage = 0
@@ -289,7 +294,7 @@
         if self.left > len(self.bits):
             self.fold()
         else:
-            self.send = merge(self.bits[self.stage], self.send, self.recv)
+            self.send = merge(self.bits[self.stage], self.send, self.recv, self.rows if self.left == 1 else None)
         self.left -= 1
         if self.left > len(self.bits):
             self.start()
@@ -349,7 +354,7 @@
 
 
 def turns(levels):
-    return "icoic" + "oi" * (2 * levels - 3) + "i"
+    return "icoioic" + "oi" * (2 * levels - 4) + "i"
 
 
 def body(latents, input_map, output_map, decay_rate, frame_step, cotangent):
@@ -376,7 +381,7 @@
 
     def drive(value, kernel_map, reverse, base, size, start=None):
         specs = [smem(), fixed(rate.shape), framed(shape, block, size, reverse, base), fixed(weights)]
-        operands = [frame_step, rate, far(value), kernel_map if reverse else far(kernel_map)]
+        operands = [far(frame_step), far(rate), far(value), kernel_map if reverse else far(kernel_map)]
         if start is not None:
             specs.append(fixed((map_rows + 8, channels)))
             operands.append(start)
@@ -463,10 +468,10 @@
             aliases,
         )(*operands)
 
-    orders = (list(range(levels)), [0] + list(range(2, levels)) + [1])
+    orders = (list(range(levels)), [0, 2, 1] + list(range(3, levels)))
     backward.combine_rest(out_send)
     arriving = backward.result()
-    out_sum = Sum(out_keep, out_send, bits, orders, count)
+    out_sum = Sum(out_keep, out_send, bits, orders, count, grad_rows)
     out_sum.start()
     out_sum.step()
 
@@ -506,7 +511,7 @@
 
     out_sum.wait(in_send)
     out_sum.step()
-    in_sum = Sum(in_keep, after(in_send, out_sum.send), bits, orders, count)
+    in_sum = Sum(in_keep, after(in_send, out_sum.send), bits, orders, count, grad_rows)
     in_sum.start()
     covers = [(adjoint_low, input_map, True), (states_low, output_map, False)]
     convs = []
@@ -522,8 +527,7 @@
             one.step()
             latest = one.send
     layer_out, grad_latents = convs
-    grad_output_map, grad_input_map = out_sum.send, in_sum.send[:grad_rows]
-    rate_rows = in_sum.send[grad_rows : grad_rows + 8]
+    grad_output_map, (grad_input_map, rate_rows) = out_sum.send, in_sum.send
     grad_log_rate = -factor * decay_rate * jnp.sum(rate_rows, axis=0)
     return (
         layer_out,

time: 140 us -> 135 us (0.964)
  waiting for transfers between devices: 63.3 us -> 51.6 us
  starting transfers between devices: 19.3 us -> 27.8 us
  local copies, waits for them, and re-layouts: 3.74 us -> 0.72 us
    ppermute x16, waiting for transfers between devices: 49.7 us -> 39.6 us  [swap(): lax.ppermute(value, 'tm', [(source, source ^ 1 << levels[source & 1]) for...]
    ppermute x16, starting transfers between devices: 5.51 us -> 14 us  [swap(): lax.ppermute(value, 'tm', [(source, source ^ 1 << levels[source & 1]) for...]
    select_n x0 -> x1, other arithmetic: none -> 1.71 us  [merge(): jnp.where(bit[0] == 0, jnp.concatenate([first[0], first[1][:cut]]), jnp.c...]
    unnamed x14 -> x10, local copies, waits for them, and re-layouts: 1.98 us -> 0.38 us
    ppermute x3, waiting for transfers between devices: 6.93 us -> 5.41 us  [start_rest(): lax.ppermute(self.message, 'tm', [(source, source + hop) for source in ra...]
    slice x1 -> x2, local copies, waits for them, and re-layouts: 1.56 us -> 0.15 us  [the longest x1 0.07 us: merge(): first[1][:cut]]
  transfers between devices with their start and end apart: 25 -> 25, of which waited for: 16 -> 17; matrix products, arithmetic and copies ran while one was open for 4% -> 4% of each run, Pallas kernels for 22% -> 23%
where the time goes in v4:
time: 135 us; the launch traced here: 134 us
  waiting for transfers between devices  51.6 us (38%)
  Pallas kernels  45.2 us (33%)
  starting transfers between devices  27.8 us (21%)
  other arithmetic  7.71 us (6%)
    ppermute x16, waiting for transfers between devices, swap(): lax.ppermute(value, 'tm', [(source, source ^ 1 << levels[source & 1]) for...  39.6 us
    pallas_call x3, Pallas kernels, drive(): call(functools.partial(drive_kernel, reverse, base, start is None), (size...  16.1 us
    ppermute x16, starting transfers between devices, swap(): lax.ppermute(value, 'tm', [(source, source ^ 1 << levels[source & 1]) for...  14 us
    pallas_call x2, Pallas kernels, conv(): call(functools.partial(conv_kernel, reverse), (size,), specs, framed(shap...  12.5 us
    ppermute x6, starting transfers between devices, start(): self.other = lax.ppermute(self.message, 'tm', pairs)  9.78 us
    pallas_call x1, Pallas kernels, body(): call(functools.partial(adjoint_kernel, factor, steps - later), grid, [sme...  8.8 us
    pallas_call x1, Pallas kernels, body(): call(functools.partial(state_kernel, factor), grid, [smem(), smem(), fixe...  7.72 us
    ppermute x6, waiting for transfers between devices, start(): self.other = lax.ppermute(self.message, 'tm', pairs)  6.61 us
  transfers between devices with their start and end apart: 25, of which 17 were waited for; matrix products, arithmetic and copies ran while one was open for 4% of the time, Pallas kernels for 23%

profile of v4, /device:TPU:0, one launch (start us, length us, event | category | flops | bytes accessed | tf_op | source)
XLA Modules:
  0.0 134.0 jit_solution(6521223258405052653)
XLA Ops:
  0.6 0.0 copy-start.1
  0.6 7.0 %drive.1 = (f32[64,2,32,256]{3,2,1,0:T(8,128)}, f32[72,256]{1,0:T(8,128)S(1)}) custom-call(f32[64]{0:T(128)} %step_ref.9, f32[1,256]{1,0:T(1,128)} %bitcast.110, bf16[64,2,32,256]{3,2,1,0:T(8,128)(2,1)} %latents_ref.1, bf16[9,256,256]{2,1,0:T(8,128)(2,1)} %weights_ref.9), custom_call_target="tpu_custom_call" | custom-call | flops 3221225472 | bytes 6291456 | tf_op jit(solution)/shard_map/drive/pallas_call | solution.py:388
  7.7 0.5 collective-permute-start
  8.1 4.5 %pull.2 = (f32[32,2,32,256]{3,2,1,0:T(8,128)}, f32[72,256]{1,0:T(8,128)S(1)}) custom-call(f32[64]{0:T(128)} %step_ref.9, f32[1,256]{1,0:T(1,128)} %bitcast.111, bf16[64,2,32,256]{3,2,1,0:T(8,128)(2,1)} %cotangent_ref.1, bf16[9,256,256]{2,1,0:T(8,128)(2,1)S(1)} %copy-done.1), custom_call_target="tpu_custom_call" | custom-call | flops 1610612736 | bytes 3145728 | tf_op jit(solution)/shard_map/pull/pallas_call | solution.py:388
  12.7 2.6 %collective-permute-start.1 = (f32[72,256]{1,0:T(8,128)S(1)}, f32[72,256]{1,0:T(8,128)S(1)}, u32[]{:S(2)}, u32[]{:S(2)}) collective-permute-start(f32[72,256]{1,0:T(8,128)S(1)} %pad_maximum_fusion), channel_id=1, source_target_pairs={{0,2},{1,3},{2,0},{3,1},{4,6},{5,7},{6,4},{7,5},{8,10},{9,11},{10,... | collective-permute-start | bytes 221192 | tf_op jit(solution)/shard_map/ppermute | solution.py:323
  15.3 4.5 %pull.3 = (f32[32,2,32,256]{3,2,1,0:T(8,128)}, f32[72,256]{1,0:T(8,128)S(1)}) custom-call(f32[64]{0:T(128)} %step_ref.9, f32[1,256]{1,0:T(1,128)} %bitcast.112, bf16[64,2,32,256]{3,2,1,0:T(8,128)(2,1)} %cotangent_ref.1, bf16[9,256,256]{2,1,0:T(8,128)(2,1)S(1)} %copy-done.1, f32[72,256]{1,0:T(8,128)S(1)} %get-tuple-element.50.refs_0_), custom_call_target="tpu_custom_call" | custom-call | flops 1610612736 | bytes 3145728 | tf_op jit(solution)/shard_map/pull/pallas_call | solution.py:388
  19.9 0.0 collective-permute-done.1
  19.9 1.6 %collective-permute-start.2 = (f32[72,256]{1,0:T(8,128)S(1)}, f32[72,256]{1,0:T(8,128)S(1)}, u32[]{:S(2)}, u32[]{:S(2)}) collective-permute-start(f32[72,256]{1,0:T(8,128)S(1)} %pad_maximum_fusion.1), channel_id=1, source_target_pairs={{0,4},{1,5},{2,6},{3,7},{4,0},{5,1},{6,2},{7,3},{8,12},{9,13},{10,... | collective-permute-start | bytes 221192 | tf_op jit(solution)/shard_map/ppermute | solution.py:323
  21.6 2.8 %collective-permute-done.2 = f32[72,256]{1,0:T(8,128)S(1)} collective-permute-done((f32[72,256]{1,0:T(8,128)S(1)}, f32[72,256]{1,0:T(8,128)S(1)}, u32[]{:S(2)}, u32[]{:S(2)}) %collective-permute-start.2) | collective-permute-done | bytes 73760 | tf_op jit(solution)/shard_map/ppermute | solution.py:323
  24.4 4.5 %collective-permute-start.3 = (f32[72,256]{1,0:T(8,128)S(1)}, f32[72,256]{1,0:T(8,128)S(1)}, u32[]{:S(2)}, u32[]{:S(2)}) collective-permute-start(f32[72,256]{1,0:T(8,128)S(1)} %pad_maximum_fusion.2), channel_id=1, source_target_pairs={{0,8},{1,9},{2,10},{3,11},{4,12},{5,13},{6,14},{7,15},{16,24},{17,... | collective-permute-start | bytes 221192 | tf_op jit(solution)/shard_map/ppermute | solution.py:323
  29.0 0.6 collective-permute-start.5
  29.5 1.3 collective-permute-done.3
  30.9 2.5 %collective-permute-done.5 = f32[72,256]{1,0:T(8,128)S(1)} collective-permute-done((f32[72,256]{1,0:T(8,128)S(1)}, f32[72,256]{1,0:T(8,128)S(1)}, u32[]{:S(2)}, u32[]{:S(2)}) %collective-permute-start.5) | collective-permute-done | bytes 73760 | tf_op jit(solution)/shard_map/ppermute | solution.py:323
  33.4 7.7 %states.1 = (bf16[64,2,32,256]{3,2,1,0:T(8,128)(2,1)}, f32[1152,256]{1,0:T(8,128)S(1)}, f32[1152,256]{1,0:T(8,128)S(1)}) custom-call(f32[64]{0:T(128)S(1)} %copy-done.4, s32[1]{0:T(128)} %bitcast.core_ref, f32[1,256]{1,0:T(1,128)S(1)} %bitcast.113, f32[64,256]{1,0:T(8,128)S(1)} %add_select_fusion.1.incoming_ref, ...), custom_call_target="tpu_custom_call" | custom-call | flops 3221225472 | bytes 8388608 | tf_op jit(solution)/shard_map/states/pallas_call | solution.py:431
  41.2 1.3 collective-permute-start.8
  42.5 1.3 collective-permute-start.7
  43.8 1.5 %collective-permute-start.6 = (f32[72,256]{1,0:T(8,128)S(1)}, f32[72,256]{1,0:T(8,128)S(1)}, u32[]{:S(2)}, u32[]{:S(2)}) collective-permute-start(f32[72,256]{1,0:T(8,128)S(1)} %pad_maximum_fusion.4), channel_id=1, source_target_pairs={{4,0},{5,1},{6,2},{7,3},{8,4},{9,5},{10,6},{11,7},{12,8},{13,9},{1... | collective-permute-start | bytes 221192 | tf_op jit(solution)/shard_map/ppermute | solution.py:339
  45.3 4.7 %collective-permute-done.8 = f32[72,256]{1,0:T(8,128)S(1)} collective-permute-done((f32[72,256]{1,0:T(8,128)S(1)}, f32[72,256]{1,0:T(8,128)S(1)}, u32[]{:S(2)}, u32[]{:S(2)}) %collective-permute-start.8) | collective-permute-done | bytes 73760 | tf_op jit(solution)/shard_map/ppermute | solution.py:339
  49.9 1.4 %add.158 = f32[1152,256]{1,0:T(8,128)S(1)} add(f32[1152,256]{1,0:T(8,128)S(1)} %get-tuple-element.63, f32[1152,256]{1,0:T(8,128)} %collective-permute-done.9) | non-fusion elementwise | flops 294912 | bytes 3538944 | tf_op jit(solution)/shard_map/add | solution.py:283
  51.4 0.6 collective-permute-start.10
  52.0 0.8 collective-permute-done.7
  52.8 8.8 %adjoint.1 = (bf16[64,2,32,256]{3,2,1,0:T(8,128)(2,1)}, f32[1216,256]{1,0:T(8,128)S(1)}, f32[1216,256]{1,0:T(8,128)S(1)}) custom-call(f32[64]{0:T(128)S(1)} %copy-done.4, s32[1]{0:T(128)} %bitcast.core_ref, f32[1,256]{1,0:T(1,128)S(1)} %bitcast.114, f32[64,256]{1,0:T(8,128)S(1)} %fusion.arriving_ref, f32[64,256]{1,0:T(8,128)S(1)} %add_select_fusion.1.incoming_ref, ...), custom_call_target="tpu_custom_call" | custom-call | flops 3221225472 | bytes 10485760 | tf_op jit(solution)/shard_map/adjoint/pallas_call | solution.py:478
  61.6 0.1 dynamic-slice_add_fusion.1
  61.7 0.1 collective-permute-start.11
  61.8 2.2 %collective-permute-start.13 = (f32[288,256]{1,0:T(8,128)S(1)}, f32[288,256]{1,0:T(8,128)S(1)}, u32[]{:S(2)}, u32[]{:S(2)}) collective-permute-start(f32[288,256]{1,0:T(8,128)S(1)} %constant_dynamic-slice_fusion.4), channel_id=1, source_target_pairs={{0,4},{1,3},{2,6},{3,1},{4,0},{5,7},{6,2},{7,5},{8,12},{9,11},{10,... | collective-permute-start | bytes 884744 | tf_op jit(solution)/shard_map/ppermute | solution.py:274
  64.0 0.9 collective-permute-done.11
  64.8 1.5 %add.163 = f32[1216,256]{1,0:T(8,128)S(1)} add(f32[1216,256]{1,0:T(8,128)S(1)} %get-tuple-element.67, f32[1216,256]{1,0:T(8,128)} %collective-permute-done.11) | non-fusion elementwise | flops 311296 | bytes 3735552 | tf_op jit(solution)/shard_map/add | solution.py:283
  66.3 0.0 copy-start.2
  66.3 0.1 constant_dynamic-slice_fusion.3
  66.4 0.9 collective-permute-start.12
  67.2 0.4 copy-done.2
  67.6 6.1 %conv.2 = bf16[64,2,32,256]{3,2,1,0:T(8,128)(2,1)} custom-call(bf16[64,2,32,256]{3,2,1,0:T(8,128)(2,1)} %get-tuple-element.72.states_ref.previous_ref.value_ref, bf16[9,256,256]{2,1,0:T(8,128)(2,1)S(1)} %copy-done.2), custom_call_target="tpu_custom_call" | custom-call | flops 3221225472 | bytes 4194304 | tf_op jit(solution)/shard_map/conv/pallas_call | solution.py:458
  73.7 1.2 collective-permute-start.15
  74.9 1.8 %collective-permute-done.12 = f32[608,256]{1,0:T(8,128)S(1)} collective-permute-done((f32[608,256]{1,0:T(8,128)S(1)}, f32[608,256]{1,0:T(8,128)S(1)}, u32[]{:S(2)}, u32[]{:S(2)}) %collective-permute-start.12) | collective-permute-done | bytes 622624 | tf_op jit(solution)/shard_map/ppermute | solution.py:274
  76.7 0.1 dynamic-slice_add_fusion
  76.8 0.0 copy-start.3
  76.8 2.2 %collective-permute-start.14 = (f32[304,256]{1,0:T(8,128)S(1)}, f32[304,256]{1,0:T(8,128)S(1)}, u32[]{:S(2)}, u32[]{:S(2)}) collective-permute-start(f32[304,256]{1,0:T(8,128)S(1)} %constant_dynamic-slice_fusion.1), channel_id=1, source_target_pairs={{0,4},{1,3},{2,6},{3,1},{4,0},{5,7},{6,2},{7,5},{8,12},{9,11},{10,... | collective-permute-start | bytes 933896 | tf_op jit(solution)/shard_map/ppermute | solution.py:274
  79.0 5.6 %collective-permute-done.15 = f32[144,256]{1,0:T(8,128)S(1)} collective-permute-done((f32[144,256]{1,0:T(8,128)S(1)}, f32[144,256]{1,0:T(8,128)S(1)}, u32[]{:S(2)}, u32[]{:S(2)}) %collective-permute-start.15) | collective-permute-done | bytes 147488 | tf_op jit(solution)/shard_map/ppermute | solution.py:274
  84.6 0.1 collective-permute-start.17
  84.6 1.4 %collective-permute-done.14 = f32[304,256]{1,0:T(8,128)S(1)} collective-permute-done((f32[304,256]{1,0:T(8,128)S(1)}, f32[304,256]{1,0:T(8,128)S(1)}, u32[]{:S(2)}, u32[]{:S(2)}) %collective-permute-start.14) | collective-permute-done | bytes 311328 | tf_op jit(solution)/shard_map/ppermute | solution.py:274
  86.1 1.6 %collective-permute-start.16 = (f32[152,256]{1,0:T(8,128)S(1)}, f32[152,256]{1,0:T(8,128)S(1)}, u32[]{:S(2)}, u32[]{:S(2)}) collective-permute-start(f32[152,256]{1,0:T(8,128)S(1)} %constant_dynamic-slice_fusion), channel_id=1, source_target_pairs={{0,8},{1,9},{2,10},{3,11},{4,12},{5,13},{6,14},{7,15},{8,0},{9,1},... | collective-permute-start | bytes 466952 | tf_op jit(solution)/shard_map/ppermute | solution.py:274
  87.7 6.5 %conv.3 = bf16[64,2,32,256]{3,2,1,0:T(8,128)(2,1)} custom-call(bf16[64,2,32,256]{3,2,1,0:T(8,128)(2,1)} %get-tuple-element.78.value_ref, bf16[9,256,256]{2,1,0:T(8,128)(2,1)S(1)} %copy-done.3), custom_call_target="tpu_custom_call" | custom-call | flops 3221225472 | bytes 4194304 | tf_op jit(solution)/shard_map/conv/pallas_call | solution.py:458
  94.1 1.8 %collective-permute-done.17 = f32[144,256]{1,0:T(8,128)S(1)} collective-permute-done((f32[144,256]{1,0:T(8,128)S(1)}, f32[144,256]{1,0:T(8,128)S(1)}, u32[]{:S(2)}, u32[]{:S(2)}) %collective-permute-start.17) | collective-permute-done | bytes 147488 | tf_op jit(solution)/shard_map/ppermute | solution.py:274
  96.0 0.3 collective-permute-start.19
  96.3 2.9 %collective-permute-done.16 = f32[152,256]{1,0:T(8,128)S(1)} collective-permute-done((f32[152,256]{1,0:T(8,128)S(1)}, f32[152,256]{1,0:T(8,128)S(1)}, u32[]{:S(2)}, u32[]{:S(2)}) %collective-permute-start.16) | collective-permute-done | bytes 155680 | tf_op jit(solution)/shard_map/ppermute | solution.py:274
  99.2 3.6 %collective-permute-done.19 = f32[288,256]{1,0:T(8,128)S(1)} collective-permute-done((f32[288,256]{1,0:T(8,128)S(1)}, f32[288,256]{1,0:T(8,128)S(1)}, u32[]{:S(2)}, u32[]{:S(2)}) %collective-permute-start.19) | collective-permute-done | bytes 294944 | tf_op jit(solution)/shard_map/ppermute | solution.py:274
  102.8 0.5 collective-permute-start.21
  103.3 1.3 %collective-permute-start.18 = (f32[152,256]{1,0:T(8,128)S(1)}, f32[152,256]{1,0:T(8,128)S(1)}, u32[]{:S(2)}, u32[]{:S(2)}) collective-permute-start(f32[152,256]{1,0:T(8,128)S(1)} %dynamic-slice_add_fusion.4), channel_id=1, source_target_pairs={{0,8},{1,9},{2,10},{3,11},{4,12},{5,13},{6,14},{7,15},{8,0},{9,1},... | collective-permute-start | bytes 466952 | tf_op jit(solution)/shard_map/ppermute | solution.py:274
  104.6 6.5 %collective-permute-done.18 = f32[152,256]{1,0:T(8,128)S(1)} collective-permute-done((f32[152,256]{1,0:T(8,128)S(1)}, f32[152,256]{1,0:T(8,128)S(1)}, u32[]{:S(2)}, u32[]{:S(2)}) %collective-permute-start.18) | collective-permute-done | bytes 155680 | tf_op jit(solution)/shard_map/ppermute | solution.py:274
  111.2 0.5 collective-permute-start.20
  111.7 1.1 collective-permute-done.21
  112.8 0.1 maximum_select_fusion.3
  112.9 5.3 %collective-permute-done.20 = f32[304,256]{1,0:T(8,128)S(1)} collective-permute-done((f32[304,256]{1,0:T(8,128)S(1)}, f32[304,256]{1,0:T(8,128)S(1)}, u32[]{:S(2)}, u32[]{:S(2)}) %collective-permute-start.20) | collective-permute-done | bytes 311328 | tf_op jit(solution)/shard_map/ppermute | solution.py:274
  118.2 1.4 %collective-permute-start.22 = (f32[608,256]{1,0:T(8,128)S(1)}, f32[608,256]{1,0:T(8,128)S(1)}, u32[]{:S(2)}, u32[]{:S(2)}) collective-permute-start(f32[608,256]{1,0:T(8,128)S(1)} %maximum_select_fusion.4), channel_id=1, source_target_pairs={{0,2},{1,5},{2,0},{3,7},{4,6},{5,1},{6,4},{7,3},{8,10},{9,13},{10,... | collective-permute-start | bytes 1867784 | tf_op jit(solution)/shard_map/ppermute | solution.py:274
  119.6 1.1 collective-permute-start.24
  120.7 7.8 %collective-permute-done.22 = f32[608,256]{1,0:T(8,128)S(1)} collective-permute-done((f32[608,256]{1,0:T(8,128)S(1)}, f32[608,256]{1,0:T(8,128)S(1)}, u32[]{:S(2)}, u32[]{:S(2)}) %collective-permute-start.22) | collective-permute-done | bytes 622624 | tf_op jit(solution)/shard_map/ppermute | solution.py:274
  128.5 0.1 maximum_select_fusion.2
  128.6 0.2 collective-permute-start.23
  128.8 0.1 slice.109
  128.9 1.7 %maximum_select_fusion.1 = f32[2304,256]{1,0:T(8,128)} fusion(f32[1152,256]{1,0:T(8,128)S(1)} %collective-permute-done.24, f32[1152,256]{1,0:T(8,128)S(1)} %maximum_select_fusion.3, pred[]{:T(512)S(6)} %eq.54), kind=kLoop, calls=%fused_computation.1 | loop fusion | flops 1769472 | bytes 4718593 | tf_op jit(solution)/shard_map/jit(_where)/select_n | solution.py:245
  130.6 1.0 collective-permute-done.23
  131.6 0.1 slice.102
  131.7 0.6 multiply_multiply_fusion
  132.3 1.7 %maximum_select_fusion = f32[2304,256]{1,0:T(8,128)} fusion(f32[1088,256]{1,0:T(8,128)S(1)} %slice.102, f32[1216,256]{1,0:T(8,128)S(1)} %maximum_select_fusion.2, f32[1088,256]{1,0:T(8,128)S(1)} %slice.109, f32[1216,256]{1,0:T(8,128)S(1)} %collective-permute-done.23, pred[]{:T(512)S(6)} %eq.54), kind=kLoop, calls=%fused_computation | loop fusion | flops 1769472 | bytes 7077889 | tf_op jit(solution)/shard_map/jit(_where)/select_n | solution.py:248
  (49 shorter events, 0.7 us)
Async XLA Ops:
  0.6 7.5 %copy-start.1 = (bf16[9,256,256]{2,1,0:T(8,128)(2,1)S(1)}, bf16[9,256,256]{2,1,0:T(8,128)(2,1)}, u32[]{:S(2)}) copy-start(bf16[9,256,256]{2,1,0:T(8,128)(2,1)} %weights_ref.8) | copy-start | bytes 3538948
  7.7 5.0 %collective-permute-start = (f32[72,256]{1,0:T(8,128)S(1)}, f32[72,256]{1,0:T(8,128)S(1)}, u32[]{:S(2)}, u32[]{:S(2)}) collective-permute-start(f32[72,256]{1,0:T(8,128)S(1)} %get-tuple-element.46), channel_id=1, source_target_pairs={{0,1},{1,0},{2,3},{3,2},{4,5},{5,4},{6,7},{7,6},{8,9},{9,8},{10,11... | collective-permute-start | bytes 221192 | tf_op jit(solution)/shard_map/ppermute | solution.py:323
  12.7 7.1 %collective-permute-start.1 = (f32[72,256]{1,0:T(8,128)S(1)}, f32[72,256]{1,0:T(8,128)S(1)}, u32[]{:S(2)}, u32[]{:S(2)}) collective-permute-start(f32[72,256]{1,0:T(8,128)S(1)} %pad_maximum_fusion), channel_id=1, source_target_pairs={{0,2},{1,3},{2,0},{3,1},{4,6},{5,7},{6,4},{7,5},{8,10},{9,11},{10,... | collective-permute-start | bytes 221192 | tf_op jit(solution)/shard_map/ppermute | solution.py:323
  19.9 13.6 %copy-start = (f32[256]{0:T(256)S(1)}, f32[256]{0:T(256)}, u32[]{:S(2)}) copy-start(f32[256]{0:T(256)} %param.9) | copy-start | bytes 3076
  19.9 13.6 %copy-start.4 = (f32[64]{0:T(128)S(1)}, f32[64]{0:T(128)}, u32[]{:S(2)}) copy-start(f32[64]{0:T(128)} %step_ref.9) | copy-start | bytes 772
  19.9 4.4 %collective-permute-start.2 = (f32[72,256]{1,0:T(8,128)S(1)}, f32[72,256]{1,0:T(8,128)S(1)}, u32[]{:S(2)}, u32[]{:S(2)}) collective-permute-start(f32[72,256]{1,0:T(8,128)S(1)} %pad_maximum_fusion.1), channel_id=1, source_target_pairs={{0,4},{1,5},{2,6},{3,7},{4,0},{5,1},{6,2},{7,3},{8,12},{9,13},{10,... | collective-permute-start | bytes 221192 | tf_op jit(solution)/shard_map/ppermute | solution.py:323
  21.6 7.4 %collective-permute-start.4 = (f32[72,256]{1,0:T(8,128)S(1)}, f32[72,256]{1,0:T(8,128)S(1)}, u32[]{:S(2)}, u32[]{:S(2)}) collective-permute-start(f32[72,256]{1,0:T(8,128)S(1)} %get-tuple-element.53), channel_id=1, source_target_pairs={{0,1},{1,0},{2,3},{3,2},{4,5},{5,4},{6,7},{7,6},{8,9},{9,8},{10,11... | collective-permute-start | bytes 221192 | tf_op jit(solution)/shard_map/ppermute | solution.py:323
  24.4 6.5 %collective-permute-start.3 = (f32[72,256]{1,0:T(8,128)S(1)}, f32[72,256]{1,0:T(8,128)S(1)}, u32[]{:S(2)}, u32[]{:S(2)}) collective-permute-start(f32[72,256]{1,0:T(8,128)S(1)} %pad_maximum_fusion.2), channel_id=1, source_target_pairs={{0,8},{1,9},{2,10},{3,11},{4,12},{5,13},{6,14},{7,15},{16,24},{17,... | collective-permute-start | bytes 221192 | tf_op jit(solution)/shard_map/ppermute | solution.py:323
  29.0 4.4 %collective-permute-start.5 = (f32[72,256]{1,0:T(8,128)S(1)}, f32[72,256]{1,0:T(8,128)S(1)}, u32[]{:S(2)}, u32[]{:S(2)}) collective-permute-start(f32[72,256]{1,0:T(8,128)S(1)} %pad_maximum_fusion.3), channel_id=1, source_target_pairs={{0,2},{1,3},{2,0},{3,1},{4,6},{5,7},{6,4},{7,5},{8,10},{9,11},{10,... | collective-permute-start | bytes 221192 | tf_op jit(solution)/shard_map/ppermute | solution.py:323
  41.2 8.7 %collective-permute-start.9 = (f32[1152,256]{1,0:T(8,128)S(1)}, f32[1152,256]{1,0:T(8,128)}, u32[]{:S(2)}, u32[]{:S(2)}) collective-permute-start(f32[1152,256]{1,0:T(8,128)S(1)} %get-tuple-element.59), channel_id=1, source_target_pairs={{0,1},{1,0},{2,3},{3,2},{4,5},{5,4},{6,7},{7,6},{8,9},{9,8},{10,11... | collective-permute-start | bytes 3538952 | tf_op jit(solution)/shard_map/ppermute | solution.py:274
  41.2 8.7 %collective-permute-start.8 = (f32[72,256]{1,0:T(8,128)S(1)}, f32[72,256]{1,0:T(8,128)S(1)}, u32[]{:S(2)}, u32[]{:S(2)}) collective-permute-start(f32[72,256]{1,0:T(8,128)S(1)} %pad_maximum_fusion.4), channel_id=1, source_target_pairs={{12,0},{13,1},{14,2},{15,3},{28,16},{29,17},{30,18},{31,19}} | collective-permute-start | bytes 221192 | tf_op jit(solution)/shard_map/ppermute | solution.py:339
  42.5 10.3 %collective-permute-start.7 = (f32[72,256]{1,0:T(8,128)S(1)}, f32[72,256]{1,0:T(8,128)S(1)}, u32[]{:S(2)}, u32[]{:S(2)}) collective-permute-start(f32[72,256]{1,0:T(8,128)S(1)} %pad_maximum_fusion.4), channel_id=1, source_target_pairs={{8,0},{9,1},{10,2},{11,3},{12,4},{13,5},{14,6},{15,7},{24,16},{25,... | collective-permute-start | bytes 221192 | tf_op jit(solution)/shard_map/ppermute | solution.py:339
  43.8 9.0 %collective-permute-start.6 = (f32[72,256]{1,0:T(8,128)S(1)}, f32[72,256]{1,0:T(8,128)S(1)}, u32[]{:S(2)}, u32[]{:S(2)}) collective-permute-start(f32[72,256]{1,0:T(8,128)S(1)} %pad_maximum_fusion.4), channel_id=1, source_target_pairs={{4,0},{5,1},{6,2},{7,3},{8,4},{9,5},{10,6},{11,7},{12,8},{13,9},{1... | collective-permute-start | bytes 221192 | tf_op jit(solution)/shard_map/ppermute | solution.py:339
  51.4 10.2 %collective-permute-start.10 = (f32[576,256]{1,0:T(8,128)S(1)}, f32[576,256]{1,0:T(8,128)S(1)}, u32[]{:S(2)}, u32[]{:S(2)}) collective-permute-start(f32[576,256]{1,0:T(8,128)S(1)} %constant_dynamic-slice_fusion.5), channel_id=1, source_target_pairs={{0,2},{1,5},{2,0},{3,7},{4,6},{5,1},{6,4},{7,3},{8,10},{9,13},{10,... | collective-permute-start | bytes 1769480 | tf_op jit(solution)/shard_map/ppermute | solution.py:274
  61.7 3.1 %collective-permute-start.11 = (f32[1216,256]{1,0:T(8,128)S(1)}, f32[1216,256]{1,0:T(8,128)}, u32[]{:S(2)}, u32[]{:S(2)}) collective-permute-start(f32[1216,256]{1,0:T(8,128)S(1)} %get-tuple-element.70), channel_id=1, source_target_pairs={{0,1},{1,0},{2,3},{3,2},{4,5},{5,4},{6,7},{7,6},{8,9},{9,8},{10,11... | collective-permute-start | bytes 3735560 | tf_op jit(solution)/shard_map/ppermute | solution.py:274
  61.8 11.9 %collective-permute-start.13 = (f32[288,256]{1,0:T(8,128)S(1)}, f32[288,256]{1,0:T(8,128)S(1)}, u32[]{:S(2)}, u32[]{:S(2)}) collective-permute-start(f32[288,256]{1,0:T(8,128)S(1)} %constant_dynamic-slice_fusion.4), channel_id=1, source_target_pairs={{0,4},{1,3},{2,6},{3,1},{4,0},{5,7},{6,2},{7,5},{8,12},{9,11},{10,... | collective-permute-start | bytes 884744 | tf_op jit(solution)/shard_map/ppermute | solution.py:274
  66.3 1.3 copy-start.2
  66.4 10.3 %collective-permute-start.12 = (f32[608,256]{1,0:T(8,128)S(1)}, f32[608,256]{1,0:T(8,128)S(1)}, u32[]{:S(2)}, u32[]{:S(2)}) collective-permute-start(f32[608,256]{1,0:T(8,128)S(1)} %constant_dynamic-slice_fusion.3), channel_id=1, source_target_pairs={{0,2},{1,5},{2,0},{3,7},{4,6},{5,1},{6,4},{7,3},{8,10},{9,13},{10,... | collective-permute-start | bytes 1867784 | tf_op jit(solution)/shard_map/ppermute | solution.py:274
  73.7 10.8 %collective-permute-start.15 = (f32[144,256]{1,0:T(8,128)S(1)}, f32[144,256]{1,0:T(8,128)S(1)}, u32[]{:S(2)}, u32[]{:S(2)}) collective-permute-start(f32[144,256]{1,0:T(8,128)S(1)} %constant_dynamic-slice_fusion.2), channel_id=1, source_target_pairs={{0,8},{1,9},{2,10},{3,11},{4,12},{5,13},{6,14},{7,15},{8,0},{9,1},... | collective-permute-start | bytes 442376 | tf_op jit(solution)/shard_map/ppermute | solution.py:274
  76.8 10.9 %copy-start.3 = (bf16[9,256,256]{2,1,0:T(8,128)(2,1)S(1)}, bf16[9,256,256]{2,1,0:T(8,128)(2,1)}, u32[]{:S(2)}) copy-start(bf16[9,256,256]{2,1,0:T(8,128)(2,1)} %weights_ref.9) | copy-start | bytes 3538948
  76.8 9.2 %collective-permute-start.14 = (f32[304,256]{1,0:T(8,128)S(1)}, f32[304,256]{1,0:T(8,128)S(1)}, u32[]{:S(2)}, u32[]{:S(2)}) collective-permute-start(f32[304,256]{1,0:T(8,128)S(1)} %constant_dynamic-slice_fusion.1), channel_id=1, source_target_pairs={{0,4},{1,3},{2,6},{3,1},{4,0},{5,7},{6,2},{7,5},{8,12},{9,11},{10,... | collective-permute-start | bytes 933896 | tf_op jit(solution)/shard_map/ppermute | solution.py:274
  84.6 11.4 %collective-permute-start.17 = (f32[144,256]{1,0:T(8,128)S(1)}, f32[144,256]{1,0:T(8,128)S(1)}, u32[]{:S(2)}, u32[]{:S(2)}) collective-permute-start(f32[144,256]{1,0:T(8,128)S(1)} %dynamic-slice_add_fusion.5), channel_id=1, source_target_pairs={{0,8},{1,9},{2,10},{3,11},{4,12},{5,13},{6,14},{7,15},{8,0},{9,1},... | collective-permute-start | bytes 442376 | tf_op jit(solution)/shard_map/ppermute | solution.py:274
  86.1 13.1 %collective-permute-start.16 = (f32[152,256]{1,0:T(8,128)S(1)}, f32[152,256]{1,0:T(8,128)S(1)}, u32[]{:S(2)}, u32[]{:S(2)}) collective-permute-start(f32[152,256]{1,0:T(8,128)S(1)} %constant_dynamic-slice_fusion), channel_id=1, source_target_pairs={{0,8},{1,9},{2,10},{3,11},{4,12},{5,13},{6,14},{7,15},{8,0},{9,1},... | collective-permute-start | bytes 466952 | tf_op jit(solution)/shard_map/ppermute | solution.py:274
  96.0 6.8 %collective-permute-start.19 = (f32[288,256]{1,0:T(8,128)S(1)}, f32[288,256]{1,0:T(8,128)S(1)}, u32[]{:S(2)}, u32[]{:S(2)}) collective-permute-start(f32[288,256]{1,0:T(8,128)S(1)} %maximum_select_fusion.7), channel_id=1, source_target_pairs={{0,4},{1,3},{2,6},{3,1},{4,0},{5,7},{6,2},{7,5},{8,12},{9,11},{10,... | collective-permute-start | bytes 884744 | tf_op jit(solution)/shard_map/ppermute | solution.py:274
  102.8 9.9 %collective-permute-start.21 = (f32[576,256]{1,0:T(8,128)S(1)}, f32[576,256]{1,0:T(8,128)S(1)}, u32[]{:S(2)}, u32[]{:S(2)}) collective-permute-start(f32[576,256]{1,0:T(8,128)S(1)} %maximum_select_fusion.5), channel_id=1, source_target_pairs={{0,2},{1,5},{2,0},{3,7},{4,6},{5,1},{6,4},{7,3},{8,10},{9,13},{10,... | collective-permute-start | bytes 1769480 | tf_op jit(solution)/shard_map/ppermute | solution.py:274
  103.3 7.9 %collective-permute-start.18 = (f32[152,256]{1,0:T(8,128)S(1)}, f32[152,256]{1,0:T(8,128)S(1)}, u32[]{:S(2)}, u32[]{:S(2)}) collective-permute-start(f32[152,256]{1,0:T(8,128)S(1)} %dynamic-slice_add_fusion.4), channel_id=1, source_target_pairs={{0,8},{1,9},{2,10},{3,11},{4,12},{5,13},{6,14},{7,15},{8,0},{9,1},... | collective-permute-start | bytes 466952 | tf_op jit(solution)/shard_map/ppermute | solution.py:274
  111.2 7.0 %collective-permute-start.20 = (f32[304,256]{1,0:T(8,128)S(1)}, f32[304,256]{1,0:T(8,128)S(1)}, u32[]{:S(2)}, u32[]{:S(2)}) collective-permute-start(f32[304,256]{1,0:T(8,128)S(1)} %maximum_select_fusion.6), channel_id=1, source_target_pairs={{0,4},{1,3},{2,6},{3,1},{4,0},{5,7},{6,2},{7,5},{8,12},{9,11},{10,... | collective-permute-start | bytes 933896 | tf_op jit(solution)/shard_map/ppermute | solution.py:274
  118.2 10.3 %collective-permute-start.22 = (f32[608,256]{1,0:T(8,128)S(1)}, f32[608,256]{1,0:T(8,128)S(1)}, u32[]{:S(2)}, u32[]{:S(2)}) collective-permute-start(f32[608,256]{1,0:T(8,128)S(1)} %maximum_select_fusion.4), channel_id=1, source_target_pairs={{0,2},{1,5},{2,0},{3,7},{4,6},{5,1},{6,4},{7,3},{8,10},{9,13},{10,... | collective-permute-start | bytes 1867784 | tf_op jit(solution)/shard_map/ppermute | solution.py:274
  119.6 9.3 %collective-permute-start.24 = (f32[1152,256]{1,0:T(8,128)S(1)}, f32[1152,256]{1,0:T(8,128)S(1)}, u32[]{:S(2)}, u32[]{:S(2)}) collective-permute-start(f32[1152,256]{1,0:T(8,128)S(1)} %maximum_select_fusion.3), channel_id=1, source_target_pairs={{0,1},{1,0},{2,3},{3,2},{4,5},{5,4},{6,7},{7,6},{8,9},{9,8},{10,11... | collective-permute-start | bytes 3538952 | tf_op jit(solution)/shard_map/ppermute | solution.py:274
  128.6 3.0 %collective-permute-start.23 = (f32[1216,256]{1,0:T(8,128)S(1)}, f32[1216,256]{1,0:T(8,128)S(1)}, u32[]{:S(2)}, u32[]{:S(2)}) collective-permute-start(f32[1216,256]{1,0:T(8,128)S(1)} %maximum_select_fusion.2), channel_id=1, source_target_pairs={{0,1},{1,0},{2,3},{3,2},{4,5},{5,4},{6,7},{7,6},{8,9},{9,8},{10,11... | collective-permute-start | bytes 3735560 | tf_op jit(solution)/shard_map/ppermute | solution.py:274

commit v5 on v4

--- a/solution.py
+++ b/solution.py
@@ -10,7 +10,7 @@
 
 F32 = jnp.float32
 BF16 = jnp.bfloat16
-VMEM_LIMIT = 20 * 1024 * 1024
+VMEM_LIMIT = 36 * 1024 * 1024
 
 
 def column_shifts(value):
@@ -364,7 +364,7 @@
     me = lax.axis_index("tm")
     bits = bits_of(me, levels)
     factor = 1.0 / math.sqrt(frames * count * height * breadth)
-    block = 16
+    block = 32
     steps = frames // block
     grid = (steps,)
     rate = decay_rate.reshape(1, channels)

time: 135 us -> 133 us (0.985)
  waiting for transfers between devices: 51.6 us -> 49.8 us
  starting transfers between devices: 27.8 us -> 29.3 us
    ppermute x16, waiting for transfers between devices: 39.6 us -> 37.8 us  [swap(): lax.ppermute(value, 'tm', [(source, source ^ 1 << levels[source & 1]) for...]
    ppermute x16, starting transfers between devices: 14 us -> 15.5 us  [swap(): lax.ppermute(value, 'tm', [(source, source ^ 1 << levels[source & 1]) for...]
where the time goes in v5:
time: 133 us
  waiting for transfers between devices  49.8 us (37%)
  Pallas kernels  44 us (33%)
  starting transfers between devices  29.3 us (22%)
  other arithmetic  7.71 us (6%)
    ppermute x16, waiting for transfers between devices, swap(): lax.ppermute(value, 'tm', [(source, source ^ 1 << levels[source & 1]) for...  37.8 us
    pallas_call x3, Pallas kernels, drive(): call(functools.partial(drive_kernel, reverse, base, start is None), (size...  15.6 us
    ppermute x16, starting transfers between devices, swap(): lax.ppermute(value, 'tm', [(source, source ^ 1 << levels[source & 1]) for...  15.5 us
    pallas_call x2, Pallas kernels, conv(): call(functools.partial(conv_kernel, reverse), (size,), specs, framed(shap...  12 us
    ppermute x6, starting transfers between devices, start(): self.other = lax.ppermute(self.message, 'tm', pairs)  9.77 us
    pallas_call x1, Pallas kernels, body(): call(functools.partial(adjoint_kernel, factor, steps - later), grid, [sme...  9.08 us
    pallas_call x1, Pallas kernels, body(): call(functools.partial(state_kernel, factor), grid, [smem(), smem(), fixe...  7.35 us
    ppermute x6, waiting for transfers between devices, start(): self.other = lax.ppermute(self.message, 'tm', pairs)  6.63 us
  transfers between devices with their start and end apart: 25, of which 17 were waited for; matrix products, arithmetic and copies ran while one was open for 4% of the time, Pallas kernels for 23%

profile of v5, /device:TPU:0, one launch (start us, length us, event | category | flops | bytes accessed | tf_op | source)
XLA Modules:
  0.0 132.6 jit_solution(3968346233122171106)
XLA Ops:
  0.6 0.0 copy-start.1
  0.6 6.7 %drive.1 = (f32[64,2,32,256]{3,2,1,0:T(8,128)}, f32[72,256]{1,0:T(8,128)S(1)}) custom-call(f32[64]{0:T(128)} %step_ref.9, f32[1,256]{1,0:T(1,128)} %bitcast.110, bf16[64,2,32,256]{3,2,1,0:T(8,128)(2,1)} %latents_ref.1, bf16[9,256,256]{2,1,0:T(8,128)(2,1)} %weights_ref.9), custom_call_target="tpu_custom_call" | custom-call | flops 3221225472 | bytes 6291456 | tf_op jit(solution)/shard_map/drive/pallas_call | solution.py:388
  7.4 0.5 collective-permute-start
  7.8 4.5 %pull.2 = (f32[32,2,32,256]{3,2,1,0:T(8,128)}, f32[72,256]{1,0:T(8,128)S(1)}) custom-call(f32[64]{0:T(128)} %step_ref.9, f32[1,256]{1,0:T(1,128)} %bitcast.111, bf16[64,2,32,256]{3,2,1,0:T(8,128)(2,1)} %cotangent_ref.1, bf16[9,256,256]{2,1,0:T(8,128)(2,1)S(1)} %copy-done.1), custom_call_target="tpu_custom_call" | custom-call | flops 1610612736 | bytes 3145728 | tf_op jit(solution)/shard_map/pull/pallas_call | solution.py:388
  12.3 2.6 %collective-permute-start.1 = (f32[72,256]{1,0:T(8,128)S(1)}, f32[72,256]{1,0:T(8,128)S(1)}, u32[]{:S(2)}, u32[]{:S(2)}) collective-permute-start(f32[72,256]{1,0:T(8,128)S(1)} %pad_maximum_fusion), channel_id=1, source_target_pairs={{0,2},{1,3},{2,0},{3,1},{4,6},{5,7},{6,4},{7,5},{8,10},{9,11},{10,... | collective-permute-start | bytes 221192 | tf_op jit(solution)/shard_map/ppermute | solution.py:323
  14.9 4.5 %pull.3 = (f32[32,2,32,256]{3,2,1,0:T(8,128)}, f32[72,256]{1,0:T(8,128)S(1)}) custom-call(f32[64]{0:T(128)} %step_ref.9, f32[1,256]{1,0:T(1,128)} %bitcast.112, bf16[64,2,32,256]{3,2,1,0:T(8,128)(2,1)} %cotangent_ref.1, bf16[9,256,256]{2,1,0:T(8,128)(2,1)S(1)} %copy-done.1, f32[72,256]{1,0:T(8,128)S(1)} %get-tuple-element.50.refs_0_), custom_call_target="tpu_custom_call" | custom-call | flops 1610612736 | bytes 3145728 | tf_op jit(solution)/shard_map/pull/pallas_call | solution.py:388
  19.4 0.0 collective-permute-done.1
  19.4 1.6 %collective-permute-start.2 = (f32[72,256]{1,0:T(8,128)S(1)}, f32[72,256]{1,0:T(8,128)S(1)}, u32[]{:S(2)}, u32[]{:S(2)}) collective-permute-start(f32[72,256]{1,0:T(8,128)S(1)} %pad_maximum_fusion.1), channel_id=1, source_target_pairs={{0,4},{1,5},{2,6},{3,7},{4,0},{5,1},{6,2},{7,3},{8,12},{9,13},{10,... | collective-permute-start | bytes 221192 | tf_op jit(solution)/shard_map/ppermute | solution.py:323
  21.1 2.8 %collective-permute-done.2 = f32[72,256]{1,0:T(8,128)S(1)} collective-permute-done((f32[72,256]{1,0:T(8,128)S(1)}, f32[72,256]{1,0:T(8,128)S(1)}, u32[]{:S(2)}, u32[]{:S(2)}) %collective-permute-start.2) | collective-permute-done | bytes 73760 | tf_op jit(solution)/shard_map/ppermute | solution.py:323
  23.9 4.5 %collective-permute-start.3 = (f32[72,256]{1,0:T(8,128)S(1)}, f32[72,256]{1,0:T(8,128)S(1)}, u32[]{:S(2)}, u32[]{:S(2)}) collective-permute-start(f32[72,256]{1,0:T(8,128)S(1)} %pad_maximum_fusion.2), channel_id=1, source_target_pairs={{0,8},{1,9},{2,10},{3,11},{4,12},{5,13},{6,14},{7,15},{16,24},{17,... | collective-permute-start | bytes 221192 | tf_op jit(solution)/shard_map/ppermute | solution.py:323
  28.5 0.6 collective-permute-start.5
  29.1 1.3 collective-permute-done.3
  30.4 2.5 %collective-permute-done.5 = f32[72,256]{1,0:T(8,128)S(1)} collective-permute-done((f32[72,256]{1,0:T(8,128)S(1)}, f32[72,256]{1,0:T(8,128)S(1)}, u32[]{:S(2)}, u32[]{:S(2)}) %collective-permute-start.5) | collective-permute-done | bytes 73760 | tf_op jit(solution)/shard_map/ppermute | solution.py:323
  33.0 7.4 %states.1 = (bf16[64,2,32,256]{3,2,1,0:T(8,128)(2,1)}, f32[1152,256]{1,0:T(8,128)S(1)}, f32[1152,256]{1,0:T(8,128)S(1)}) custom-call(f32[64]{0:T(128)S(1)} %copy-done.4, s32[1]{0:T(128)} %bitcast.core_ref, f32[1,256]{1,0:T(1,128)S(1)} %bitcast.113, f32[64,256]{1,0:T(8,128)S(1)} %add_select_fusion.1.incoming_ref, ...), custom_call_target="tpu_custom_call" | custom-call | flops 3221225472 | bytes 8388608 | tf_op jit(solution)/shard_map/states/pallas_call | solution.py:431
  40.3 1.3 collective-permute-start.8
  41.6 1.3 collective-permute-start.7
  42.9 1.5 %collective-permute-start.6 = (f32[72,256]{1,0:T(8,128)S(1)}, f32[72,256]{1,0:T(8,128)S(1)}, u32[]{:S(2)}, u32[]{:S(2)}) collective-permute-start(f32[72,256]{1,0:T(8,128)S(1)} %pad_maximum_fusion.4), channel_id=1, source_target_pairs={{4,0},{5,1},{6,2},{7,3},{8,4},{9,5},{10,6},{11,7},{12,8},{13,9},{1... | collective-permute-start | bytes 221192 | tf_op jit(solution)/shard_map/ppermute | solution.py:339
  44.4 4.7 %collective-permute-done.8 = f32[72,256]{1,0:T(8,128)S(1)} collective-permute-done((f32[72,256]{1,0:T(8,128)S(1)}, f32[72,256]{1,0:T(8,128)S(1)}, u32[]{:S(2)}, u32[]{:S(2)}) %collective-permute-start.8) | collective-permute-done | bytes 73760 | tf_op jit(solution)/shard_map/ppermute | solution.py:339
  49.1 1.4 %add.158 = f32[1152,256]{1,0:T(8,128)S(1)} add(f32[1152,256]{1,0:T(8,128)S(1)} %get-tuple-element.63, f32[1152,256]{1,0:T(8,128)} %collective-permute-done.9) | non-fusion elementwise | flops 294912 | bytes 3538944 | tf_op jit(solution)/shard_map/add | solution.py:283
  50.6 0.6 collective-permute-start.10
  51.1 0.8 collective-permute-done.7
  52.0 9.1 %adjoint.1 = (bf16[64,2,32,256]{3,2,1,0:T(8,128)(2,1)}, f32[1216,256]{1,0:T(8,128)S(1)}, f32[1216,256]{1,0:T(8,128)S(1)}) custom-call(f32[64]{0:T(128)S(1)} %copy-done.4, s32[1]{0:T(128)} %bitcast.core_ref, f32[1,256]{1,0:T(1,128)S(1)} %bitcast.114, f32[64,256]{1,0:T(8,128)S(1)} %fusion.arriving_ref, f32[64,256]{1,0:T(8,128)S(1)} %add_select_fusion.1.incoming_ref, ...), custom_call_target="tpu_custom_call" | custom-call | flops 3221225472 | bytes 10485760 | tf_op jit(solution)/shard_map/adjoint/pallas_call | solution.py:478
  61.0 0.1 dynamic-slice_add_fusion.1
  61.2 0.1 collective-permute-start.11
  61.3 2.2 %collective-permute-start.13 = (f32[288,256]{1,0:T(8,128)S(1)}, f32[288,256]{1,0:T(8,128)S(1)}, u32[]{:S(2)}, u32[]{:S(2)}) collective-permute-start(f32[288,256]{1,0:T(8,128)S(1)} %constant_dynamic-slice_fusion.4), channel_id=1, source_target_pairs={{0,4},{1,3},{2,6},{3,1},{4,0},{5,7},{6,2},{7,5},{8,12},{9,11},{10,... | collective-permute-start | bytes 884744 | tf_op jit(solution)/shard_map/ppermute | solution.py:274
  63.4 0.9 collective-permute-done.11
  64.3 1.5 %add.163 = f32[1216,256]{1,0:T(8,128)S(1)} add(f32[1216,256]{1,0:T(8,128)S(1)} %get-tuple-element.67, f32[1216,256]{1,0:T(8,128)} %collective-permute-done.11) | non-fusion elementwise | flops 311296 | bytes 3735552 | tf_op jit(solution)/shard_map/add | solution.py:283
  65.8 0.0 copy-start.2
  65.8 0.1 constant_dynamic-slice_fusion.3
  65.8 0.8 collective-permute-start.12
  66.7 0.4 copy-done.2
  67.0 5.8 %conv.2 = bf16[64,2,32,256]{3,2,1,0:T(8,128)(2,1)} custom-call(bf16[64,2,32,256]{3,2,1,0:T(8,128)(2,1)} %get-tuple-element.72.states_ref.previous_ref.value_ref, bf16[9,256,256]{2,1,0:T(8,128)(2,1)S(1)} %copy-done.2), custom_call_target="tpu_custom_call" | custom-call | flops 3221225472 | bytes 4194304 | tf_op jit(solution)/shard_map/conv/pallas_call | solution.py:458
  72.9 1.2 collective-permute-start.15
  74.1 2.0 %collective-permute-done.12 = f32[608,256]{1,0:T(8,128)S(1)} collective-permute-done((f32[608,256]{1,0:T(8,128)S(1)}, f32[608,256]{1,0:T(8,128)S(1)}, u32[]{:S(2)}, u32[]{:S(2)}) %collective-permute-start.12) | collective-permute-done | bytes 622624 | tf_op jit(solution)/shard_map/ppermute | solution.py:274
  76.1 0.1 dynamic-slice_add_fusion
  76.2 0.0 copy-start.3
  76.3 2.2 %collective-permute-start.14 = (f32[304,256]{1,0:T(8,128)S(1)}, f32[304,256]{1,0:T(8,128)S(1)}, u32[]{:S(2)}, u32[]{:S(2)}) collective-permute-start(f32[304,256]{1,0:T(8,128)S(1)} %constant_dynamic-slice_fusion.1), channel_id=1, source_target_pairs={{0,4},{1,3},{2,6},{3,1},{4,0},{5,7},{6,2},{7,5},{8,12},{9,11},{10,... | collective-permute-start | bytes 933896 | tf_op jit(solution)/shard_map/ppermute | solution.py:274
  78.4 5.3 %collective-permute-done.15 = f32[144,256]{1,0:T(8,128)S(1)} collective-permute-done((f32[144,256]{1,0:T(8,128)S(1)}, f32[144,256]{1,0:T(8,128)S(1)}, u32[]{:S(2)}, u32[]{:S(2)}) %collective-permute-start.15) | collective-permute-done | bytes 147488 | tf_op jit(solution)/shard_map/ppermute | solution.py:274
  83.7 0.1 collective-permute-start.17
  83.8 1.7 %collective-permute-done.14 = f32[304,256]{1,0:T(8,128)S(1)} collective-permute-done((f32[304,256]{1,0:T(8,128)S(1)}, f32[304,256]{1,0:T(8,128)S(1)}, u32[]{:S(2)}, u32[]{:S(2)}) %collective-permute-start.14) | collective-permute-done | bytes 311328 | tf_op jit(solution)/shard_map/ppermute | solution.py:274
  85.6 1.3 collective-permute-start.16
  86.9 6.2 %conv.3 = bf16[64,2,32,256]{3,2,1,0:T(8,128)(2,1)} custom-call(bf16[64,2,32,256]{3,2,1,0:T(8,128)(2,1)} %get-tuple-element.78.value_ref, bf16[9,256,256]{2,1,0:T(8,128)(2,1)S(1)} %copy-done.3), custom_call_target="tpu_custom_call" | custom-call | flops 3221225472 | bytes 4194304 | tf_op jit(solution)/shard_map/conv/pallas_call | solution.py:458
  93.0 2.1 %collective-permute-done.17 = f32[144,256]{1,0:T(8,128)S(1)} collective-permute-done((f32[144,256]{1,0:T(8,128)S(1)}, f32[144,256]{1,0:T(8,128)S(1)}, u32[]{:S(2)}, u32[]{:S(2)}) %collective-permute-start.17) | collective-permute-done | bytes 147488 | tf_op jit(solution)/shard_map/ppermute | solution.py:274
  95.1 0.3 collective-permute-start.19
  95.5 2.9 %collective-permute-done.16 = f32[152,256]{1,0:T(8,128)S(1)} collective-permute-done((f32[152,256]{1,0:T(8,128)S(1)}, f32[152,256]{1,0:T(8,128)S(1)}, u32[]{:S(2)}, u32[]{:S(2)}) %collective-permute-start.16) | collective-permute-done | bytes 155680 | tf_op jit(solution)/shard_map/ppermute | solution.py:274
  98.4 3.6 %collective-permute-done.19 = f32[288,256]{1,0:T(8,128)S(1)} collective-permute-done((f32[288,256]{1,0:T(8,128)S(1)}, f32[288,256]{1,0:T(8,128)S(1)}, u32[]{:S(2)}, u32[]{:S(2)}) %collective-permute-start.19) | collective-permute-done | bytes 294944 | tf_op jit(solution)/shard_map/ppermute | solution.py:274
  102.0 0.2 collective-permute-start.21
  102.2 1.7 %collective-permute-start.18 = (f32[152,256]{1,0:T(8,128)S(1)}, f32[152,256]{1,0:T(8,128)S(1)}, u32[]{:S(2)}, u32[]{:S(2)}) collective-permute-start(f32[152,256]{1,0:T(8,128)S(1)} %dynamic-slice_add_fusion.4), channel_id=1, source_target_pairs={{0,8},{1,9},{2,10},{3,11},{4,12},{5,13},{6,14},{7,15},{8,0},{9,1},... | collective-permute-start | bytes 466952 | tf_op jit(solution)/shard_map/ppermute | solution.py:274
  103.9 5.8 %collective-permute-done.18 = f32[152,256]{1,0:T(8,128)S(1)} collective-permute-done((f32[152,256]{1,0:T(8,128)S(1)}, f32[152,256]{1,0:T(8,128)S(1)}, u32[]{:S(2)}, u32[]{:S(2)}) %collective-permute-start.18) | collective-permute-done | bytes 155680 | tf_op jit(solution)/shard_map/ppermute | solution.py:274
  109.7 1.3 collective-permute-start.20
  110.9 1.0 collective-permute-done.21
  111.9 0.1 maximum_select_fusion.3
  112.0 4.7 %collective-permute-done.20 = f32[304,256]{1,0:T(8,128)S(1)} collective-permute-done((f32[304,256]{1,0:T(8,128)S(1)}, f32[304,256]{1,0:T(8,128)S(1)}, u32[]{:S(2)}, u32[]{:S(2)}) %collective-permute-start.20) | collective-permute-done | bytes 311328 | tf_op jit(solution)/shard_map/ppermute | solution.py:274
  116.7 2.0 %collective-permute-start.22 = (f32[608,256]{1,0:T(8,128)S(1)}, f32[608,256]{1,0:T(8,128)S(1)}, u32[]{:S(2)}, u32[]{:S(2)}) collective-permute-start(f32[608,256]{1,0:T(8,128)S(1)} %maximum_select_fusion.4), channel_id=1, source_target_pairs={{0,2},{1,5},{2,0},{3,7},{4,6},{5,1},{6,4},{7,3},{8,10},{9,13},{10,... | collective-permute-start | bytes 1867784 | tf_op jit(solution)/shard_map/ppermute | solution.py:274
  118.7 1.1 collective-permute-start.24
  119.9 7.2 %collective-permute-done.22 = f32[608,256]{1,0:T(8,128)S(1)} collective-permute-done((f32[608,256]{1,0:T(8,128)S(1)}, f32[608,256]{1,0:T(8,128)S(1)}, u32[]{:S(2)}, u32[]{:S(2)}) %collective-permute-start.22) | collective-permute-done | bytes 622624 | tf_op jit(solution)/shard_map/ppermute | solution.py:274
  127.0 0.1 maximum_select_fusion.2
  127.2 0.5 collective-permute-start.23
  127.7 0.1 slice.109
  127.8 1.7 %maximum_select_fusion.1 = f32[2304,256]{1,0:T(8,128)} fusion(f32[1152,256]{1,0:T(8,128)S(1)} %collective-permute-done.24, f32[1152,256]{1,0:T(8,128)S(1)} %maximum_select_fusion.3, pred[]{:T(512)S(6)} %eq.54), kind=kLoop, calls=%fused_computation.1 | loop fusion | flops 1769472 | bytes 4718593 | tf_op jit(solution)/shard_map/jit(_where)/select_n | solution.py:245
  129.5 0.8 collective-permute-done.23
  130.3 0.1 slice.102
  130.3 0.6 multiply_multiply_fusion
  130.9 1.7 %maximum_select_fusion = f32[2304,256]{1,0:T(8,128)} fusion(f32[1088,256]{1,0:T(8,128)S(1)} %slice.102, f32[1216,256]{1,0:T(8,128)S(1)} %maximum_select_fusion.2, f32[1088,256]{1,0:T(8,128)S(1)} %slice.109, f32[1216,256]{1,0:T(8,128)S(1)} %collective-permute-done.23, pred[]{:T(512)S(6)} %eq.54), kind=kLoop, calls=%fused_computation | loop fusion | flops 1769472 | bytes 7077889 | tf_op jit(solution)/shard_map/jit(_where)/select_n | solution.py:248
  (49 shorter events, 0.7 us)
Async XLA Ops:
  0.6 7.2 %copy-start.1 = (bf16[9,256,256]{2,1,0:T(8,128)(2,1)S(1)}, bf16[9,256,256]{2,1,0:T(8,128)(2,1)}, u32[]{:S(2)}) copy-start(bf16[9,256,256]{2,1,0:T(8,128)(2,1)} %weights_ref.8) | copy-start | bytes 3538948
  7.4 4.9 %collective-permute-start = (f32[72,256]{1,0:T(8,128)S(1)}, f32[72,256]{1,0:T(8,128)S(1)}, u32[]{:S(2)}, u32[]{:S(2)}) collective-permute-start(f32[72,256]{1,0:T(8,128)S(1)} %get-tuple-element.46), channel_id=1, source_target_pairs={{0,1},{1,0},{2,3},{3,2},{4,5},{5,4},{6,7},{7,6},{8,9},{9,8},{10,11... | collective-permute-start | bytes 221192 | tf_op jit(solution)/shard_map/ppermute | solution.py:323
  12.3 7.1 %collective-permute-start.1 = (f32[72,256]{1,0:T(8,128)S(1)}, f32[72,256]{1,0:T(8,128)S(1)}, u32[]{:S(2)}, u32[]{:S(2)}) collective-permute-start(f32[72,256]{1,0:T(8,128)S(1)} %pad_maximum_fusion), channel_id=1, source_target_pairs={{0,2},{1,3},{2,0},{3,1},{4,6},{5,7},{6,4},{7,5},{8,10},{9,11},{10,... | collective-permute-start | bytes 221192 | tf_op jit(solution)/shard_map/ppermute | solution.py:323
  19.4 13.6 %copy-start = (f32[256]{0:T(256)S(1)}, f32[256]{0:T(256)}, u32[]{:S(2)}) copy-start(f32[256]{0:T(256)} %param.9) | copy-start | bytes 3076
  19.4 13.6 %copy-start.4 = (f32[64]{0:T(128)S(1)}, f32[64]{0:T(128)}, u32[]{:S(2)}) copy-start(f32[64]{0:T(128)} %step_ref.9) | copy-start | bytes 772
  19.4 4.5 %collective-permute-start.2 = (f32[72,256]{1,0:T(8,128)S(1)}, f32[72,256]{1,0:T(8,128)S(1)}, u32[]{:S(2)}, u32[]{:S(2)}) collective-permute-start(f32[72,256]{1,0:T(8,128)S(1)} %pad_maximum_fusion.1), channel_id=1, source_target_pairs={{0,4},{1,5},{2,6},{3,7},{4,0},{5,1},{6,2},{7,3},{8,12},{9,13},{10,... | collective-permute-start | bytes 221192 | tf_op jit(solution)/shard_map/ppermute | solution.py:323
  21.1 7.4 %collective-permute-start.4 = (f32[72,256]{1,0:T(8,128)S(1)}, f32[72,256]{1,0:T(8,128)S(1)}, u32[]{:S(2)}, u32[]{:S(2)}) collective-permute-start(f32[72,256]{1,0:T(8,128)S(1)} %get-tuple-element.53), channel_id=1, source_target_pairs={{0,1},{1,0},{2,3},{3,2},{4,5},{5,4},{6,7},{7,6},{8,9},{9,8},{10,11... | collective-permute-start | bytes 221192 | tf_op jit(solution)/shard_map/ppermute | solution.py:323
  23.9 6.5 %collective-permute-start.3 = (f32[72,256]{1,0:T(8,128)S(1)}, f32[72,256]{1,0:T(8,128)S(1)}, u32[]{:S(2)}, u32[]{:S(2)}) collective-permute-start(f32[72,256]{1,0:T(8,128)S(1)} %pad_maximum_fusion.2), channel_id=1, source_target_pairs={{0,8},{1,9},{2,10},{3,11},{4,12},{5,13},{6,14},{7,15},{16,24},{17,... | collective-permute-start | bytes 221192 | tf_op jit(solution)/shard_map/ppermute | solution.py:323
  28.5 4.4 %collective-permute-start.5 = (f32[72,256]{1,0:T(8,128)S(1)}, f32[72,256]{1,0:T(8,128)S(1)}, u32[]{:S(2)}, u32[]{:S(2)}) collective-permute-start(f32[72,256]{1,0:T(8,128)S(1)} %pad_maximum_fusion.3), channel_id=1, source_target_pairs={{0,2},{1,3},{2,0},{3,1},{4,6},{5,7},{6,4},{7,5},{8,10},{9,11},{10,... | collective-permute-start | bytes 221192 | tf_op jit(solution)/shard_map/ppermute | solution.py:323
  40.3 8.7 %collective-permute-start.9 = (f32[1152,256]{1,0:T(8,128)S(1)}, f32[1152,256]{1,0:T(8,128)}, u32[]{:S(2)}, u32[]{:S(2)}) collective-permute-start(f32[1152,256]{1,0:T(8,128)S(1)} %get-tuple-element.59), channel_id=1, source_target_pairs={{0,1},{1,0},{2,3},{3,2},{4,5},{5,4},{6,7},{7,6},{8,9},{9,8},{10,11... | collective-permute-start | bytes 3538952 | tf_op jit(solution)/shard_map/ppermute | solution.py:274
  40.3 8.7 %collective-permute-start.8 = (f32[72,256]{1,0:T(8,128)S(1)}, f32[72,256]{1,0:T(8,128)S(1)}, u32[]{:S(2)}, u32[]{:S(2)}) collective-permute-start(f32[72,256]{1,0:T(8,128)S(1)} %pad_maximum_fusion.4), channel_id=1, source_target_pairs={{12,0},{13,1},{14,2},{15,3},{28,16},{29,17},{30,18},{31,19}} | collective-permute-start | bytes 221192 | tf_op jit(solution)/shard_map/ppermute | solution.py:339
  41.6 10.3 %collective-permute-start.7 = (f32[72,256]{1,0:T(8,128)S(1)}, f32[72,256]{1,0:T(8,128)S(1)}, u32[]{:S(2)}, u32[]{:S(2)}) collective-permute-start(f32[72,256]{1,0:T(8,128)S(1)} %pad_maximum_fusion.4), channel_id=1, source_target_pairs={{8,0},{9,1},{10,2},{11,3},{12,4},{13,5},{14,6},{15,7},{24,16},{25,... | collective-permute-start | bytes 221192 | tf_op jit(solution)/shard_map/ppermute | solution.py:339
  42.9 9.0 %collective-permute-start.6 = (f32[72,256]{1,0:T(8,128)S(1)}, f32[72,256]{1,0:T(8,128)S(1)}, u32[]{:S(2)}, u32[]{:S(2)}) collective-permute-start(f32[72,256]{1,0:T(8,128)S(1)} %pad_maximum_fusion.4), channel_id=1, source_target_pairs={{4,0},{5,1},{6,2},{7,3},{8,4},{9,5},{10,6},{11,7},{12,8},{13,9},{1... | collective-permute-start | bytes 221192 | tf_op jit(solution)/shard_map/ppermute | solution.py:339
  50.6 10.5 %collective-permute-start.10 = (f32[576,256]{1,0:T(8,128)S(1)}, f32[576,256]{1,0:T(8,128)S(1)}, u32[]{:S(2)}, u32[]{:S(2)}) collective-permute-start(f32[576,256]{1,0:T(8,128)S(1)} %constant_dynamic-slice_fusion.5), channel_id=1, source_target_pairs={{0,2},{1,5},{2,0},{3,7},{4,6},{5,1},{6,4},{7,3},{8,10},{9,13},{10,... | collective-permute-start | bytes 1769480 | tf_op jit(solution)/shard_map/ppermute | solution.py:274
  61.2 3.1 %collective-permute-start.11 = (f32[1216,256]{1,0:T(8,128)S(1)}, f32[1216,256]{1,0:T(8,128)}, u32[]{:S(2)}, u32[]{:S(2)}) collective-permute-start(f32[1216,256]{1,0:T(8,128)S(1)} %get-tuple-element.70), channel_id=1, source_target_pairs={{0,1},{1,0},{2,3},{3,2},{4,5},{5,4},{6,7},{7,6},{8,9},{9,8},{10,11... | collective-permute-start | bytes 3735560 | tf_op jit(solution)/shard_map/ppermute | solution.py:274
  61.3 11.6 %collective-permute-start.13 = (f32[288,256]{1,0:T(8,128)S(1)}, f32[288,256]{1,0:T(8,128)S(1)}, u32[]{:S(2)}, u32[]{:S(2)}) collective-permute-start(f32[288,256]{1,0:T(8,128)S(1)} %constant_dynamic-slice_fusion.4), channel_id=1, source_target_pairs={{0,4},{1,3},{2,6},{3,1},{4,0},{5,7},{6,2},{7,5},{8,12},{9,11},{10,... | collective-permute-start | bytes 884744 | tf_op jit(solution)/shard_map/ppermute | solution.py:274
  65.8 1.3 copy-start.2
  65.8 10.3 %collective-permute-start.12 = (f32[608,256]{1,0:T(8,128)S(1)}, f32[608,256]{1,0:T(8,128)S(1)}, u32[]{:S(2)}, u32[]{:S(2)}) collective-permute-start(f32[608,256]{1,0:T(8,128)S(1)} %constant_dynamic-slice_fusion.3), channel_id=1, source_target_pairs={{0,2},{1,5},{2,0},{3,7},{4,6},{5,1},{6,4},{7,3},{8,10},{9,13},{10,... | collective-permute-start | bytes 1867784 | tf_op jit(solution)/shard_map/ppermute | solution.py:274
  72.9 10.8 %collective-permute-start.15 = (f32[144,256]{1,0:T(8,128)S(1)}, f32[144,256]{1,0:T(8,128)S(1)}, u32[]{:S(2)}, u32[]{:S(2)}) collective-permute-start(f32[144,256]{1,0:T(8,128)S(1)} %constant_dynamic-slice_fusion.2), channel_id=1, source_target_pairs={{0,8},{1,9},{2,10},{3,11},{4,12},{5,13},{6,14},{7,15},{8,0},{9,1},... | collective-permute-start | bytes 442376 | tf_op jit(solution)/shard_map/ppermute | solution.py:274
  76.2 10.7 %copy-start.3 = (bf16[9,256,256]{2,1,0:T(8,128)(2,1)S(1)}, bf16[9,256,256]{2,1,0:T(8,128)(2,1)}, u32[]{:S(2)}) copy-start(bf16[9,256,256]{2,1,0:T(8,128)(2,1)} %weights_ref.9) | copy-start | bytes 3538948
  76.3 9.3 %collective-permute-start.14 = (f32[304,256]{1,0:T(8,128)S(1)}, f32[304,256]{1,0:T(8,128)S(1)}, u32[]{:S(2)}, u32[]{:S(2)}) collective-permute-start(f32[304,256]{1,0:T(8,128)S(1)} %constant_dynamic-slice_fusion.1), channel_id=1, source_target_pairs={{0,4},{1,3},{2,6},{3,1},{4,0},{5,7},{6,2},{7,5},{8,12},{9,11},{10,... | collective-permute-start | bytes 933896 | tf_op jit(solution)/shard_map/ppermute | solution.py:274
  83.7 11.4 %collective-permute-start.17 = (f32[144,256]{1,0:T(8,128)S(1)}, f32[144,256]{1,0:T(8,128)S(1)}, u32[]{:S(2)}, u32[]{:S(2)}) collective-permute-start(f32[144,256]{1,0:T(8,128)S(1)} %dynamic-slice_add_fusion.5), channel_id=1, source_target_pairs={{0,8},{1,9},{2,10},{3,11},{4,12},{5,13},{6,14},{7,15},{8,0},{9,1},... | collective-permute-start | bytes 442376 | tf_op jit(solution)/shard_map/ppermute | solution.py:274
  85.6 12.8 %collective-permute-start.16 = (f32[152,256]{1,0:T(8,128)S(1)}, f32[152,256]{1,0:T(8,128)S(1)}, u32[]{:S(2)}, u32[]{:S(2)}) collective-permute-start(f32[152,256]{1,0:T(8,128)S(1)} %constant_dynamic-slice_fusion), channel_id=1, source_target_pairs={{0,8},{1,9},{2,10},{3,11},{4,12},{5,13},{6,14},{7,15},{8,0},{9,1},... | collective-permute-start | bytes 466952 | tf_op jit(solution)/shard_map/ppermute | solution.py:274
  95.1 6.8 %collective-permute-start.19 = (f32[288,256]{1,0:T(8,128)S(1)}, f32[288,256]{1,0:T(8,128)S(1)}, u32[]{:S(2)}, u32[]{:S(2)}) collective-permute-start(f32[288,256]{1,0:T(8,128)S(1)} %maximum_select_fusion.7), channel_id=1, source_target_pairs={{0,4},{1,3},{2,6},{3,1},{4,0},{5,7},{6,2},{7,5},{8,12},{9,11},{10,... | collective-permute-start | bytes 884744 | tf_op jit(solution)/shard_map/ppermute | solution.py:274
  102.0 9.9 %collective-permute-start.21 = (f32[576,256]{1,0:T(8,128)S(1)}, f32[576,256]{1,0:T(8,128)S(1)}, u32[]{:S(2)}, u32[]{:S(2)}) collective-permute-start(f32[576,256]{1,0:T(8,128)S(1)} %maximum_select_fusion.5), channel_id=1, source_target_pairs={{0,2},{1,5},{2,0},{3,7},{4,6},{5,1},{6,4},{7,3},{8,10},{9,13},{10,... | collective-permute-start | bytes 1769480 | tf_op jit(solution)/shard_map/ppermute | solution.py:274
  102.2 7.5 %collective-permute-start.18 = (f32[152,256]{1,0:T(8,128)S(1)}, f32[152,256]{1,0:T(8,128)S(1)}, u32[]{:S(2)}, u32[]{:S(2)}) collective-permute-start(f32[152,256]{1,0:T(8,128)S(1)} %dynamic-slice_add_fusion.4), channel_id=1, source_target_pairs={{0,8},{1,9},{2,10},{3,11},{4,12},{5,13},{6,14},{7,15},{8,0},{9,1},... | collective-permute-start | bytes 466952 | tf_op jit(solution)/shard_map/ppermute | solution.py:274
  109.7 7.0 %collective-permute-start.20 = (f32[304,256]{1,0:T(8,128)S(1)}, f32[304,256]{1,0:T(8,128)S(1)}, u32[]{:S(2)}, u32[]{:S(2)}) collective-permute-start(f32[304,256]{1,0:T(8,128)S(1)} %maximum_select_fusion.6), channel_id=1, source_target_pairs={{0,4},{1,3},{2,6},{3,1},{4,0},{5,7},{6,2},{7,5},{8,12},{9,11},{10,... | collective-permute-start | bytes 933896 | tf_op jit(solution)/shard_map/ppermute | solution.py:274
  116.7 10.3 %collective-permute-start.22 = (f32[608,256]{1,0:T(8,128)S(1)}, f32[608,256]{1,0:T(8,128)S(1)}, u32[]{:S(2)}, u32[]{:S(2)}) collective-permute-start(f32[608,256]{1,0:T(8,128)S(1)} %maximum_select_fusion.4), channel_id=1, source_target_pairs={{0,2},{1,5},{2,0},{3,7},{4,6},{5,1},{6,4},{7,3},{8,10},{9,13},{10,... | collective-permute-start | bytes 1867784 | tf_op jit(solution)/shard_map/ppermute | solution.py:274
  118.7 9.0 %collective-permute-start.24 = (f32[1152,256]{1,0:T(8,128)S(1)}, f32[1152,256]{1,0:T(8,128)S(1)}, u32[]{:S(2)}, u32[]{:S(2)}) collective-permute-start(f32[1152,256]{1,0:T(8,128)S(1)} %maximum_select_fusion.3), channel_id=1, source_target_pairs={{0,1},{1,0},{2,3},{3,2},{4,5},{5,4},{6,7},{7,6},{8,9},{9,8},{10,11... | collective-permute-start | bytes 3538952 | tf_op jit(solution)/shard_map/ppermute | solution.py:274
  127.2 3.1 %collective-permute-start.23 = (f32[1216,256]{1,0:T(8,128)S(1)}, f32[1216,256]{1,0:T(8,128)S(1)}, u32[]{:S(2)}, u32[]{:S(2)}) collective-permute-start(f32[1216,256]{1,0:T(8,128)S(1)} %maximum_select_fusion.2), channel_id=1, source_target_pairs={{0,1},{1,0},{2,3},{3,2},{4,5},{5,4},{6,7},{7,6},{8,9},{9,8},{10,11... | collective-permute-start | bytes 3735560 | tf_op jit(solution)/shard_map/ppermute | solution.py:274

commit v6 on v5

--- a/solution.py
+++ b/solution.py
@@ -354,7 +354,7 @@
 
 
 def turns(levels):
-    return "icoioic" + "oi" * (2 * levels - 4) + "i"
+    return "icoioioc" + "io" * (2 * levels - 5) + "ii"
 
 
 def body(latents, input_map, output_map, decay_rate, frame_step, cotangent):

time: 133 us -> 133 us (level)
  starting transfers between devices: 29.3 us -> 31.3 us
  waiting for transfers between devices: 49.8 us -> 48.2 us
    ppermute x16, starting transfers between devices: 15.5 us -> 17.5 us  [swap(): lax.ppermute(value, 'tm', [(source, source ^ 1 << levels[source & 1]) for...]
    ppermute x16, waiting for transfers between devices: 37.8 us -> 36.2 us  [swap(): lax.ppermute(value, 'tm', [(source, source ^ 1 << levels[source & 1]) for...]
  transfers between devices with their start and end apart: 25 -> 25, of which waited for: 17 -> 16; matrix products, arithmetic and copies ran while one was open for 4% -> 4% of each run, Pallas kernels for 23% -> 23%
where the time goes in v6:
time: 133 us
  waiting for transfers between devices  48.2 us (36%)
  Pallas kernels  44 us (33%)
  starting transfers between devices  31.3 us (24%)
  other arithmetic  7.7 us (6%)
    ppermute x16, waiting for transfers between devices, swap(): lax.ppermute(value, 'tm', [(source, source ^ 1 << levels[source & 1]) for...  36.2 us
    ppermute x16, starting transfers between devices, swap(): lax.ppermute(value, 'tm', [(source, source ^ 1 << levels[source & 1]) for...  17.5 us
    pallas_call x3, Pallas kernels, drive(): call(functools.partial(drive_kernel, reverse, base, start is None), (size...  15.6 us
    pallas_call x2, Pallas kernels, conv(): call(functools.partial(conv_kernel, reverse), (size,), specs, framed(shap...  12 us
    ppermute x6, starting transfers between devices, start(): self.other = lax.ppermute(self.message, 'tm', pairs)  9.77 us
    pallas_call x1, Pallas kernels, body(): call(functools.partial(adjoint_kernel, factor, steps - later), grid, [sme...  9.08 us
    pallas_call x1, Pallas kernels, body(): call(functools.partial(state_kernel, factor), grid, [smem(), smem(), fixe...  7.35 us
    ppermute x6, waiting for transfers between devices, start(): self.other = lax.ppermute(self.message, 'tm', pairs)  6.63 us
  transfers between devices with their start and end apart: 25, of which 16 were waited for; matrix products, arithmetic and copies ran while one was open for 4% of the time, Pallas kernels for 23%

profile of v6, /device:TPU:0, one launch (start us, length us, event | category | flops | bytes accessed | tf_op | source)
XLA Modules:
  0.0 133.0 jit_solution(1546757090263301482)
XLA Ops:
  0.6 0.0 copy-start.1
  0.6 6.7 %drive.1 = (f32[64,2,32,256]{3,2,1,0:T(8,128)}, f32[72,256]{1,0:T(8,128)S(1)}) custom-call(f32[64]{0:T(128)} %step_ref.9, f32[1,256]{1,0:T(1,128)} %bitcast.110, bf16[64,2,32,256]{3,2,1,0:T(8,128)(2,1)} %latents_ref.1, bf16[9,256,256]{2,1,0:T(8,128)(2,1)} %weights_ref.9), custom_call_target="tpu_custom_call" | custom-call | flops 3221225472 | bytes 6291456 | tf_op jit(solution)/shard_map/drive/pallas_call | solution.py:388
  7.4 0.5 collective-permute-start
  7.8 4.5 %pull.2 = (f32[32,2,32,256]{3,2,1,0:T(8,128)}, f32[72,256]{1,0:T(8,128)S(1)}) custom-call(f32[64]{0:T(128)} %step_ref.9, f32[1,256]{1,0:T(1,128)} %bitcast.111, bf16[64,2,32,256]{3,2,1,0:T(8,128)(2,1)} %cotangent_ref.1, bf16[9,256,256]{2,1,0:T(8,128)(2,1)S(1)} %copy-done.1), custom_call_target="tpu_custom_call" | custom-call | flops 1610612736 | bytes 3145728 | tf_op jit(solution)/shard_map/pull/pallas_call | solution.py:388
  12.3 0.0 collective-permute-done
  12.3 2.6 %collective-permute-start.1 = (f32[72,256]{1,0:T(8,128)S(1)}, f32[72,256]{1,0:T(8,128)S(1)}, u32[]{:S(2)}, u32[]{:S(2)}) collective-permute-start(f32[72,256]{1,0:T(8,128)S(1)} %pad_maximum_fusion), channel_id=1, source_target_pairs={{0,2},{1,3},{2,0},{3,1},{4,6},{5,7},{6,4},{7,5},{8,10},{9,11},{10,... | collective-permute-start | bytes 221192 | tf_op jit(solution)/shard_map/ppermute | solution.py:323
  14.9 4.5 %pull.3 = (f32[32,2,32,256]{3,2,1,0:T(8,128)}, f32[72,256]{1,0:T(8,128)S(1)}) custom-call(f32[64]{0:T(128)} %step_ref.9, f32[1,256]{1,0:T(1,128)} %bitcast.112, bf16[64,2,32,256]{3,2,1,0:T(8,128)(2,1)} %cotangent_ref.1, bf16[9,256,256]{2,1,0:T(8,128)(2,1)S(1)} %copy-done.1, f32[72,256]{1,0:T(8,128)S(1)} %get-tuple-element.50.refs_0_), custom_call_target="tpu_custom_call" | custom-call | flops 1610612736 | bytes 3145728 | tf_op jit(solution)/shard_map/pull/pallas_call | solution.py:388
  19.4 0.0 collective-permute-done.1
  19.4 1.6 %collective-permute-start.2 = (f32[72,256]{1,0:T(8,128)S(1)}, f32[72,256]{1,0:T(8,128)S(1)}, u32[]{:S(2)}, u32[]{:S(2)}) collective-permute-start(f32[72,256]{1,0:T(8,128)S(1)} %pad_maximum_fusion.1), channel_id=1, source_target_pairs={{0,4},{1,5},{2,6},{3,7},{4,0},{5,1},{6,2},{7,3},{8,12},{9,13},{10,... | collective-permute-start | bytes 221192 | tf_op jit(solution)/shard_map/ppermute | solution.py:323
  21.1 2.8 %collective-permute-done.2 = f32[72,256]{1,0:T(8,128)S(1)} collective-permute-done((f32[72,256]{1,0:T(8,128)S(1)}, f32[72,256]{1,0:T(8,128)S(1)}, u32[]{:S(2)}, u32[]{:S(2)}) %collective-permute-start.2) | collective-permute-done | bytes 73760 | tf_op jit(solution)/shard_map/ppermute | solution.py:323
  23.9 4.5 %collective-permute-start.3 = (f32[72,256]{1,0:T(8,128)S(1)}, f32[72,256]{1,0:T(8,128)S(1)}, u32[]{:S(2)}, u32[]{:S(2)}) collective-permute-start(f32[72,256]{1,0:T(8,128)S(1)} %pad_maximum_fusion.2), channel_id=1, source_target_pairs={{0,8},{1,9},{2,10},{3,11},{4,12},{5,13},{6,14},{7,15},{16,24},{17,... | collective-permute-start | bytes 221192 | tf_op jit(solution)/shard_map/ppermute | solution.py:323
  28.5 0.6 collective-permute-start.5
  29.1 1.3 collective-permute-done.3
  30.4 2.5 %collective-permute-done.5 = f32[72,256]{1,0:T(8,128)S(1)} collective-permute-done((f32[72,256]{1,0:T(8,128)S(1)}, f32[72,256]{1,0:T(8,128)S(1)}, u32[]{:S(2)}, u32[]{:S(2)}) %collective-permute-start.5) | collective-permute-done | bytes 73760 | tf_op jit(solution)/shard_map/ppermute | solution.py:323
  33.0 7.4 %states.1 = (bf16[64,2,32,256]{3,2,1,0:T(8,128)(2,1)}, f32[1152,256]{1,0:T(8,128)S(1)}, f32[1152,256]{1,0:T(8,128)S(1)}) custom-call(f32[64]{0:T(128)S(1)} %copy-done.4, s32[1]{0:T(128)} %bitcast.core_ref, f32[1,256]{1,0:T(1,128)S(1)} %bitcast.113, f32[64,256]{1,0:T(8,128)S(1)} %add_select_fusion.1.incoming_ref, ...), custom_call_target="tpu_custom_call" | custom-call | flops 3221225472 | bytes 8388608 | tf_op jit(solution)/shard_map/states/pallas_call | solution.py:431
  40.3 1.3 collective-permute-start.8
  41.6 1.3 collective-permute-start.7
  42.9 1.5 %collective-permute-start.6 = (f32[72,256]{1,0:T(8,128)S(1)}, f32[72,256]{1,0:T(8,128)S(1)}, u32[]{:S(2)}, u32[]{:S(2)}) collective-permute-start(f32[72,256]{1,0:T(8,128)S(1)} %pad_maximum_fusion.4), channel_id=1, source_target_pairs={{4,0},{5,1},{6,2},{7,3},{8,4},{9,5},{10,6},{11,7},{12,8},{13,9},{1... | collective-permute-start | bytes 221192 | tf_op jit(solution)/shard_map/ppermute | solution.py:339
  44.4 4.7 %collective-permute-done.8 = f32[72,256]{1,0:T(8,128)S(1)} collective-permute-done((f32[72,256]{1,0:T(8,128)S(1)}, f32[72,256]{1,0:T(8,128)S(1)}, u32[]{:S(2)}, u32[]{:S(2)}) %collective-permute-start.8) | collective-permute-done | bytes 73760 | tf_op jit(solution)/shard_map/ppermute | solution.py:339
  49.1 1.4 %add.158 = f32[1152,256]{1,0:T(8,128)S(1)} add(f32[1152,256]{1,0:T(8,128)S(1)} %get-tuple-element.63, f32[1152,256]{1,0:T(8,128)} %collective-permute-done.9) | non-fusion elementwise | flops 294912 | bytes 3538944 | tf_op jit(solution)/shard_map/add | solution.py:283
  50.6 0.6 collective-permute-start.10
  51.1 0.8 collective-permute-done.7
  52.0 9.1 %adjoint.1 = (bf16[64,2,32,256]{3,2,1,0:T(8,128)(2,1)}, f32[1216,256]{1,0:T(8,128)S(1)}, f32[1216,256]{1,0:T(8,128)S(1)}) custom-call(f32[64]{0:T(128)S(1)} %copy-done.4, s32[1]{0:T(128)} %bitcast.core_ref, f32[1,256]{1,0:T(1,128)S(1)} %bitcast.114, f32[64,256]{1,0:T(8,128)S(1)} %fusion.arriving_ref, f32[64,256]{1,0:T(8,128)S(1)} %add_select_fusion.1.incoming_ref, ...), custom_call_target="tpu_custom_call" | custom-call | flops 3221225472 | bytes 10485760 | tf_op jit(solution)/shard_map/adjoint/pallas_call | solution.py:478
  61.0 0.1 dynamic-slice_add_fusion.1
  61.2 0.1 collective-permute-start.11
  61.3 2.2 %collective-permute-start.12 = (f32[288,256]{1,0:T(8,128)S(1)}, f32[288,256]{1,0:T(8,128)S(1)}, u32[]{:S(2)}, u32[]{:S(2)}) collective-permute-start(f32[288,256]{1,0:T(8,128)S(1)} %constant_dynamic-slice_fusion.4), channel_id=1, source_target_pairs={{0,4},{1,3},{2,6},{3,1},{4,0},{5,7},{6,2},{7,5},{8,12},{9,11},{10,... | collective-permute-start | bytes 884744 | tf_op jit(solution)/shard_map/ppermute | solution.py:274
  63.4 0.9 collective-permute-done.11
  64.3 1.5 %add.163 = f32[1216,256]{1,0:T(8,128)S(1)} add(f32[1216,256]{1,0:T(8,128)S(1)} %get-tuple-element.67, f32[1216,256]{1,0:T(8,128)} %collective-permute-done.11) | non-fusion elementwise | flops 311296 | bytes 3735552 | tf_op jit(solution)/shard_map/add | solution.py:283
  65.8 0.0 copy-start.2
  65.8 0.1 constant_dynamic-slice_fusion.3
  65.8 0.8 collective-permute-start.14
  66.7 0.4 copy-done.2
  67.0 5.8 %conv.2 = bf16[64,2,32,256]{3,2,1,0:T(8,128)(2,1)} custom-call(bf16[64,2,32,256]{3,2,1,0:T(8,128)(2,1)} %get-tuple-element.72.states_ref.previous_ref.value_ref, bf16[9,256,256]{2,1,0:T(8,128)(2,1)S(1)} %copy-done.2), custom_call_target="tpu_custom_call" | custom-call | flops 3221225472 | bytes 4194304 | tf_op jit(solution)/shard_map/conv/pallas_call | solution.py:458
  72.9 1.2 collective-permute-start.13
  74.1 2.0 %collective-permute-done.14 = f32[608,256]{1,0:T(8,128)S(1)} collective-permute-done((f32[608,256]{1,0:T(8,128)S(1)}, f32[608,256]{1,0:T(8,128)S(1)}, u32[]{:S(2)}, u32[]{:S(2)}) %collective-permute-start.14) | collective-permute-done | bytes 622624 | tf_op jit(solution)/shard_map/ppermute | solution.py:274
  76.1 0.1 dynamic-slice_add_fusion
  76.2 0.0 copy-start.3
  76.3 2.2 %collective-permute-start.16 = (f32[304,256]{1,0:T(8,128)S(1)}, f32[304,256]{1,0:T(8,128)S(1)}, u32[]{:S(2)}, u32[]{:S(2)}) collective-permute-start(f32[304,256]{1,0:T(8,128)S(1)} %constant_dynamic-slice_fusion.1), channel_id=1, source_target_pairs={{0,4},{1,3},{2,6},{3,1},{4,0},{5,7},{6,2},{7,5},{8,12},{9,11},{10,... | collective-permute-start | bytes 933896 | tf_op jit(solution)/shard_map/ppermute | solution.py:274
  78.4 5.3 %collective-permute-done.13 = f32[144,256]{1,0:T(8,128)S(1)} collective-permute-done((f32[144,256]{1,0:T(8,128)S(1)}, f32[144,256]{1,0:T(8,128)S(1)}, u32[]{:S(2)}, u32[]{:S(2)}) %collective-permute-start.13) | collective-permute-done | bytes 147488 | tf_op jit(solution)/shard_map/ppermute | solution.py:274
  83.7 0.1 collective-permute-start.15
  83.8 1.7 %collective-permute-done.16 = f32[304,256]{1,0:T(8,128)S(1)} collective-permute-done((f32[304,256]{1,0:T(8,128)S(1)}, f32[304,256]{1,0:T(8,128)S(1)}, u32[]{:S(2)}, u32[]{:S(2)}) %collective-permute-start.16) | collective-permute-done | bytes 311328 | tf_op jit(solution)/shard_map/ppermute | solution.py:274
  85.6 1.3 collective-permute-start.17
  86.9 8.2 %collective-permute-done.15 = f32[144,256]{1,0:T(8,128)S(1)} collective-permute-done((f32[144,256]{1,0:T(8,128)S(1)}, f32[144,256]{1,0:T(8,128)S(1)}, u32[]{:S(2)}, u32[]{:S(2)}) %collective-permute-start.15) | collective-permute-done | bytes 147488 | tf_op jit(solution)/shard_map/ppermute | solution.py:274
  95.1 0.3 collective-permute-start.19
  95.5 6.2 %conv.3 = bf16[64,2,32,256]{3,2,1,0:T(8,128)(2,1)} custom-call(bf16[64,2,32,256]{3,2,1,0:T(8,128)(2,1)} %get-tuple-element.79.value_ref, bf16[9,256,256]{2,1,0:T(8,128)(2,1)S(1)} %copy-done.3), custom_call_target="tpu_custom_call" | custom-call | flops 3221225472 | bytes 4194304 | tf_op jit(solution)/shard_map/conv/pallas_call | solution.py:458
  101.7 0.3 collective-permute-done.19
  102.0 0.2 collective-permute-start.21
  102.2 3.2 %collective-permute-start.18 = (f32[152,256]{1,0:T(8,128)S(1)}, f32[152,256]{1,0:T(8,128)S(1)}, u32[]{:S(2)}, u32[]{:S(2)}) collective-permute-start(f32[152,256]{1,0:T(8,128)S(1)} %dynamic-slice_add_fusion.4), channel_id=1, source_target_pairs={{0,8},{1,9},{2,10},{3,11},{4,12},{5,13},{6,14},{7,15},{8,0},{9,1},... | collective-permute-start | bytes 466952 | tf_op jit(solution)/shard_map/ppermute | solution.py:274
  105.4 4.5 %collective-permute-done.18 = f32[152,256]{1,0:T(8,128)S(1)} collective-permute-done((f32[152,256]{1,0:T(8,128)S(1)}, f32[152,256]{1,0:T(8,128)S(1)}, u32[]{:S(2)}, u32[]{:S(2)}) %collective-permute-start.18) | collective-permute-done | bytes 155680 | tf_op jit(solution)/shard_map/ppermute | solution.py:274
  109.9 1.7 %collective-permute-start.20 = (f32[304,256]{1,0:T(8,128)S(1)}, f32[304,256]{1,0:T(8,128)S(1)}, u32[]{:S(2)}, u32[]{:S(2)}) collective-permute-start(f32[304,256]{1,0:T(8,128)S(1)} %maximum_select_fusion.6), channel_id=1, source_target_pairs={{0,4},{1,3},{2,6},{3,1},{4,0},{5,7},{6,2},{7,5},{8,12},{9,11},{10,... | collective-permute-start | bytes 933896 | tf_op jit(solution)/shard_map/ppermute | solution.py:274
  111.6 0.3 collective-permute-done.21
  111.9 0.1 maximum_select_fusion.3
  112.0 5.0 %collective-permute-done.20 = f32[304,256]{1,0:T(8,128)S(1)} collective-permute-done((f32[304,256]{1,0:T(8,128)S(1)}, f32[304,256]{1,0:T(8,128)S(1)}, u32[]{:S(2)}, u32[]{:S(2)}) %collective-permute-start.20) | collective-permute-done | bytes 311328 | tf_op jit(solution)/shard_map/ppermute | solution.py:274
  117.1 1.8 %collective-permute-start.22 = (f32[608,256]{1,0:T(8,128)S(1)}, f32[608,256]{1,0:T(8,128)S(1)}, u32[]{:S(2)}, u32[]{:S(2)}) collective-permute-start(f32[608,256]{1,0:T(8,128)S(1)} %maximum_select_fusion.4), channel_id=1, source_target_pairs={{0,2},{1,5},{2,0},{3,7},{4,6},{5,1},{6,4},{7,3},{8,10},{9,13},{10,... | collective-permute-start | bytes 1867784 | tf_op jit(solution)/shard_map/ppermute | solution.py:274
  118.9 1.3 %collective-permute-start.24 = (f32[1152,256]{1,0:T(8,128)S(1)}, f32[1152,256]{1,0:T(8,128)S(1)}, u32[]{:S(2)}, u32[]{:S(2)}) collective-permute-start(f32[1152,256]{1,0:T(8,128)S(1)} %maximum_select_fusion.3), channel_id=1, source_target_pairs={{0,1},{1,0},{2,3},{3,2},{4,5},{5,4},{6,7},{7,6},{8,9},{9,8},{10,11... | collective-permute-start | bytes 3538952 | tf_op jit(solution)/shard_map/ppermute | solution.py:274
  120.2 7.2 %collective-permute-done.22 = f32[608,256]{1,0:T(8,128)S(1)} collective-permute-done((f32[608,256]{1,0:T(8,128)S(1)}, f32[608,256]{1,0:T(8,128)S(1)}, u32[]{:S(2)}, u32[]{:S(2)}) %collective-permute-start.22) | collective-permute-done | bytes 622624 | tf_op jit(solution)/shard_map/ppermute | solution.py:274
  127.4 0.1 maximum_select_fusion.2
  127.5 0.5 collective-permute-start.23
  128.0 0.1 slice.109
  128.1 1.7 %maximum_select_fusion.1 = f32[2304,256]{1,0:T(8,128)} fusion(f32[1152,256]{1,0:T(8,128)S(1)} %collective-permute-done.24, f32[1152,256]{1,0:T(8,128)S(1)} %maximum_select_fusion.3, pred[]{:T(512)S(6)} %eq.54), kind=kLoop, calls=%fused_computation.1 | loop fusion | flops 1769472 | bytes 4718593 | tf_op jit(solution)/shard_map/jit(_where)/select_n | solution.py:245
  129.8 0.8 collective-permute-done.23
  130.6 0.1 slice.102
  130.7 0.6 multiply_multiply_fusion
  131.3 1.7 %maximum_select_fusion = f32[2304,256]{1,0:T(8,128)} fusion(f32[1088,256]{1,0:T(8,128)S(1)} %slice.102, f32[1216,256]{1,0:T(8,128)S(1)} %maximum_select_fusion.2, f32[1088,256]{1,0:T(8,128)S(1)} %slice.109, f32[1216,256]{1,0:T(8,128)S(1)} %collective-permute-done.23, pred[]{:T(512)S(6)} %eq.54), kind=kLoop, calls=%fused_computation | loop fusion | flops 1769472 | bytes 7077889 | tf_op jit(solution)/shard_map/jit(_where)/select_n | solution.py:248
  (49 shorter events, 0.7 us)
Async XLA Ops:
  0.6 7.2 %copy-start.1 = (bf16[9,256,256]{2,1,0:T(8,128)(2,1)S(1)}, bf16[9,256,256]{2,1,0:T(8,128)(2,1)}, u32[]{:S(2)}) copy-start(bf16[9,256,256]{2,1,0:T(8,128)(2,1)} %weights_ref.8) | copy-start | bytes 3538948
  7.4 4.9 %collective-permute-start = (f32[72,256]{1,0:T(8,128)S(1)}, f32[72,256]{1,0:T(8,128)S(1)}, u32[]{:S(2)}, u32[]{:S(2)}) collective-permute-start(f32[72,256]{1,0:T(8,128)S(1)} %get-tuple-element.46), channel_id=1, source_target_pairs={{0,1},{1,0},{2,3},{3,2},{4,5},{5,4},{6,7},{7,6},{8,9},{9,8},{10,11... | collective-permute-start | bytes 221192 | tf_op jit(solution)/shard_map/ppermute | solution.py:323
  12.3 7.1 %collective-permute-start.1 = (f32[72,256]{1,0:T(8,128)S(1)}, f32[72,256]{1,0:T(8,128)S(1)}, u32[]{:S(2)}, u32[]{:S(2)}) collective-permute-start(f32[72,256]{1,0:T(8,128)S(1)} %pad_maximum_fusion), channel_id=1, source_target_pairs={{0,2},{1,3},{2,0},{3,1},{4,6},{5,7},{6,4},{7,5},{8,10},{9,11},{10,... | collective-permute-start | bytes 221192 | tf_op jit(solution)/shard_map/ppermute | solution.py:323
  19.4 13.6 %copy-start = (f32[256]{0:T(256)S(1)}, f32[256]{0:T(256)}, u32[]{:S(2)}) copy-start(f32[256]{0:T(256)} %param.9) | copy-start | bytes 3076
  19.4 13.6 %copy-start.4 = (f32[64]{0:T(128)S(1)}, f32[64]{0:T(128)}, u32[]{:S(2)}) copy-start(f32[64]{0:T(128)} %step_ref.9) | copy-start | bytes 772
  19.4 4.5 %collective-permute-start.2 = (f32[72,256]{1,0:T(8,128)S(1)}, f32[72,256]{1,0:T(8,128)S(1)}, u32[]{:S(2)}, u32[]{:S(2)}) collective-permute-start(f32[72,256]{1,0:T(8,128)S(1)} %pad_maximum_fusion.1), channel_id=1, source_target_pairs={{0,4},{1,5},{2,6},{3,7},{4,0},{5,1},{6,2},{7,3},{8,12},{9,13},{10,... | collective-permute-start | bytes 221192 | tf_op jit(solution)/shard_map/ppermute | solution.py:323
  21.1 7.4 %collective-permute-start.4 = (f32[72,256]{1,0:T(8,128)S(1)}, f32[72,256]{1,0:T(8,128)S(1)}, u32[]{:S(2)}, u32[]{:S(2)}) collective-permute-start(f32[72,256]{1,0:T(8,128)S(1)} %get-tuple-element.53), channel_id=1, source_target_pairs={{0,1},{1,0},{2,3},{3,2},{4,5},{5,4},{6,7},{7,6},{8,9},{9,8},{10,11... | collective-permute-start | bytes 221192 | tf_op jit(solution)/shard_map/ppermute | solution.py:323
  23.9 6.5 %collective-permute-start.3 = (f32[72,256]{1,0:T(8,128)S(1)}, f32[72,256]{1,0:T(8,128)S(1)}, u32[]{:S(2)}, u32[]{:S(2)}) collective-permute-start(f32[72,256]{1,0:T(8,128)S(1)} %pad_maximum_fusion.2), channel_id=1, source_target_pairs={{0,8},{1,9},{2,10},{3,11},{4,12},{5,13},{6,14},{7,15},{16,24},{17,... | collective-permute-start | bytes 221192 | tf_op jit(solution)/shard_map/ppermute | solution.py:323
  28.5 4.4 %collective-permute-start.5 = (f32[72,256]{1,0:T(8,128)S(1)}, f32[72,256]{1,0:T(8,128)S(1)}, u32[]{:S(2)}, u32[]{:S(2)}) collective-permute-start(f32[72,256]{1,0:T(8,128)S(1)} %pad_maximum_fusion.3), channel_id=1, source_target_pairs={{0,2},{1,3},{2,0},{3,1},{4,6},{5,7},{6,4},{7,5},{8,10},{9,11},{10,... | collective-permute-start | bytes 221192 | tf_op jit(solution)/shard_map/ppermute | solution.py:323
  40.3 8.7 %collective-permute-start.9 = (f32[1152,256]{1,0:T(8,128)S(1)}, f32[1152,256]{1,0:T(8,128)}, u32[]{:S(2)}, u32[]{:S(2)}) collective-permute-start(f32[1152,256]{1,0:T(8,128)S(1)} %get-tuple-element.59), channel_id=1, source_target_pairs={{0,1},{1,0},{2,3},{3,2},{4,5},{5,4},{6,7},{7,6},{8,9},{9,8},{10,11... | collective-permute-start | bytes 3538952 | tf_op jit(solution)/shard_map/ppermute | solution.py:274
  40.3 8.7 %collective-permute-start.8 = (f32[72,256]{1,0:T(8,128)S(1)}, f32[72,256]{1,0:T(8,128)S(1)}, u32[]{:S(2)}, u32[]{:S(2)}) collective-permute-start(f32[72,256]{1,0:T(8,128)S(1)} %pad_maximum_fusion.4), channel_id=1, source_target_pairs={{12,0},{13,1},{14,2},{15,3},{28,16},{29,17},{30,18},{31,19}} | collective-permute-start | bytes 221192 | tf_op jit(solution)/shard_map/ppermute | solution.py:339
  41.6 10.3 %collective-permute-start.7 = (f32[72,256]{1,0:T(8,128)S(1)}, f32[72,256]{1,0:T(8,128)S(1)}, u32[]{:S(2)}, u32[]{:S(2)}) collective-permute-start(f32[72,256]{1,0:T(8,128)S(1)} %pad_maximum_fusion.4), channel_id=1, source_target_pairs={{8,0},{9,1},{10,2},{11,3},{12,4},{13,5},{14,6},{15,7},{24,16},{25,... | collective-permute-start | bytes 221192 | tf_op jit(solution)/shard_map/ppermute | solution.py:339
  42.9 9.0 %collective-permute-start.6 = (f32[72,256]{1,0:T(8,128)S(1)}, f32[72,256]{1,0:T(8,128)S(1)}, u32[]{:S(2)}, u32[]{:S(2)}) collective-permute-start(f32[72,256]{1,0:T(8,128)S(1)} %pad_maximum_fusion.4), channel_id=1, source_target_pairs={{4,0},{5,1},{6,2},{7,3},{8,4},{9,5},{10,6},{11,7},{12,8},{13,9},{1... | collective-permute-start | bytes 221192 | tf_op jit(solution)/shard_map/ppermute | solution.py:339
  50.6 10.5 %collective-permute-start.10 = (f32[576,256]{1,0:T(8,128)S(1)}, f32[576,256]{1,0:T(8,128)S(1)}, u32[]{:S(2)}, u32[]{:S(2)}) collective-permute-start(f32[576,256]{1,0:T(8,128)S(1)} %constant_dynamic-slice_fusion.5), channel_id=1, source_target_pairs={{0,2},{1,5},{2,0},{3,7},{4,6},{5,1},{6,4},{7,3},{8,10},{9,13},{10,... | collective-permute-start | bytes 1769480 | tf_op jit(solution)/shard_map/ppermute | solution.py:274
  61.2 3.1 %collective-permute-start.11 = (f32[1216,256]{1,0:T(8,128)S(1)}, f32[1216,256]{1,0:T(8,128)}, u32[]{:S(2)}, u32[]{:S(2)}) collective-permute-start(f32[1216,256]{1,0:T(8,128)S(1)} %get-tuple-element.70), channel_id=1, source_target_pairs={{0,1},{1,0},{2,3},{3,2},{4,5},{5,4},{6,7},{7,6},{8,9},{9,8},{10,11... | collective-permute-start | bytes 3735560 | tf_op jit(solution)/shard_map/ppermute | solution.py:274
  61.3 11.6 %collective-permute-start.12 = (f32[288,256]{1,0:T(8,128)S(1)}, f32[288,256]{1,0:T(8,128)S(1)}, u32[]{:S(2)}, u32[]{:S(2)}) collective-permute-start(f32[288,256]{1,0:T(8,128)S(1)} %constant_dynamic-slice_fusion.4), channel_id=1, source_target_pairs={{0,4},{1,3},{2,6},{3,1},{4,0},{5,7},{6,2},{7,5},{8,12},{9,11},{10,... | collective-permute-start | bytes 884744 | tf_op jit(solution)/shard_map/ppermute | solution.py:274
  65.8 1.3 copy-start.2
  65.8 10.3 %collective-permute-start.14 = (f32[608,256]{1,0:T(8,128)S(1)}, f32[608,256]{1,0:T(8,128)S(1)}, u32[]{:S(2)}, u32[]{:S(2)}) collective-permute-start(f32[608,256]{1,0:T(8,128)S(1)} %constant_dynamic-slice_fusion.3), channel_id=1, source_target_pairs={{0,2},{1,5},{2,0},{3,7},{4,6},{5,1},{6,4},{7,3},{8,10},{9,13},{10,... | collective-permute-start | bytes 1867784 | tf_op jit(solution)/shard_map/ppermute | solution.py:274
  72.9 10.8 %collective-permute-start.13 = (f32[144,256]{1,0:T(8,128)S(1)}, f32[144,256]{1,0:T(8,128)S(1)}, u32[]{:S(2)}, u32[]{:S(2)}) collective-permute-start(f32[144,256]{1,0:T(8,128)S(1)} %constant_dynamic-slice_fusion.2), channel_id=1, source_target_pairs={{0,8},{1,9},{2,10},{3,11},{4,12},{5,13},{6,14},{7,15},{8,0},{9,1},... | collective-permute-start | bytes 442376 | tf_op jit(solution)/shard_map/ppermute | solution.py:274
  76.2 19.2 %copy-start.3 = (bf16[9,256,256]{2,1,0:T(8,128)(2,1)S(1)}, bf16[9,256,256]{2,1,0:T(8,128)(2,1)}, u32[]{:S(2)}) copy-start(bf16[9,256,256]{2,1,0:T(8,128)(2,1)} %weights_ref.9) | copy-start | bytes 3538948
  76.3 9.3 %collective-permute-start.16 = (f32[304,256]{1,0:T(8,128)S(1)}, f32[304,256]{1,0:T(8,128)S(1)}, u32[]{:S(2)}, u32[]{:S(2)}) collective-permute-start(f32[304,256]{1,0:T(8,128)S(1)} %constant_dynamic-slice_fusion.1), channel_id=1, source_target_pairs={{0,4},{1,3},{2,6},{3,1},{4,0},{5,7},{6,2},{7,5},{8,12},{9,11},{10,... | collective-permute-start | bytes 933896 | tf_op jit(solution)/shard_map/ppermute | solution.py:274
  83.7 11.4 %collective-permute-start.15 = (f32[144,256]{1,0:T(8,128)S(1)}, f32[144,256]{1,0:T(8,128)S(1)}, u32[]{:S(2)}, u32[]{:S(2)}) collective-permute-start(f32[144,256]{1,0:T(8,128)S(1)} %dynamic-slice_add_fusion.5), channel_id=1, source_target_pairs={{0,8},{1,9},{2,10},{3,11},{4,12},{5,13},{6,14},{7,15},{8,0},{9,1},... | collective-permute-start | bytes 442376 | tf_op jit(solution)/shard_map/ppermute | solution.py:274
  85.6 16.1 %collective-permute-start.17 = (f32[152,256]{1,0:T(8,128)S(1)}, f32[152,256]{1,0:T(8,128)S(1)}, u32[]{:S(2)}, u32[]{:S(2)}) collective-permute-start(f32[152,256]{1,0:T(8,128)S(1)} %constant_dynamic-slice_fusion), channel_id=1, source_target_pairs={{0,8},{1,9},{2,10},{3,11},{4,12},{5,13},{6,14},{7,15},{8,0},{9,1},... | collective-permute-start | bytes 466952 | tf_op jit(solution)/shard_map/ppermute | solution.py:274
  95.1 6.8 %collective-permute-start.19 = (f32[288,256]{1,0:T(8,128)S(1)}, f32[288,256]{1,0:T(8,128)S(1)}, u32[]{:S(2)}, u32[]{:S(2)}) collective-permute-start(f32[288,256]{1,0:T(8,128)S(1)} %maximum_select_fusion.7), channel_id=1, source_target_pairs={{0,4},{1,3},{2,6},{3,1},{4,0},{5,7},{6,2},{7,5},{8,12},{9,11},{10,... | collective-permute-start | bytes 884744 | tf_op jit(solution)/shard_map/ppermute | solution.py:274
  102.0 9.9 %collective-permute-start.21 = (f32[576,256]{1,0:T(8,128)S(1)}, f32[576,256]{1,0:T(8,128)S(1)}, u32[]{:S(2)}, u32[]{:S(2)}) collective-permute-start(f32[576,256]{1,0:T(8,128)S(1)} %maximum_select_fusion.5), channel_id=1, source_target_pairs={{0,2},{1,5},{2,0},{3,7},{4,6},{5,1},{6,4},{7,3},{8,10},{9,13},{10,... | collective-permute-start | bytes 1769480 | tf_op jit(solution)/shard_map/ppermute | solution.py:274
  102.2 7.7 %collective-permute-start.18 = (f32[152,256]{1,0:T(8,128)S(1)}, f32[152,256]{1,0:T(8,128)S(1)}, u32[]{:S(2)}, u32[]{:S(2)}) collective-permute-start(f32[152,256]{1,0:T(8,128)S(1)} %dynamic-slice_add_fusion.4), channel_id=1, source_target_pairs={{0,8},{1,9},{2,10},{3,11},{4,12},{5,13},{6,14},{7,15},{8,0},{9,1},... | collective-permute-start | bytes 466952 | tf_op jit(solution)/shard_map/ppermute | solution.py:274
  109.9 7.2 %collective-permute-start.20 = (f32[304,256]{1,0:T(8,128)S(1)}, f32[304,256]{1,0:T(8,128)S(1)}, u32[]{:S(2)}, u32[]{:S(2)}) collective-permute-start(f32[304,256]{1,0:T(8,128)S(1)} %maximum_select_fusion.6), channel_id=1, source_target_pairs={{0,4},{1,3},{2,6},{3,1},{4,0},{5,7},{6,2},{7,5},{8,12},{9,11},{10,... | collective-permute-start | bytes 933896 | tf_op jit(solution)/shard_map/ppermute | solution.py:274
  117.1 10.3 %collective-permute-start.22 = (f32[608,256]{1,0:T(8,128)S(1)}, f32[608,256]{1,0:T(8,128)S(1)}, u32[]{:S(2)}, u32[]{:S(2)}) collective-permute-start(f32[608,256]{1,0:T(8,128)S(1)} %maximum_select_fusion.4), channel_id=1, source_target_pairs={{0,2},{1,5},{2,0},{3,7},{4,6},{5,1},{6,4},{7,3},{8,10},{9,13},{10,... | collective-permute-start | bytes 1867784 | tf_op jit(solution)/shard_map/ppermute | solution.py:274
  118.9 9.2 %collective-permute-start.24 = (f32[1152,256]{1,0:T(8,128)S(1)}, f32[1152,256]{1,0:T(8,128)S(1)}, u32[]{:S(2)}, u32[]{:S(2)}) collective-permute-start(f32[1152,256]{1,0:T(8,128)S(1)} %maximum_select_fusion.3), channel_id=1, source_target_pairs={{0,1},{1,0},{2,3},{3,2},{4,5},{5,4},{6,7},{7,6},{8,9},{9,8},{10,11... | collective-permute-start | bytes 3538952 | tf_op jit(solution)/shard_map/ppermute | solution.py:274
  127.5 3.1 %collective-permute-start.23 = (f32[1216,256]{1,0:T(8,128)S(1)}, f32[1216,256]{1,0:T(8,128)S(1)}, u32[]{:S(2)}, u32[]{:S(2)}) collective-permute-start(f32[1216,256]{1,0:T(8,128)S(1)} %maximum_select_fusion.2), channel_id=1, source_target_pairs={{0,1},{1,0},{2,3},{3,2},{4,5},{5,4},{6,7},{7,6},{8,9},{9,8},{10,11... | collective-permute-start | bytes 3735560 | tf_op jit(solution)/shard_map/ppermute | solution.py:274
